TPU v7x, 32 devices: a whole 2x2x4 slice. The times are simulated.
32 devices in a mesh: ctx: 16 (over z, y, x), head: 2 (over core), dp: 1.
Axes of the slice: x: 2, y: 2, z: 4, core: 2. Of those that a mesh axis runs over, the one named last changes fastest.
Arguments:
- queries: bfloat16 [2048, 4096], P(('dp', 'ctx'), 'head'), may hold values from -24 to 24
- key_rows: bfloat16 [2048, 1024], P(('dp', 'ctx'), 'head'), may hold values from -6 to 6
- value_rows: bfloat16 [2048, 1024], P(('dp', 'ctx'), 'head'), may hold values from -24 to 24
- grad_out: bfloat16 [2048, 4096], P(('dp', 'ctx'), 'head'), may hold values from -12 to 12
- doc_ids: int32 [2048], P(('dp', 'ctx')), may hold values from 0 to 4, never falling along the last dimension, each value on 1 to 1024 neighbouring positions
- loss_mask: int32 [2048], P(('dp', 'ctx')), may hold values from 0 to 1
- windows: int32 [32], P('head'), may hold values from 32 to 768, as said below
Outputs:
- attended: bfloat16 [2048, 4096], P(('dp', 'ctx'), 'head')
- grad_queries: bfloat16 [2048, 4096], P(('dp', 'ctx'), 'head')
- grad_keys: bfloat16 [2048, 1024], P(('dp', 'ctx'), 'head')
- grad_values: bfloat16 [2048, 1024], P(('dp', 'ctx'), 'head')
Inputs may be any that keep to these rules, and one draw needn't show every extreme that they name: `windows`: some query head in every aligned group of 8 heads has the window 768.
All inputs are finite; a program needn't handle non-finite values.
Results may differ from a plain program's by a relative error of at most 0.0078.
Values may be sent and summed in bfloat16 or wider, within the bound.
No kernel may reach another device: no remote copies, remote signals or barrier semaphores. Data moves between devices by JAX's collectives and lax.ppermute only.
A program may use at most 64 MiB of HBM per device.

v0:
```python
import jax
import jax.numpy as jnp
from jax import lax
from jax.sharding import PartitionSpec as P

HEAD_DIM = 128
HOPS = 6


def from_behind(shard, axis, by):
    count = lax.axis_size(axis)
    pairs = [(i, i + by) for i in range(count) if 0 <= i + by < count]
    return lax.ppermute(shard, axis, pairs)


def softmax_rows(scores, score_mask):
    scores = jnp.where(score_mask, scores, -jnp.inf)
    row_max = jnp.max(scores, axis=-1, keepdims=True)
    raised = jnp.exp(scores - row_max)
    return raised / jnp.sum(raised, axis=-1, keepdims=True)


def dense_pass(query_grp, grad_grp, key_head, value_head, score_mask, score_scale):
    scores = (
        jnp.einsum("rgd,kd->grk", query_grp, key_head, preferred_element_type=jnp.float32)
        * score_scale
    )
    weights = softmax_rows(scores, score_mask)
    weights_low = weights.astype(jnp.bfloat16)
    output = jnp.einsum("grk,kd->rgd", weights_low, value_head, preferred_element_type=jnp.float32)
    row_dot = jnp.sum(grad_grp.astype(jnp.float32) * output, axis=-1)
    grad_prob = jnp.einsum("rgd,kd->grk", grad_grp, value_head, preferred_element_type=jnp.float32)
    grad_score = (weights * (grad_prob - jnp.transpose(row_dot)[:, :, None])).astype(jnp.bfloat16)
    grad_query = (
        jnp.einsum("grk,kd->rgd", grad_score, key_head, preferred_element_type=jnp.float32)
        * score_scale
    )
    grad_key = (
        jnp.einsum("grk,rgd->kd", grad_score, query_grp, preferred_element_type=jnp.float32)
        * score_scale
    )
    grad_value = jnp.einsum(
        "grk,rgd->kd", weights_low, grad_grp, preferred_element_type=jnp.float32
    )
    return (output, grad_query, grad_key, grad_value)


def per_device(queries, key_rows, value_rows, grad_out, doc_ids, loss_mask, windows):
    row_count = key_rows.shape[0]
    kv_local = key_rows.shape[1] // HEAD_DIM
    head_local = queries.shape[1] // HEAD_DIM
    group_size = head_local // kv_local
    score_scale = HEAD_DIM ** (-0.5)
    position = lax.axis_index("ctx")
    mask_float = loss_mask.astype(jnp.float32)
    loss_count = lax.psum(jnp.sum(mask_float), "ctx")
    factor = row_count * lax.axis_size("ctx") / jnp.maximum(loss_count, 1.0)
    cotangent = (grad_out.astype(jnp.float32) * mask_float[:, None] * factor).astype(jnp.bfloat16)
    own_shard = (key_rows, value_rows, doc_ids)
    halo_list = []
    moving = own_shard
    for travel_step in range(HOPS):
        moving = from_behind((moving[0], moving[1], moving[2]), "ctx", 1)
        halo_list.append(moving)
    ordered = halo_list[::-1] + [own_shard]
    key_all = jnp.concatenate([piece[0] for piece in ordered], axis=0)
    value_all = jnp.concatenate([piece[1] for piece in ordered], axis=0)
    doc_all = jnp.concatenate([piece[2] for piece in ordered], axis=0)
    offsets = jnp.arange(row_count, dtype=jnp.int32)
    query_pos = position * row_count + offsets
    key_pos = jnp.concatenate(
        [(position - (HOPS - index)) * row_count + offsets for index in range(HOPS + 1)], axis=0
    )
    distance = query_pos[:, None] - key_pos[None, :]
    admissible = (key_pos[None, :] >= 0) & (distance >= 0) & (doc_ids[:, None] == doc_all[None, :])
    results = []
    for kv_head in range(kv_local):
        low_col = kv_head * group_size * HEAD_DIM
        high_col = (kv_head + 1) * group_size * HEAD_DIM
        query_grp = queries[:, low_col:high_col].reshape(row_count, group_size, HEAD_DIM)
        grad_grp = cotangent[:, low_col:high_col].reshape(row_count, group_size, HEAD_DIM)
        key_head = key_all[:, kv_head * HEAD_DIM : (kv_head + 1) * HEAD_DIM]
        value_head = value_all[:, kv_head * HEAD_DIM : (kv_head + 1) * HEAD_DIM]
        head_reach = windows[kv_head * group_size : (kv_head + 1) * group_size]
        score_mask = admissible[None] & (distance[None] < head_reach[:, None, None])
        results.append(
            dense_pass(query_grp, grad_grp, key_head, value_head, score_mask, score_scale)
        )
    attended = jnp.concatenate(
        [entry[0].reshape(row_count, group_size * HEAD_DIM) for entry in results], axis=1
    ).astype(jnp.bfloat16)
    grad_queries = jnp.concatenate(
        [entry[1].reshape(row_count, group_size * HEAD_DIM) for entry in results], axis=1
    ).astype(jnp.bfloat16)
    key_grad_all = jnp.concatenate([entry[2] for entry in results], axis=1)
    value_grad_all = jnp.concatenate([entry[3] for entry in results], axis=1)

    def block_of(array, index):
        return array[index * row_count : (index + 1) * row_count]

    travel = (block_of(key_grad_all, 0), block_of(value_grad_all, 0))
    for travel_step in range(HOPS):
        travel = from_behind((travel[0], travel[1]), "ctx", -1)
        travel = (
            travel[0] + block_of(key_grad_all, travel_step + 1),
            travel[1] + block_of(value_grad_all, travel_step + 1),
        )
    total_key, total_value = travel
    return (
        attended,
        grad_queries,
        total_key.astype(jnp.bfloat16),
        total_value.astype(jnp.bfloat16),
    )


def solution(mesh):
    return jax.shard_map(
        per_device,
        mesh=mesh,
        in_specs=(
            P(("dp", "ctx"), "head"),
            P(("dp", "ctx"), "head"),
            P(("dp", "ctx"), "head"),
            P(("dp", "ctx"), "head"),
            P(("dp", "ctx")),
            P(("dp", "ctx")),
            P("head"),
        ),
        out_specs=(
            P(("dp", "ctx"), "head"),
            P(("dp", "ctx"), "head"),
            P(("dp", "ctx"), "head"),
            P(("dp", "ctx"), "head"),
        ),
        check_vma=False,
    )
```

profile of v0, /device:TPU:0, one launch (start us, length us, event | category | flops | bytes accessed | tf_op | source)
XLA Modules:
  0.0 230.9 jit_solution(421692749174872316)
XLA Ops:
  0.6 5.0 %collective-permute-start.6 = (s32[128]{0:T(128)}, s32[128]{0:T(128)S(1)}, u32[]{:S(2)}, u32[]{:S(2)}) collective-permute-start(s32[128]{0:T(128)} %param.11), channel_id=1, source_target_pairs={{0,2},{2,4},{4,6},{6,8},{8,10},{10,12},{12,14},{14,16},{16,18},{18... | collective-permute-start | bytes 1544 | tf_op jit(solution)/shard_map/ppermute | solution.py:13
  6.7 3.4 %collective-permute-start = (bf16[128,512]{0,1:T(8,128)(2,1)S(1)}, bf16[128,512]{0,1:T(8,128)(2,1)S(1)}, u32[]{:S(2)}, u32[]{:S(2)}) collective-permute-start(bf16[128,512]{0,1:T(8,128)(2,1)S(1)} %copy.59), channel_id=1, source_target_pairs={{0,2},{2,4},{4,6},{6,8},{8,10},{10,12},{12,14},{14,16},{16,18},{18... | collective-permute-start | bytes 393224 | tf_op jit(solution)/shard_map/ppermute | solution.py:13
  10.1 3.4 %collective-permute-start.12 = (bf16[128,512]{1,0:T(8,128)(2,1)}, bf16[128,512]{1,0:T(8,128)(2,1)S(1)}, u32[]{:S(2)}, u32[]{:S(2)}) collective-permute-start(bf16[128,512]{1,0:T(8,128)(2,1)} %param.8), channel_id=1, source_target_pairs={{0,2},{2,4},{4,6},{6,8},{8,10},{10,12},{12,14},{14,16},{16,18},{18... | collective-permute-start | bytes 393224 | tf_op jit(solution)/shard_map/ppermute | solution.py:13
  15.4 38.7 %psum.7 = f32[]{:T(128)} all-reduce(f32[]{:T(128)} %convert_reduce_fusion), channel_id=1, replica_groups=mesh['ctx'=16,'head'=2,'dp'=1] {'ctx'}, use_global_device_ids=true, to_apply=%region_9.10 | all-reduce | flops 1 | bytes 8 | tf_op jit(solution)/shard_map/psum | solution.py:56
  56.2 2.4 %collective-permute-start.7 = (s32[128]{0:T(128)S(1)}, s32[128]{0:T(128)S(1)}, u32[]{:S(2)}, u32[]{:S(2)}) collective-permute-start(s32[128]{0:T(128)S(1)} %collective-permute-done.6), channel_id=1, source_target_pairs={{0,2},{2,4},{4,6},{6,8},{8,10},{10,12},{12,14},{14,16},{16,18},{18... | collective-permute-start | bytes 1544 | tf_op jit(solution)/shard_map/ppermute | solution.py:13
  59.9 4.1 %collective-permute-start.8 = (s32[128]{0:T(128)S(1)}, s32[128]{0:T(128)S(1)}, u32[]{:S(2)}, u32[]{:S(2)}) collective-permute-start(s32[128]{0:T(128)S(1)} %collective-permute-done.7), channel_id=1, source_target_pairs={{0,2},{2,4},{4,6},{6,8},{8,10},{10,12},{12,14},{14,16},{16,18},{18... | collective-permute-start | bytes 1544 | tf_op jit(solution)/shard_map/ppermute | solution.py:13
  65.4 4.1 %collective-permute-start.9 = (s32[128]{0:T(128)S(1)}, s32[128]{0:T(128)S(1)}, u32[]{:S(2)}, u32[]{:S(2)}) collective-permute-start(s32[128]{0:T(128)S(1)} %collective-permute-done.8), channel_id=1, source_target_pairs={{0,2},{2,4},{4,6},{6,8},{8,10},{10,12},{12,14},{14,16},{16,18},{18... | collective-permute-start | bytes 1544 | tf_op jit(solution)/shard_map/ppermute | solution.py:13
  70.8 4.1 %collective-permute-start.10 = (s32[128]{0:T(128)S(1)}, s32[128]{0:T(128)S(1)}, u32[]{:S(2)}, u32[]{:S(2)}) collective-permute-start(s32[128]{0:T(128)S(1)} %collective-permute-done.9), channel_id=1, source_target_pairs={{0,2},{2,4},{4,6},{6,8},{8,10},{10,12},{12,14},{14,16},{16,18},{18... | collective-permute-start | bytes 1544 | tf_op jit(solution)/shard_map/ppermute | solution.py:13
  74.9 4.6 %collective-permute-start.13 = (bf16[128,512]{1,0:T(8,128)(2,1)S(1)}, bf16[128,512]{1,0:T(8,128)(2,1)S(1)}, u32[]{:S(2)}, u32[]{:S(2)}) collective-permute-start(bf16[128,512]{1,0:T(8,128)(2,1)S(1)} %collective-permute-done.12), channel_id=1, source_target_pairs={{0,2},{2,4},{4,6},{6,8},{8,10},{10,12},{12,14},{14,16},{16,18},{18... | collective-permute-start | bytes 393224 | tf_op jit(solution)/shard_map/ppermute | solution.py:13
  85.2 3.9 %collective-permute-start.1 = (bf16[128,512]{0,1:T(8,128)(2,1)S(1)}, bf16[128,512]{0,1:T(8,128)(2,1)S(1)}, u32[]{:S(2)}, u32[]{:S(2)}) collective-permute-start(bf16[128,512]{0,1:T(8,128)(2,1)S(1)} %collective-permute-done), channel_id=1, source_target_pairs={{0,2},{2,4},{4,6},{6,8},{8,10},{10,12},{12,14},{14,16},{16,18},{18... | collective-permute-start | bytes 393224 | tf_op jit(solution)/shard_map/ppermute | solution.py:13
  89.1 3.8 %collective-permute-start.14 = (bf16[128,512]{1,0:T(8,128)(2,1)S(1)}, bf16[128,512]{1,0:T(8,128)(2,1)S(1)}, u32[]{:S(2)}, u32[]{:S(2)}) collective-permute-start(bf16[128,512]{1,0:T(8,128)(2,1)S(1)} %collective-permute-done.13), channel_id=1, source_target_pairs={{0,2},{2,4},{4,6},{6,8},{8,10},{10,12},{12,14},{14,16},{16,18},{18... | collective-permute-start | bytes 393224 | tf_op jit(solution)/shard_map/ppermute | solution.py:13
  92.9 4.2 %collective-permute-start.2 = (bf16[128,512]{0,1:T(8,128)(2,1)S(1)}, bf16[128,512]{0,1:T(8,128)(2,1)S(1)}, u32[]{:S(2)}, u32[]{:S(2)}) collective-permute-start(bf16[128,512]{0,1:T(8,128)(2,1)S(1)} %collective-permute-done.1), channel_id=1, source_target_pairs={{0,2},{2,4},{4,6},{6,8},{8,10},{10,12},{12,14},{14,16},{16,18},{18... | collective-permute-start | bytes 393224 | tf_op jit(solution)/shard_map/ppermute | solution.py:13
  97.2 4.2 %collective-permute-start.15 = (bf16[128,512]{1,0:T(8,128)(2,1)S(1)}, bf16[128,512]{1,0:T(8,128)(2,1)S(1)}, u32[]{:S(2)}, u32[]{:S(2)}) collective-permute-start(bf16[128,512]{1,0:T(8,128)(2,1)S(1)} %collective-permute-done.14), channel_id=1, source_target_pairs={{0,2},{2,4},{4,6},{6,8},{8,10},{10,12},{12,14},{14,16},{16,18},{18... | collective-permute-start | bytes 393224 | tf_op jit(solution)/shard_map/ppermute | solution.py:13
  101.4 2.9 %collective-permute-start.3 = (bf16[128,512]{0,1:T(8,128)(2,1)S(1)}, bf16[128,512]{0,1:T(8,128)(2,1)S(1)}, u32[]{:S(2)}, u32[]{:S(2)}) collective-permute-start(bf16[128,512]{0,1:T(8,128)(2,1)S(1)} %collective-permute-done.2), channel_id=1, source_target_pairs={{0,2},{2,4},{4,6},{6,8},{8,10},{10,12},{12,14},{14,16},{16,18},{18... | collective-permute-start | bytes 393224 | tf_op jit(solution)/shard_map/ppermute | solution.py:13
  104.4 5.3 %collective-permute-start.16 = (bf16[128,512]{1,0:T(8,128)(2,1)S(1)}, bf16[128,512]{1,0:T(8,128)(2,1)S(1)}, u32[]{:S(2)}, u32[]{:S(2)}) collective-permute-start(bf16[128,512]{1,0:T(8,128)(2,1)S(1)} %collective-permute-done.15), channel_id=1, source_target_pairs={{0,2},{2,4},{4,6},{6,8},{8,10},{10,12},{12,14},{14,16},{16,18},{18... | collective-permute-start | bytes 393224 | tf_op jit(solution)/shard_map/ppermute | solution.py:13
  109.8 3.7 %collective-permute-start.4 = (bf16[128,512]{0,1:T(8,128)(2,1)S(1)}, bf16[128,512]{0,1:T(8,128)(2,1)S(1)}, u32[]{:S(2)}, u32[]{:S(2)}) collective-permute-start(bf16[128,512]{0,1:T(8,128)(2,1)S(1)} %collective-permute-done.3), channel_id=1, source_target_pairs={{0,2},{2,4},{4,6},{6,8},{8,10},{10,12},{12,14},{14,16},{16,18},{18... | collective-permute-start | bytes 393224 | tf_op jit(solution)/shard_map/ppermute | solution.py:13
  113.5 6.2 %collective-permute-start.17 = (bf16[128,512]{1,0:T(8,128)(2,1)S(1)}, bf16[128,512]{1,0:T(8,128)(2,1)S(1)}, u32[]{:S(2)}, u32[]{:S(2)}) collective-permute-start(bf16[128,512]{1,0:T(8,128)(2,1)S(1)} %collective-permute-done.16), channel_id=1, source_target_pairs={{0,2},{2,4},{4,6},{6,8},{8,10},{10,12},{12,14},{14,16},{16,18},{18... | collective-permute-start | bytes 393224 | tf_op jit(solution)/shard_map/ppermute | solution.py:13
  121.1 2.4 %collective-permute-start.5 = (bf16[128,512]{0,1:T(8,128)(2,1)S(1)}, bf16[128,512]{0,1:T(8,128)(2,1)S(1)}, u32[]{:S(2)}, u32[]{:S(2)}) collective-permute-start(bf16[128,512]{0,1:T(8,128)(2,1)S(1)} %collective-permute-done.4), channel_id=1, source_target_pairs={{0,2},{2,4},{4,6},{6,8},{8,10},{10,12},{12,14},{14,16},{16,18},{18... | collective-permute-start | bytes 393224 | tf_op jit(solution)/shard_map/ppermute | solution.py:13
  123.7 2.3 %collective-permute-done.5 = bf16[128,512]{0,1:T(8,128)(2,1)S(1)} collective-permute-done((bf16[128,512]{0,1:T(8,128)(2,1)S(1)}, bf16[128,512]{0,1:T(8,128)(2,1)S(1)}, u32[]{:S(2)}, u32[]{:S(2)}) %collective-permute-start.5) | collective-permute-done | bytes 131104 | tf_op jit(solution)/shard_map/ppermute | solution.py:13
  134.4 2.0 fusion.43
  142.4 2.0 fusion.42
  149.9 2.1 fusion.41
  159.9 9.7 %collective-permute-done.24 = f32[128,512]{0,1:T(8,128)S(1)} collective-permute-done((f32[128,512]{0,1:T(8,128)S(1)}, f32[128,512]{0,1:T(8,128)S(1)}, u32[]{:S(2)}, u32[]{:S(2)}) %collective-permute-start.24) | collective-permute-done | bytes 262176 | tf_op jit(solution)/shard_map/ppermute | solution.py:13
  171.1 4.1 %collective-permute-done.18 = f32[128,512]{0,1:T(8,128)S(1)} collective-permute-done((f32[128,512]{0,1:T(8,128)S(1)}, f32[128,512]{0,1:T(8,128)S(1)}, u32[]{:S(2)}, u32[]{:S(2)}) %collective-permute-start.18) | collective-permute-done | bytes 262176 | tf_op jit(solution)/shard_map/ppermute | solution.py:13
  176.9 4.2 %collective-permute-done.25 = f32[128,512]{0,1:T(8,128)S(1)} collective-permute-done((f32[128,512]{0,1:T(8,128)S(1)}, f32[128,512]{0,1:T(8,128)S(1)}, u32[]{:S(2)}, u32[]{:S(2)}) %collective-permute-start.25) | collective-permute-done | bytes 262176 | tf_op jit(solution)/shard_map/ppermute | solution.py:13
  182.4 4.8 %collective-permute-done.19 = f32[128,512]{0,1:T(8,128)S(1)} collective-permute-done((f32[128,512]{0,1:T(8,128)S(1)}, f32[128,512]{0,1:T(8,128)S(1)}, u32[]{:S(2)}, u32[]{:S(2)}) %collective-permute-start.19) | collective-permute-done | bytes 262176 | tf_op jit(solution)/shard_map/ppermute | solution.py:13
  188.9 5.0 %collective-permute-done.26 = f32[128,512]{0,1:T(8,128)S(1)} collective-permute-done((f32[128,512]{0,1:T(8,128)S(1)}, f32[128,512]{0,1:T(8,128)S(1)}, u32[]{:S(2)}, u32[]{:S(2)}) %collective-permute-start.26) | collective-permute-done | bytes 262176 | tf_op jit(solution)/shard_map/ppermute | solution.py:13
  195.3 4.2 %collective-permute-done.20 = f32[128,512]{0,1:T(8,128)S(1)} collective-permute-done((f32[128,512]{0,1:T(8,128)S(1)}, f32[128,512]{0,1:T(8,128)S(1)}, u32[]{:S(2)}, u32[]{:S(2)}) %collective-permute-start.20) | collective-permute-done | bytes 262176 | tf_op jit(solution)/shard_map/ppermute | solution.py:13
  201.3 4.3 %collective-permute-done.27 = f32[128,512]{0,1:T(8,128)S(1)} collective-permute-done((f32[128,512]{0,1:T(8,128)S(1)}, f32[128,512]{0,1:T(8,128)S(1)}, u32[]{:S(2)}, u32[]{:S(2)}) %collective-permute-start.27) | collective-permute-done | bytes 262176 | tf_op jit(solution)/shard_map/ppermute | solution.py:13
  212.9 2.8 %collective-permute-done.28 = f32[128,512]{0,1:T(8,128)} collective-permute-done((f32[128,512]{0,1:T(8,128)}, f32[128,512]{0,1:T(8,128)}, u32[]{:S(2)}, u32[]{:S(2)}) %collective-permute-start.28) | collective-permute-done | bytes 262176 | tf_op jit(solution)/shard_map/ppermute | solution.py:13
  222.4 3.5 %collective-permute-done.29 = f32[128,512]{0,1:T(8,128)S(1)} collective-permute-done((f32[128,512]{0,1:T(8,128)S(1)}, f32[128,512]{0,1:T(8,128)S(1)}, u32[]{:S(2)}, u32[]{:S(2)}) %collective-permute-start.29) | collective-permute-done | bytes 262176 | tf_op jit(solution)/shard_map/ppermute | solution.py:13
  226.7 2.4 %collective-permute-done.23 = f32[128,512]{0,1:T(8,128)S(1)} collective-permute-done((f32[128,512]{0,1:T(8,128)S(1)}, f32[128,512]{0,1:T(8,128)S(1)}, u32[]{:S(2)}, u32[]{:S(2)}) %collective-permute-start.23) | collective-permute-done | bytes 262176 | tf_op jit(solution)/shard_map/ppermute | solution.py:13
  (193 shorter events, 68.4 us)
Async XLA Ops:
  0.6 55.4 %copy-start.23 = (bf16[128,2048]{1,0:T(8,128)(2,1)S(1)}, bf16[128,2048]{1,0:T(8,128)(2,1)}, u32[]{:S(2)}) copy-start(bf16[128,2048]{1,0:T(8,128)(2,1)} %param.7) | copy-start | bytes 1572868
  0.6 55.6 %collective-permute-start.6 = (s32[128]{0:T(128)}, s32[128]{0:T(128)S(1)}, u32[]{:S(2)}, u32[]{:S(2)}) collective-permute-start(s32[128]{0:T(128)} %param.11), channel_id=1, source_target_pairs={{0,2},{2,4},{4,6},{6,8},{8,10},{10,12},{12,14},{14,16},{16,18},{18... | collective-permute-start | bytes 1544 | tf_op jit(solution)/shard_map/ppermute | solution.py:13
  6.7 78.5 %collective-permute-start = (bf16[128,512]{0,1:T(8,128)(2,1)S(1)}, bf16[128,512]{0,1:T(8,128)(2,1)S(1)}, u32[]{:S(2)}, u32[]{:S(2)}) collective-permute-start(bf16[128,512]{0,1:T(8,128)(2,1)S(1)} %copy.59), channel_id=1, source_target_pairs={{0,2},{2,4},{4,6},{6,8},{8,10},{10,12},{12,14},{14,16},{16,18},{18... | collective-permute-start | bytes 393224 | tf_op jit(solution)/shard_map/ppermute | solution.py:13
  10.1 64.9 %collective-permute-start.12 = (bf16[128,512]{1,0:T(8,128)(2,1)}, bf16[128,512]{1,0:T(8,128)(2,1)S(1)}, u32[]{:S(2)}, u32[]{:S(2)}) collective-permute-start(bf16[128,512]{1,0:T(8,128)(2,1)} %param.8), channel_id=1, source_target_pairs={{0,2},{2,4},{4,6},{6,8},{8,10},{10,12},{12,14},{14,16},{16,18},{18... | collective-permute-start | bytes 393224 | tf_op jit(solution)/shard_map/ppermute | solution.py:13
  15.4 64.2 %copy-start.28 = (s32[16]{0:T(128)S(1)}, s32[16]{0:T(128)}, u32[]{:S(2)}) copy-start(s32[16]{0:T(128)} %param.13) | copy-start | bytes 196
  56.2 3.7 %collective-permute-start.7 = (s32[128]{0:T(128)S(1)}, s32[128]{0:T(128)S(1)}, u32[]{:S(2)}, u32[]{:S(2)}) collective-permute-start(s32[128]{0:T(128)S(1)} %collective-permute-done.6), channel_id=1, source_target_pairs={{0,2},{2,4},{4,6},{6,8},{8,10},{10,12},{12,14},{14,16},{16,18},{18... | collective-permute-start | bytes 1544 | tf_op jit(solution)/shard_map/ppermute | solution.py:13
  59.9 5.4 %collective-permute-start.8 = (s32[128]{0:T(128)S(1)}, s32[128]{0:T(128)S(1)}, u32[]{:S(2)}, u32[]{:S(2)}) collective-permute-start(s32[128]{0:T(128)S(1)} %collective-permute-done.7), channel_id=1, source_target_pairs={{0,2},{2,4},{4,6},{6,8},{8,10},{10,12},{12,14},{14,16},{16,18},{18... | collective-permute-start | bytes 1544 | tf_op jit(solution)/shard_map/ppermute | solution.py:13
  65.4 5.4 %collective-permute-start.9 = (s32[128]{0:T(128)S(1)}, s32[128]{0:T(128)S(1)}, u32[]{:S(2)}, u32[]{:S(2)}) collective-permute-start(s32[128]{0:T(128)S(1)} %collective-permute-done.8), channel_id=1, source_target_pairs={{0,2},{2,4},{4,6},{6,8},{8,10},{10,12},{12,14},{14,16},{16,18},{18... | collective-permute-start | bytes 1544 | tf_op jit(solution)/shard_map/ppermute | solution.py:13
  70.8 9.9 %collective-permute-start.10 = (s32[128]{0:T(128)S(1)}, s32[128]{0:T(128)S(1)}, u32[]{:S(2)}, u32[]{:S(2)}) collective-permute-start(s32[128]{0:T(128)S(1)} %collective-permute-done.9), channel_id=1, source_target_pairs={{0,2},{2,4},{4,6},{6,8},{8,10},{10,12},{12,14},{14,16},{16,18},{18... | collective-permute-start | bytes 1544 | tf_op jit(solution)/shard_map/ppermute | solution.py:13
  74.9 14.2 %collective-permute-start.13 = (bf16[128,512]{1,0:T(8,128)(2,1)S(1)}, bf16[128,512]{1,0:T(8,128)(2,1)S(1)}, u32[]{:S(2)}, u32[]{:S(2)}) collective-permute-start(bf16[128,512]{1,0:T(8,128)(2,1)S(1)} %collective-permute-done.12), channel_id=1, source_target_pairs={{0,2},{2,4},{4,6},{6,8},{8,10},{10,12},{12,14},{14,16},{16,18},{18... | collective-permute-start | bytes 393224 | tf_op jit(solution)/shard_map/ppermute | solution.py:13
  80.7 4.5 %collective-permute-start.11 = (s32[128]{0:T(128)S(1)}, s32[128]{0:T(128)S(1)}, u32[]{:S(2)}, u32[]{:S(2)}) collective-permute-start(s32[128]{0:T(128)S(1)} %collective-permute-done.10), channel_id=1, source_target_pairs={{0,2},{2,4},{4,6},{6,8},{8,10},{10,12},{12,14},{14,16},{16,18},{18... | collective-permute-start | bytes 1544 | tf_op jit(solution)/shard_map/ppermute | solution.py:13
  85.2 7.7 %collective-permute-start.1 = (bf16[128,512]{0,1:T(8,128)(2,1)S(1)}, bf16[128,512]{0,1:T(8,128)(2,1)S(1)}, u32[]{:S(2)}, u32[]{:S(2)}) collective-permute-start(bf16[128,512]{0,1:T(8,128)(2,1)S(1)} %collective-permute-done), channel_id=1, source_target_pairs={{0,2},{2,4},{4,6},{6,8},{8,10},{10,12},{12,14},{14,16},{16,18},{18... | collective-permute-start | bytes 393224 | tf_op jit(solution)/shard_map/ppermute | solution.py:13
  89.1 8.0 %collective-permute-start.14 = (bf16[128,512]{1,0:T(8,128)(2,1)S(1)}, bf16[128,512]{1,0:T(8,128)(2,1)S(1)}, u32[]{:S(2)}, u32[]{:S(2)}) collective-permute-start(bf16[128,512]{1,0:T(8,128)(2,1)S(1)} %collective-permute-done.13), channel_id=1, source_target_pairs={{0,2},{2,4},{4,6},{6,8},{8,10},{10,12},{12,14},{14,16},{16,18},{18... | collective-permute-start | bytes 393224 | tf_op jit(solution)/shard_map/ppermute | solution.py:13
  92.9 8.5 %collective-permute-start.2 = (bf16[128,512]{0,1:T(8,128)(2,1)S(1)}, bf16[128,512]{0,1:T(8,128)(2,1)S(1)}, u32[]{:S(2)}, u32[]{:S(2)}) collective-permute-start(bf16[128,512]{0,1:T(8,128)(2,1)S(1)} %collective-permute-done.1), channel_id=1, source_target_pairs={{0,2},{2,4},{4,6},{6,8},{8,10},{10,12},{12,14},{14,16},{16,18},{18... | collective-permute-start | bytes 393224 | tf_op jit(solution)/shard_map/ppermute | solution.py:13
  97.2 7.2 %collective-permute-start.15 = (bf16[128,512]{1,0:T(8,128)(2,1)S(1)}, bf16[128,512]{1,0:T(8,128)(2,1)S(1)}, u32[]{:S(2)}, u32[]{:S(2)}) collective-permute-start(bf16[128,512]{1,0:T(8,128)(2,1)S(1)} %collective-permute-done.14), channel_id=1, source_target_pairs={{0,2},{2,4},{4,6},{6,8},{8,10},{10,12},{12,14},{14,16},{16,18},{18... | collective-permute-start | bytes 393224 | tf_op jit(solution)/shard_map/ppermute | solution.py:13
  101.4 8.3 %collective-permute-start.3 = (bf16[128,512]{0,1:T(8,128)(2,1)S(1)}, bf16[128,512]{0,1:T(8,128)(2,1)S(1)}, u32[]{:S(2)}, u32[]{:S(2)}) collective-permute-start(bf16[128,512]{0,1:T(8,128)(2,1)S(1)} %collective-permute-done.2), channel_id=1, source_target_pairs={{0,2},{2,4},{4,6},{6,8},{8,10},{10,12},{12,14},{14,16},{16,18},{18... | collective-permute-start | bytes 393224 | tf_op jit(solution)/shard_map/ppermute | solution.py:13
  104.4 9.1 %collective-permute-start.16 = (bf16[128,512]{1,0:T(8,128)(2,1)S(1)}, bf16[128,512]{1,0:T(8,128)(2,1)S(1)}, u32[]{:S(2)}, u32[]{:S(2)}) collective-permute-start(bf16[128,512]{1,0:T(8,128)(2,1)S(1)} %collective-permute-done.15), channel_id=1, source_target_pairs={{0,2},{2,4},{4,6},{6,8},{8,10},{10,12},{12,14},{14,16},{16,18},{18... | collective-permute-start | bytes 393224 | tf_op jit(solution)/shard_map/ppermute | solution.py:13
  109.8 11.3 %collective-permute-start.4 = (bf16[128,512]{0,1:T(8,128)(2,1)S(1)}, bf16[128,512]{0,1:T(8,128)(2,1)S(1)}, u32[]{:S(2)}, u32[]{:S(2)}) collective-permute-start(bf16[128,512]{0,1:T(8,128)(2,1)S(1)} %collective-permute-done.3), channel_id=1, source_target_pairs={{0,2},{2,4},{4,6},{6,8},{8,10},{10,12},{12,14},{14,16},{16,18},{18... | collective-permute-start | bytes 393224 | tf_op jit(solution)/shard_map/ppermute | solution.py:13
  113.5 10.0 %collective-permute-start.17 = (bf16[128,512]{1,0:T(8,128)(2,1)S(1)}, bf16[128,512]{1,0:T(8,128)(2,1)S(1)}, u32[]{:S(2)}, u32[]{:S(2)}) collective-permute-start(bf16[128,512]{1,0:T(8,128)(2,1)S(1)} %collective-permute-done.16), channel_id=1, source_target_pairs={{0,2},{2,4},{4,6},{6,8},{8,10},{10,12},{12,14},{14,16},{16,18},{18... | collective-permute-start | bytes 393224 | tf_op jit(solution)/shard_map/ppermute | solution.py:13
  121.1 4.9 %collective-permute-start.5 = (bf16[128,512]{0,1:T(8,128)(2,1)S(1)}, bf16[128,512]{0,1:T(8,128)(2,1)S(1)}, u32[]{:S(2)}, u32[]{:S(2)}) collective-permute-start(bf16[128,512]{0,1:T(8,128)(2,1)S(1)} %collective-permute-done.4), channel_id=1, source_target_pairs={{0,2},{2,4},{4,6},{6,8},{8,10},{10,12},{12,14},{14,16},{16,18},{18... | collective-permute-start | bytes 393224 | tf_op jit(solution)/shard_map/ppermute | solution.py:13
  156.1 13.5 %collective-permute-start.24 = (f32[128,512]{0,1:T(8,128)S(1)}, f32[128,512]{0,1:T(8,128)S(1)}, u32[]{:S(2)}, u32[]{:S(2)}) collective-permute-start(f32[128,512]{0,1:T(8,128)S(1)} %slice.155), channel_id=1, source_target_pairs={{2,0},{4,2},{6,4},{8,6},{10,8},{12,10},{14,12},{16,14},{18,16},{20... | collective-permute-start | bytes 786440 | tf_op jit(solution)/shard_map/ppermute | solution.py:13
  158.4 16.8 %collective-permute-start.18 = (f32[128,512]{0,1:T(8,128)S(1)}, f32[128,512]{0,1:T(8,128)S(1)}, u32[]{:S(2)}, u32[]{:S(2)}) collective-permute-start(f32[128,512]{0,1:T(8,128)S(1)} %slice.148), channel_id=1, source_target_pairs={{2,0},{4,2},{6,4},{8,6},{10,8},{12,10},{14,12},{16,14},{18,16},{20... | collective-permute-start | bytes 786440 | tf_op jit(solution)/shard_map/ppermute | solution.py:13
  169.6 11.5 %collective-permute-start.25 = (f32[128,512]{0,1:T(8,128)S(1)}, f32[128,512]{0,1:T(8,128)S(1)}, u32[]{:S(2)}, u32[]{:S(2)}) collective-permute-start(f32[128,512]{0,1:T(8,128)S(1)} %slice_add_fusion.5), channel_id=1, source_target_pairs={{2,0},{4,2},{6,4},{8,6},{10,8},{12,10},{14,12},{16,14},{18,16},{20... | collective-permute-start | bytes 786440 | tf_op jit(solution)/shard_map/ppermute | solution.py:13
  175.2 12.0 %collective-permute-start.19 = (f32[128,512]{0,1:T(8,128)S(1)}, f32[128,512]{0,1:T(8,128)S(1)}, u32[]{:S(2)}, u32[]{:S(2)}) collective-permute-start(f32[128,512]{0,1:T(8,128)S(1)} %slice_add_fusion.11), channel_id=1, source_target_pairs={{2,0},{4,2},{6,4},{8,6},{10,8},{12,10},{14,12},{16,14},{18,16},{20... | collective-permute-start | bytes 786440 | tf_op jit(solution)/shard_map/ppermute | solution.py:13
  181.1 12.8 %collective-permute-start.26 = (f32[128,512]{0,1:T(8,128)S(1)}, f32[128,512]{0,1:T(8,128)S(1)}, u32[]{:S(2)}, u32[]{:S(2)}) collective-permute-start(f32[128,512]{0,1:T(8,128)S(1)} %slice_add_fusion.4), channel_id=1, source_target_pairs={{2,0},{4,2},{6,4},{8,6},{10,8},{12,10},{14,12},{16,14},{18,16},{20... | collective-permute-start | bytes 786440 | tf_op jit(solution)/shard_map/ppermute | solution.py:13
  187.3 12.2 %collective-permute-start.20 = (f32[128,512]{0,1:T(8,128)S(1)}, f32[128,512]{0,1:T(8,128)S(1)}, u32[]{:S(2)}, u32[]{:S(2)}) collective-permute-start(f32[128,512]{0,1:T(8,128)S(1)} %slice_add_fusion.10), channel_id=1, source_target_pairs={{2,0},{4,2},{6,4},{8,6},{10,8},{12,10},{14,12},{16,14},{18,16},{20... | collective-permute-start | bytes 786440 | tf_op jit(solution)/shard_map/ppermute | solution.py:13
  194.0 11.6 %collective-permute-start.27 = (f32[128,512]{0,1:T(8,128)S(1)}, f32[128,512]{0,1:T(8,128)S(1)}, u32[]{:S(2)}, u32[]{:S(2)}) collective-permute-start(f32[128,512]{0,1:T(8,128)S(1)} %slice_add_fusion.3), channel_id=1, source_target_pairs={{2,0},{4,2},{6,4},{8,6},{10,8},{12,10},{14,12},{16,14},{18,16},{20... | collective-permute-start | bytes 786440 | tf_op jit(solution)/shard_map/ppermute | solution.py:13
  199.5 9.2 %collective-permute-start.21 = (f32[128,512]{0,1:T(8,128)S(1)}, f32[128,512]{0,1:T(8,128)S(1)}, u32[]{:S(2)}, u32[]{:S(2)}) collective-permute-start(f32[128,512]{0,1:T(8,128)S(1)} %slice_add_fusion.9), channel_id=1, source_target_pairs={{2,0},{4,2},{6,4},{8,6},{10,8},{12,10},{14,12},{16,14},{18,16},{20... | collective-permute-start | bytes 786440 | tf_op jit(solution)/shard_map/ppermute | solution.py:13
  206.3 9.4 %collective-permute-start.28 = (f32[128,512]{0,1:T(8,128)}, f32[128,512]{0,1:T(8,128)}, u32[]{:S(2)}, u32[]{:S(2)}) collective-permute-start(f32[128,512]{0,1:T(8,128)} %slice_add_fusion.2), channel_id=1, source_target_pairs={{2,0},{4,2},{6,4},{8,6},{10,8},{12,10},{14,12},{16,14},{18,16},{20... | collective-permute-start | bytes 786440 | tf_op jit(solution)/shard_map/ppermute | solution.py:13
  209.4 9.5 %collective-permute-start.22 = (f32[128,512]{0,1:T(8,128)}, f32[128,512]{0,1:T(8,128)}, u32[]{:S(2)}, u32[]{:S(2)}) collective-permute-start(f32[128,512]{0,1:T(8,128)} %slice_add_fusion.8), channel_id=1, source_target_pairs={{2,0},{4,2},{6,4},{8,6},{10,8},{12,10},{14,12},{16,14},{18,16},{20... | collective-permute-start | bytes 786440 | tf_op jit(solution)/shard_map/ppermute | solution.py:13
  216.7 9.2 %collective-permute-start.29 = (f32[128,512]{0,1:T(8,128)S(1)}, f32[128,512]{0,1:T(8,128)S(1)}, u32[]{:S(2)}, u32[]{:S(2)}) collective-permute-start(f32[128,512]{0,1:T(8,128)S(1)} %slice_add_fusion.1), channel_id=1, source_target_pairs={{2,0},{4,2},{6,4},{8,6},{10,8},{12,10},{14,12},{16,14},{18,16},{20... | collective-permute-start | bytes 786440 | tf_op jit(solution)/shard_map/ppermute | solution.py:13
  219.9 9.2 %collective-permute-start.23 = (f32[128,512]{0,1:T(8,128)S(1)}, f32[128,512]{0,1:T(8,128)S(1)}, u32[]{:S(2)}, u32[]{:S(2)}) collective-permute-start(f32[128,512]{0,1:T(8,128)S(1)} %slice_add_fusion.7), channel_id=1, source_target_pairs={{2,0},{4,2},{6,4},{8,6},{10,8},{12,10},{14,12},{16,14},{18,16},{20... | collective-permute-start | bytes 786440 | tf_op jit(solution)/shard_map/ppermute | solution.py:13
  (28 other events, 317.8 us)
where the time goes:
time: 235 us; the launch traced here: 231 us
  starting transfers between devices  86.2 us (37%)
  waiting for transfers between devices  52.2 us (22%)
  blocking collectives  38.7 us (16%)
  matrix products  22.5 us (10%)
  local copies, waits for them, and re-layouts  16.7 us (7%)
  other arithmetic  12.2 us (5%)
  between operations  2.47 us (1%)
    ppermute x30, starting transfers between devices, from_behind(): return lax.ppermute(shard, axis, pairs)  86.2 us
    ppermute x30, waiting for transfers between devices, from_behind(): return lax.ppermute(shard, axis, pairs)  52.2 us
    psum x1, blocking collectives, per_device(): loss_count = lax.psum(jnp.sum(mask_float), 'ctx')  38.7 us
    unnamed x85, local copies, waits for them, and re-layouts  13.5 us
    sub x4, matrix products, softmax_rows(): raised = jnp.exp(scores - row_max)  7.96 us
  transfers between devices with their start and end apart: 30, of which 16 were waited for; matrix products, arithmetic and copies ran while one was open for 9% of the time, Pallas kernels for 0%

commit v1 on v0

v1 whole, which is shorter than its diff:
```python
import functools

import jax
import jax.numpy as jnp
from jax import lax
from jax.experimental import pallas as pl
from jax.experimental.pallas import tpu as pltpu
from jax.sharding import PartitionSpec as P

HEAD_DIM = 128
WINDOW = 768
AXIS = "ctx"
PAD = 16
PAIR = 2
BF16 = jnp.bfloat16
F32 = jnp.float32
NEG = -1e30
NT = (((1,), (1,)), ((), ()))
NN = (((1,), (0,)), ((), ()))


def dot(a, b, dims=NN):
    return lax.dot_general(a, b, dims, preferred_element_type=F32)


def block_at(index, size):
    return pl.ds(pl.multiple_of(index * size, size), size)


def call(kernel, out_shape, scalars, vectors, scratch=(), flops=0, nbytes=0, vmem=None):
    return pl.pallas_call(
        kernel,
        out_shape=out_shape,
        in_specs=[pl.BlockSpec(memory_space=pltpu.SMEM)] * len(scalars)
        + [pl.BlockSpec(memory_space=pltpu.VMEM)] * len(vectors),
        out_specs=jax.tree.map(lambda _: pl.BlockSpec(memory_space=pltpu.VMEM), out_shape),
        scratch_shapes=list(scratch),
        cost_estimate=pl.CostEstimate(flops=flops, bytes_accessed=nbytes, transcendentals=0),
        compiler_params=pltpu.CompilerParams(vmem_limit_bytes=vmem),
    )(*scalars, *vectors)


def pack_kv_kernel(group, r_ref, key_ref, value_ref, doc_ref, mask_ref, *out_refs):
    r = r_ref[0]
    rows = key_ref.shape[0]
    line = jnp.concatenate([doc_ref[...].astype(F32), mask_ref[...].astype(F32)], axis=1)
    tail = jnp.broadcast_to(line, (PAD, 2 * HEAD_DIM)).astype(BF16)
    for j in range(group):
        cols = block_at(r ^ j, HEAD_DIM)
        out_refs[j][0:rows, 0:HEAD_DIM] = key_ref[:, cols]
        out_refs[j][0:rows, HEAD_DIM:] = value_ref[:, cols]
        out_refs[j][rows:, :] = tail


def pack_qg_kernel(group, r_ref, query_ref, grad_ref, *out_refs):
    r = r_ref[0]
    width = query_ref.shape[1] // group
    for j in range(group):
        cols = block_at(r ^ j, width)
        out_refs[j][:, 0:width] = query_ref[:, cols]
        out_refs[j][:, width:] = grad_ref[:, cols]


def gather_kernel(group, needs, r_ref, *refs):
    slots, outs = refs[:group], refs[group:]
    r = r_ref[0]
    full, count_ref = outs[0], outs[-1]
    rows = full.shape[1] - PAD
    total = jnp.zeros((1, HEAD_DIM), F32)
    for j in range(group):
        full[r ^ j] = slots[j][...]
        total = total + slots[j][rows : rows + 1, HEAD_DIM:].astype(F32)
    count_ref[...] = jnp.broadcast_to(jnp.sum(total, axis=1, keepdims=True), count_ref.shape)
    for need, out in zip([n for n in needs if n < group], outs[1:-1]):
        out[...] = full[group - need :]


def attention_kernel(
    group, needs, heads, token_count, r_ref, base_ref, window_ref, count_ref, own_ref, *refs
):
    halo_refs, refs = refs[: len(needs)], refs[len(needs) :]
    qg_refs, refs = refs[:group], refs[group:]
    out_refs, refs = refs[:group], refs[group:]
    own_out, refs = refs[0], refs[1:]
    halo_outs, refs = refs[: len(needs)], refs[len(needs) :]
    keys, values, keys_t, values_t, dkeys, dvalues, qg, od, lines = refs
    r = r_ref[0]
    rows = own_ref.shape[1] - PAD
    hops = sum(needs)
    blocks = hops + group
    span = (hops + 1) * rows
    width = heads * HEAD_DIM
    scale = HEAD_DIM**-0.5
    exp_scale = scale * 1.4426950408889634
    lowest = jnp.maximum(hops * rows - base_ref[0], 0)

    pieces = []
    for need, ref in reversed(list(zip(needs, halo_refs))):
        pieces += [(ref, i) for i in range(need)]
    pieces += [(own_ref, i) for i in range(group)]
    lines[...] = jnp.zeros_like(lines)
    factor = token_count / jnp.maximum(count_ref[0:1, :], 1.0)
    for kb, (ref, i) in enumerate(pieces):
        at = slice(kb * rows, (kb + 1) * rows)
        key, value = ref[i, 0:rows, 0:HEAD_DIM], ref[i, 0:rows, HEAD_DIM:]
        keys[at, :] = key
        values[at, :] = value
        keys_t[:, at] = key.T
        values_t[:, at] = value.T
        doc = ref[i, rows : rows + 1, 0:HEAD_DIM].astype(F32)
        if kb < hops:
            doc = jnp.where(kb * rows < lowest, -1.0, doc)
        else:
            s = kb - hops
            mask = ref[i, rows : rows + 1, HEAD_DIM:].astype(F32)
            lines[blocks + s : blocks + s + 1, :] = mask * factor
        lines[kb : kb + 1, :] = doc
    columns = lines[...].T
    dkeys[...] = jnp.zeros_like(dkeys)
    dvalues[...] = jnp.zeros_like(dvalues)
    for j in range(group):
        qg[r ^ j] = qg_refs[j][...]

    lane = lax.broadcasted_iota(jnp.int32, (1, rows), 1)
    pos = lax.broadcasted_iota(jnp.int32, (span, PAIR * rows), 0)
    diag = lax.broadcasted_iota(jnp.int32, (rows, PAIR * rows), 0)
    own_lane = jnp.concatenate([lane] * PAIR, axis=1)
    for s in range(group):
        at = slice(s * rows, s * rows + span)
        doc_row = lines[hops + s : hops + s + 1, :]
        start = jnp.zeros((1, rows), F32)
        for kb in range(s, s + hops + 1):
            before = jnp.where(columns[:, kb : kb + 1] < doc_row, 1.0, 0.0)
            start = start + jnp.sum(before, axis=0, keepdims=True)
        start = jnp.maximum(start.astype(jnp.int32), lowest - s * rows)
        cot_col = columns[:, blocks + s : blocks + s + 1]
        for h0 in range(0, heads, PAIR):
            hs = range(h0, h0 + PAIR)
            low = jnp.concatenate(
                [
                    jnp.maximum(start, hops * rows + 1 + lane - window_ref[r * heads + h])
                    for h in hs
                ],
                axis=1,
            )
            query = jnp.concatenate(
                [qg[s, :, h * HEAD_DIM : (h + 1) * HEAD_DIM] for h in hs], axis=0
            )
            cots = [
                qg[s, :, width + h * HEAD_DIM : width + (h + 1) * HEAD_DIM].astype(F32) * cot_col
                for h in hs
            ]
            cots = [c.astype(BF16) for c in cots]
            cot = jnp.concatenate(cots, axis=0)
            cot_t = jnp.concatenate([c.T for c in cots], axis=1).astype(F32)
            scores = dot(keys[at, :], query, NT)
            allowed = pos >= low
            scores = jnp.where(allowed, scores, NEG)
            last = jnp.where(diag <= own_lane, scores[hops * rows :], NEG)
            scores = jnp.concatenate([scores[: hops * rows], last], axis=0)
            row_max = jnp.max(scores, axis=0, keepdims=True)
            raised = jnp.exp2(scores * exp_scale - row_max * exp_scale)
            weights = raised * (1.0 / jnp.sum(raised, axis=0, keepdims=True))
            weights_low = weights.astype(BF16)
            output_t = dot(values_t[:, at], weights_low)
            row_dot = jnp.sum(cot_t * output_t, axis=0, keepdims=True)
            grad_prob = dot(values[at, :], cot, NT)
            grad_score = (weights * (grad_prob - row_dot)).astype(BF16)
            dvalues[at, :] += dot(weights_low, cot)
            dkeys[at, :] += dot(grad_score, query)
            grad_query_t = dot(keys_t[:, at], grad_score) * scale
            for i, h in enumerate(hs):
                cut = slice(i * rows, (i + 1) * rows)
                od[s, :, h * HEAD_DIM : (h + 1) * HEAD_DIM] = output_t[:, cut].T.astype(BF16)
                od[s, :, width + h * HEAD_DIM : width + (h + 1) * HEAD_DIM] = grad_query_t[
                    :, cut
                ].T.astype(BF16)

    for j in range(group):
        out_refs[j][...] = od[r ^ j]
    first = hops * rows
    own_out[:, 0:HEAD_DIM] = dkeys[first:, :]
    own_out[:, HEAD_DIM:] = dvalues[first:, :]
    for need, out in zip(needs, halo_outs):
        first -= need * rows
        out[:, 0:HEAD_DIM] = dkeys[first : first + need * rows, :].astype(BF16)
        out[:, HEAD_DIM:] = dvalues[first : first + need * rows, :].astype(BF16)


def add_kv_kernel(group, needs, r_ref, own_ref, *refs):
    halo_refs, out_refs, total = refs[: len(needs)], refs[len(needs) : -1], refs[-1]
    r = r_ref[0]
    rows = own_ref.shape[0] // group
    scale = HEAD_DIM**-0.5
    for s in range(group):
        part = own_ref[s * rows : (s + 1) * rows, :]
        for need, ref in zip(needs, halo_refs):
            i = s - (group - need)
            if i >= 0:
                part = part + ref[i * rows : (i + 1) * rows, :].astype(F32)
        total[s, :, 0:HEAD_DIM] = (part[:, 0:HEAD_DIM] * scale).astype(BF16)
        total[s, :, HEAD_DIM:] = part[:, HEAD_DIM:].astype(BF16)
    for j in range(group):
        out_refs[j][...] = total[r ^ j]


def unpack_kernel(group, r_ref, *refs):
    slots, (left_ref, right_ref) = refs[:group], refs[group:]
    r = r_ref[0]
    width = left_ref.shape[1] // group
    for j in range(group):
        cols = block_at(r ^ j, width)
        left_ref[:, cols] = slots[j][:, 0:width]
        right_ref[:, cols] = slots[j][:, width:]


def per_device(queries, key_rows, value_rows, grad_out, doc_ids, loss_mask, windows):
    count = lax.axis_size(AXIS)
    rows = key_rows.shape[0]
    group = key_rows.shape[1] // HEAD_DIM
    heads = queries.shape[1] // key_rows.shape[1]
    width = heads * HEAD_DIM
    assert rows == HEAD_DIM and count % group == 0 and group & (group - 1) == 0
    hops = (WINDOW - 1 + rows - 1) // rows
    needs = [min(group, hops - k) for k in range(0, hops, group)]
    blocks = hops + group
    index = lax.axis_index(AXIS)
    r = (index % group).reshape(1)
    base = ((index // group) * (group * rows)).reshape(1)
    shape = jax.ShapeDtypeStruct

    def swap(array, by):
        return lax.ppermute(array, AXIS, [(i, i ^ by) for i in range(count)])

    def shift(array, by):
        pairs = [(i, i + by) for i in range(count) if 0 <= i + by < count]
        return lax.ppermute(array, AXIS, pairs)

    message = shape((rows + PAD, 2 * HEAD_DIM), BF16)
    kv = call(
        functools.partial(pack_kv_kernel, group),
        [message] * group,
        [r],
        [key_rows, value_rows, doc_ids.reshape(1, rows), loss_mask.reshape(1, rows)],
    )
    kv = [kv[0]] + [swap(kv[j], j) for j in range(1, group)]
    qg = call(
        functools.partial(pack_qg_kernel, group),
        [shape((rows, 2 * width), BF16)] * group,
        [r],
        [queries, grad_out],
    )
    qg = [qg[0]] + [swap(qg[j], j) for j in range(1, group)]
    *held, counted = call(
        functools.partial(gather_kernel, group, needs),
        [shape((n, rows + PAD, 2 * HEAD_DIM), BF16) for n in [group] + [n for n in needs if n < group]]
        + [shape((8, HEAD_DIM), F32)],
        [r],
        kv,
    )
    parts = iter(held[1:])
    halo = [
        shift(held[0] if need == group else next(parts), group * (k + 1))
        for k, need in enumerate(needs)
    ]
    by = group
    while by < count:
        counted = counted + swap(counted, by)
        by *= 2

    vmem = pltpu.VMEM
    results = call(
        functools.partial(attention_kernel, group, needs, heads, float(count * rows)),
        [shape((rows, 2 * width), BF16)] * group
        + [shape((group * rows, 2 * HEAD_DIM), F32)]
        + [shape((n * rows, 2 * HEAD_DIM), BF16) for n in needs],
        [r, base, windows],
        [counted, held[0], *halo, *qg],
        scratch=[
            vmem((blocks * rows, HEAD_DIM), BF16),
            vmem((blocks * rows, HEAD_DIM), BF16),
            vmem((HEAD_DIM, blocks * rows), BF16),
            vmem((HEAD_DIM, blocks * rows), BF16),
            vmem((blocks * rows, HEAD_DIM), F32),
            vmem((blocks * rows, HEAD_DIM), F32),
            vmem((group, rows, 2 * width), BF16),
            vmem((group, rows, 2 * width), BF16),
            vmem((HEAD_DIM, HEAD_DIM), F32),
        ],
        flops=12 * group * heads * rows * (hops + 1) * rows * HEAD_DIM,
        nbytes=4 << 20,
        vmem=40 << 20,
    )
    od, own, parts = results[:group], results[group], results[group + 1 :]
    back = [shift(part, -group * (k + 1)) for k, part in enumerate(parts)]
    od = [od[0]] + [swap(od[j], j) for j in range(1, group)]
    dkv = call(
        functools.partial(add_kv_kernel, group, needs),
        [shape((rows, 2 * HEAD_DIM), BF16)] * group,
        [r],
        [own, *back],
        scratch=[vmem((group, rows, 2 * HEAD_DIM), BF16)],
    )
    dkv = [dkv[0]] + [swap(dkv[j], j) for j in range(1, group)]
    attended, grad_queries = call(
        functools.partial(unpack_kernel, group), [shape((rows, group * width), BF16)] * 2, [r], od
    )
    grad_keys, grad_values = call(
        functools.partial(unpack_kernel, group),
        [shape((rows, group * HEAD_DIM), BF16)] * 2,
        [r],
        dkv,
    )
    return attended, grad_queries, grad_keys, grad_values


def solution(mesh):
    rows = P(("dp", "ctx"), "head")
    tokens = P(("dp", "ctx"))
    return jax.shard_map(
        per_device,
        mesh=mesh,
        in_specs=(rows, rows, rows, rows, tokens, tokens, P("head")),
        out_specs=(rows, rows, rows, rows),
        check_vma=False,
    )
```

time: 235 us -> 78.4 us (0.33); the launches traced: 231 us -> 78 us
  starting transfers between devices: 86.2 us -> 29.9 us
  blocking collectives: 38.7 us -> 0 us
  waiting for transfers between devices: 52.2 us -> 19 us
  matrix products: 22.5 us -> 0 us
  Pallas kernels: 0 us -> 22.4 us
  other arithmetic: 12.2 us -> 0.01 us
  local copies, waits for them, and re-layouts: 16.7 us -> 5.91 us
    ppermute x30 -> x18, starting transfers between devices: 86.2 us -> 29.9 us  [the longest x14 19.1 us: swap(): return lax.ppermute(array, AXIS, [(i, i ^ by) for i in range(count)])]
    psum x1 -> x0, blocking collectives: 38.7 us -> none  [per_device(): loss_count = lax.psum(jnp.sum(mask_float), 'ctx')]
    ppermute x30 -> x18, waiting for transfers between devices: 52.2 us -> 19 us  [the longest x4 9.56 us: shift(): return lax.ppermute(array, AXIS, pairs)]
    pallas_call x0 -> x7, Pallas kernels: none -> 22.4 us  [call(): pl.pallas_call(kernel, out_shape=out_shape, in_specs=[pl.BlockSpec(memory...]
    dot_general x20 -> x0, matrix products: 14.5 us -> none  [the longest x4 4.19 us: dense_pass(): jnp.einsum('grk,rgd->kd', weights_low, grad_grp, preferred_element_type=j...]
    sub x4 -> x0, matrix products: 7.96 us -> none  [softmax_rows(): raised = jnp.exp(scores - row_max)]
    unnamed x85 -> x36, local copies, waits for them, and re-layouts: 13.5 us -> 5.91 us
    add x11 -> x2, other arithmetic: 3.69 us -> 0.01 us  [per_device(): counted = counted + swap(counted, by)]
  transfers between devices with their start and end apart: 30 -> 18, of which waited for: 16 -> 7; matrix products, arithmetic and copies ran while one was open for 9% -> 0% of each run, Pallas kernels for 0% -> 8%
where the time goes in v1:
time: 78.4 us; the launch traced here: 78 us
  starting transfers between devices  29.9 us (38%)
  Pallas kernels  22.4 us (29%)
  waiting for transfers between devices  19 us (24%)
  local copies, waits for them, and re-layouts  5.91 us (8%)
  between operations  0.82 us (1%)
    pallas_call x7, Pallas kernels, call(): pl.pallas_call(kernel, out_shape=out_shape, in_specs=[pl.BlockSpec(memory...  22.4 us
    ppermute x14, starting transfers between devices, swap(): return lax.ppermute(array, AXIS, [(i, i ^ by) for i in range(count)])  19.1 us
    ppermute x4, starting transfers between devices, shift(): return lax.ppermute(array, AXIS, pairs)  10.8 us
    ppermute x4, waiting for transfers between devices, shift(): return lax.ppermute(array, AXIS, pairs)  9.56 us
    ppermute x14, waiting for transfers between devices, swap(): return lax.ppermute(array, AXIS, [(i, i ^ by) for i in range(count)])  9.45 us
    unnamed x36, local copies, waits for them, and re-layouts  5.91 us
  transfers between devices with their start and end apart: 18, of which 7 were waited for; matrix products, arithmetic and copies ran while one was open for 0% of the time, Pallas kernels for 8%

profile of v1, /device:TPU:0, one launch (start us, length us, event | category | flops | bytes accessed | tf_op | source)
XLA Modules:
  0.0 78.0 jit_solution(3024801255468659674)
XLA Ops:
  0.6 1.7 %shard_map.102 = (bf16[144,256]{1,0:T(8,128)(2,1)}, bf16[144,256]{1,0:T(8,128)(2,1)}, bf16[144,256]{1,0:T(8,128)(2,1)}, bf16[144,256]{1,0:T(8,128)(2,1)}) custom-call(s32[1]{0:T(128)} %bitcast.r_ref, bf16[128,512]{1,0:T(8,128)(2,1)} %key_ref.1, bf16[128,512]{1,0:T(8,128)(2,1)} %value_ref.1, s32[1,128]{1,0:T(1,128)} %bitcast.4, s32[1,128]{1,0:T(1,128)} %bitcast.5), custom_call_target="tpu_custom_call" | custom-call | tf_op jit(solution)/shard_map/pallas_call | solution.py:31
  2.4 2.9 %collective-permute-start = (bf16[144,256]{1,0:T(8,128)(2,1)}, bf16[144,256]{1,0:T(8,128)(2,1)S(1)}, u32[]{:S(2)}, u32[]{:S(2)}) collective-permute-start(bf16[144,256]{1,0:T(8,128)(2,1)} %get-tuple-element.31), channel_id=1, source_target_pairs={{0,2},{2,0},{4,6},{6,4},{8,10},{10,8},{12,14},{14,12},{16,18},{18,... | collective-permute-start | bytes 221192 | tf_op jit(solution)/shard_map/ppermute | solution.py:233
  5.3 1.5 %collective-permute-start.1 = (bf16[144,256]{1,0:T(8,128)(2,1)}, bf16[144,256]{1,0:T(8,128)(2,1)S(1)}, u32[]{:S(2)}, u32[]{:S(2)}) collective-permute-start(bf16[144,256]{1,0:T(8,128)(2,1)} %get-tuple-element.32), channel_id=1, source_target_pairs={{0,4},{2,6},{4,0},{6,2},{8,12},{10,14},{12,8},{14,10},{16,20},{18,... | collective-permute-start | bytes 221192 | tf_op jit(solution)/shard_map/ppermute | solution.py:233
  6.8 1.3 %collective-permute-done.refs_1_ = bf16[144,256]{1,0:T(8,128)(2,1)S(1)} collective-permute-done((bf16[144,256]{1,0:T(8,128)(2,1)}, bf16[144,256]{1,0:T(8,128)(2,1)S(1)}, u32[]{:S(2)}, u32[]{:S(2)}) %collective-permute-start) | collective-permute-done | bytes 73760 | tf_op jit(solution)/shard_map/ppermute | solution.py:233
  8.2 1.7 %collective-permute-done.1.refs_2_ = bf16[144,256]{1,0:T(8,128)(2,1)S(1)} collective-permute-done((bf16[144,256]{1,0:T(8,128)(2,1)}, bf16[144,256]{1,0:T(8,128)(2,1)S(1)}, u32[]{:S(2)}, u32[]{:S(2)}) %collective-permute-start.1) | collective-permute-done | bytes 73760 | tf_op jit(solution)/shard_map/ppermute | solution.py:233
  9.9 2.4 %collective-permute-done.2.refs_3_ = bf16[144,256]{1,0:T(8,128)(2,1)S(1)} collective-permute-done((bf16[144,256]{1,0:T(8,128)(2,1)}, bf16[144,256]{1,0:T(8,128)(2,1)S(1)}, u32[]{:S(2)}, u32[]{:S(2)}) %collective-permute-start.2) | collective-permute-done | bytes 73760 | tf_op jit(solution)/shard_map/ppermute | solution.py:233
  12.3 0.6 copy-done.12
  12.9 1.8 %shard_map.103 = (bf16[4,144,256]{2,1,0:T(8,128)(2,1)}, bf16[2,144,256]{2,1,0:T(8,128)(2,1)}, f32[8,128]{1,0:T(8,128)}) custom-call(s32[1]{0:T(128)} %bitcast.r_ref, bf16[144,256]{1,0:T(8,128)(2,1)} %get-tuple-element.30.refs_0_, bf16[144,256]{1,0:T(8,128)(2,1)} %copy-done.10, bf16[144,256]{1,0:T(8,128)(2,1)} %copy-done.11, bf16[144,256]{1,0:T(8,128)(2,1)} %copy-done.12), custom_call_target="tpu_custom_call" | custom-call | tf_op jit(solution)/shard_map/pallas_call | solution.py:31
  14.7 3.6 %collective-permute-start.5 = (bf16[4,144,256]{2,1,0:T(8,128)(2,1)}, bf16[4,144,256]{2,1,0:T(8,128)(2,1)S(1)}, u32[]{:S(2)}, u32[]{:S(2)}) collective-permute-start(bf16[4,144,256]{2,1,0:T(8,128)(2,1)} %get-tuple-element.35.own_ref), channel_id=1, source_target_pairs={{0,8},{2,10},{4,12},{6,14},{8,16},{10,18},{12,20},{14,22},{16,24},... | collective-permute-start | bytes 884744 | tf_op jit(solution)/shard_map/ppermute | solution.py:237
  18.3 2.2 %shard_map.104 = (bf16[128,1024]{1,0:T(8,128)(2,1)}, bf16[128,1024]{1,0:T(8,128)(2,1)}, bf16[128,1024]{1,0:T(8,128)(2,1)}, bf16[128,1024]{1,0:T(8,128)(2,1)}) custom-call(s32[1]{0:T(128)} %bitcast.r_ref, bf16[128,2048]{1,0:T(8,128)(2,1)} %query_ref.1, bf16[128,2048]{1,0:T(8,128)(2,1)} %grad_ref.1), custom_call_target="tpu_custom_call" | custom-call | tf_op jit(solution)/shard_map/pallas_call | solution.py:31
  21.7 2.4 %collective-permute-start.9 = (bf16[128,1024]{1,0:T(8,128)(2,1)}, bf16[128,1024]{1,0:T(8,128)(2,1)S(1)}, u32[]{:S(2)}, u32[]{:S(2)}) collective-permute-start(bf16[128,1024]{1,0:T(8,128)(2,1)} %get-tuple-element.40), channel_id=1, source_target_pairs={{0,6},{2,4},{4,2},{6,0},{8,14},{10,12},{12,10},{14,8},{16,22},{18,... | collective-permute-start | bytes 786440 | tf_op jit(solution)/shard_map/ppermute | solution.py:233
  24.1 1.6 %collective-permute-start.3 = (f32[8,128]{1,0:T(8,128)S(1)}, f32[8,128]{1,0:T(8,128)S(1)}, u32[]{:S(2)}, u32[]{:S(2)}) collective-permute-start(f32[8,128]{1,0:T(8,128)S(1)} %copy-done.16), channel_id=1, source_target_pairs={{0,8},{2,10},{4,12},{6,14},{8,0},{10,2},{12,4},{14,6},{16,24},{18,... | collective-permute-start | bytes 12296 | tf_op jit(solution)/shard_map/ppermute | solution.py:233
  25.6 2.0 %collective-permute-done.3 = f32[8,128]{1,0:T(8,128)S(1)} collective-permute-done((f32[8,128]{1,0:T(8,128)S(1)}, f32[8,128]{1,0:T(8,128)S(1)}, u32[]{:S(2)}, u32[]{:S(2)}) %collective-permute-start.3) | collective-permute-done | bytes 4128 | tf_op jit(solution)/shard_map/ppermute | solution.py:233
  27.7 2.6 %collective-permute-start.4 = (f32[8,128]{1,0:T(8,128)S(1)}, f32[8,128]{1,0:T(8,128)S(1)}, u32[]{:S(2)}, u32[]{:S(2)}) collective-permute-start(f32[8,128]{1,0:T(8,128)S(1)} %add.12), channel_id=1, source_target_pairs={{0,16},{2,18},{4,20},{6,22},{8,24},{10,26},{12,28},{14,30},{16,0},... | collective-permute-start | bytes 12296 | tf_op jit(solution)/shard_map/ppermute | solution.py:233
  30.3 1.9 %collective-permute-done.4 = f32[8,128]{1,0:T(8,128)S(1)} collective-permute-done((f32[8,128]{1,0:T(8,128)S(1)}, f32[8,128]{1,0:T(8,128)S(1)}, u32[]{:S(2)}, u32[]{:S(2)}) %collective-permute-start.4) | collective-permute-done | bytes 4128 | tf_op jit(solution)/shard_map/ppermute | solution.py:233
  32.2 4.6 %collective-permute-start.6 = (bf16[2,144,256]{2,1,0:T(8,128)(2,1)S(1)}, bf16[2,144,256]{2,1,0:T(8,128)(2,1)S(1)}, u32[]{:S(2)}, u32[]{:S(2)}) collective-permute-start(bf16[2,144,256]{2,1,0:T(8,128)(2,1)S(1)} %copy-done.17), channel_id=1, source_target_pairs={{0,16},{2,18},{4,20},{6,22},{8,24},{10,26},{12,28},{14,30},{1,17},... | collective-permute-start | bytes 442376 | tf_op jit(solution)/shard_map/ppermute | solution.py:237
  36.8 2.6 %collective-permute-done.6.refs_1_ = bf16[2,144,256]{2,1,0:T(8,128)(2,1)S(1)} collective-permute-done((bf16[2,144,256]{2,1,0:T(8,128)(2,1)S(1)}, bf16[2,144,256]{2,1,0:T(8,128)(2,1)S(1)}, u32[]{:S(2)}, u32[]{:S(2)}) %collective-permute-start.6) | collective-permute-done | bytes 147488 | tf_op jit(solution)/shard_map/ppermute | solution.py:237
  39.5 0.6 copy-done.4
  40.1 0.9 %copy-done.3 = bf16[128,1024]{1,0:T(8,128)(2,1)S(1)} copy-done((bf16[128,1024]{1,0:T(8,128)(2,1)S(1)}, bf16[128,1024]{1,0:T(8,128)(2,1)}, u32[]{:S(2)}) %copy-start.3) | copy-done | bytes 262168
  41.1 10.8 %shard_map.105 = (bf16[128,1024]{1,0:T(8,128)(2,1)S(1)}, bf16[128,1024]{1,0:T(8,128)(2,1)S(1)}, bf16[128,1024]{1,0:T(8,128)(2,1)S(1)}, bf16[128,1024]{1,0:T(8,12...) custom-call(s32[1]{0:T(128)} %bitcast.r_ref, s32[1]{0:T(128)} %bitcast.1.base_ref, ...), custom_call_target="tpu_custom_call" | custom-call | flops 2818572288 | bytes 4194304 | tf_op jit(solution)/shard_map/pallas_call | solution.py:31
  51.9 0.8 %copy-done = f32[512,256]{1,0:T(8,128)} copy-done((f32[512,256]{1,0:T(8,128)}, f32[512,256]{1,0:T(8,128)S(1)}, u32[]{:S(2)}) %copy-start) | copy-done | bytes 524312
  52.7 0.7 copy-done.1
  53.3 1.3 %collective-permute-start.13 = (bf16[512,256]{1,0:T(8,128)(2,1)S(1)}, bf16[512,256]{1,0:T(8,128)(2,1)S(1)}, u32[]{:S(2)}, u32[]{:S(2)}) collective-permute-start(bf16[512,256]{1,0:T(8,128)(2,1)S(1)} %get-tuple-element.48), channel_id=1, source_target_pairs={{8,0},{10,2},{12,4},{14,6},{16,8},{18,10},{20,12},{22,14},{24,16},... | collective-permute-start | bytes 786440 | tf_op jit(solution)/shard_map/ppermute | solution.py:237
  55.8 2.4 %collective-permute-start.12 = (bf16[128,1024]{1,0:T(8,128)(2,1)S(1)}, bf16[128,1024]{1,0:T(8,128)(2,1)S(1)}, u32[]{:S(2)}, u32[]{:S(2)}) collective-permute-start(bf16[128,1024]{1,0:T(8,128)(2,1)S(1)} %get-tuple-element.44), channel_id=1, source_target_pairs={{0,6},{2,4},{4,2},{6,0},{8,14},{10,12},{12,10},{14,8},{16,22},{18,... | collective-permute-start | bytes 786440 | tf_op jit(solution)/shard_map/ppermute | solution.py:233
  58.2 1.3 %collective-permute-start.14 = (bf16[256,256]{1,0:T(8,128)(2,1)S(1)}, bf16[256,256]{1,0:T(8,128)(2,1)S(1)}, u32[]{:S(2)}, u32[]{:S(2)}) collective-permute-start(bf16[256,256]{1,0:T(8,128)(2,1)S(1)} %get-tuple-element.49), channel_id=1, source_target_pairs={{16,0},{18,2},{20,4},{22,6},{24,8},{26,10},{28,12},{30,14},{17,1},... | collective-permute-start | bytes 393224 | tf_op jit(solution)/shard_map/ppermute | solution.py:237
  59.5 6.9 %collective-permute-done.14.refs_1_ = bf16[256,256]{1,0:T(8,128)(2,1)S(1)} collective-permute-done((bf16[256,256]{1,0:T(8,128)(2,1)S(1)}, bf16[256,256]{1,0:T(8,128)(2,1)S(1)}, u32[]{:S(2)}, u32[]{:S(2)}) %collective-permute-start.14) | collective-permute-done | bytes 131104 | tf_op jit(solution)/shard_map/ppermute | solution.py:237
  66.4 0.6 copy-done.9
  67.2 1.9 %shard_map.107 = (bf16[128,256]{1,0:T(8,128)(2,1)}, bf16[128,256]{1,0:T(8,128)(2,1)}, bf16[128,256]{1,0:T(8,128)(2,1)}, bf16[128,256]{1,0:T(8,128)(2,1)}) custom-call(s32[1]{0:T(128)} %bitcast.r_ref, f32[512,256]{1,0:T(8,128)} %copy-done, bf16[512,256]{1,0:T(8,128)(2,1)} %copy-done.5, bf16[256,256]{1,0:T(8,128)(2,1)} %copy-done.9), custom_call_target="tpu_custom_call" | custom-call | tf_op jit(solution)/shard_map/pallas_call | solution.py:31
  70.2 2.4 %collective-permute-start.17 = (bf16[128,256]{1,0:T(8,128)(2,1)}, bf16[128,256]{1,0:T(8,128)(2,1)S(1)}, u32[]{:S(2)}, u32[]{:S(2)}) collective-permute-start(bf16[128,256]{1,0:T(8,128)(2,1)} %get-tuple-element.53), channel_id=1, source_target_pairs={{0,6},{2,4},{4,2},{6,0},{8,14},{10,12},{12,10},{14,8},{16,22},{18,... | collective-permute-start | bytes 196616 | tf_op jit(solution)/shard_map/ppermute | solution.py:233
  72.6 0.7 copy-done.7
  73.4 2.2 %shard_map.106 = (bf16[128,2048]{1,0:T(8,128)(2,1)}, bf16[128,2048]{1,0:T(8,128)(2,1)}) custom-call(s32[1]{0:T(128)} %bitcast.r_ref, bf16[128,1024]{1,0:T(8,128)(2,1)} %copy-done.1, bf16[128,1024]{1,0:T(8,128)(2,1)} %copy-done.6, bf16[128,1024]{1,0:T(8,128)(2,1)} %copy-done.7, bf16[128,1024]{1,0:T(8,128)(2,1)} %copy-done.8), custom_call_target="tpu_custom_call" | custom-call | tf_op jit(solution)/shard_map/pallas_call | solution.py:31
  76.3 1.7 %shard_map.108 = (bf16[128,512]{1,0:T(8,128)(2,1)}, bf16[128,512]{1,0:T(8,128)(2,1)}) custom-call(s32[1]{0:T(128)} %bitcast.r_ref, bf16[128,256]{1,0:T(8,128)(2,1)} %get-tuple-element.50.refs_0_, bf16[128,256]{1,0:T(8,128)(2,1)} %copy-done.13, bf16[128,256]{1,0:T(8,128)(2,1)} %copy-done.14, bf16[128,256]{1,0:T(8,128)(2,1)} %copy-done.15), custom_call_target="tpu_custom_call" | custom-call | tf_op jit(solution)/shard_map/pallas_call | solution.py:31
  (49 shorter events, 4.2 us)
Async XLA Ops:
  2.4 5.8 %collective-permute-start = (bf16[144,256]{1,0:T(8,128)(2,1)}, bf16[144,256]{1,0:T(8,128)(2,1)S(1)}, u32[]{:S(2)}, u32[]{:S(2)}) collective-permute-start(bf16[144,256]{1,0:T(8,128)(2,1)} %get-tuple-element.31), channel_id=1, source_target_pairs={{0,2},{2,0},{4,6},{6,4},{8,10},{10,8},{12,14},{14,12},{16,18},{18,... | collective-permute-start | bytes 221192 | tf_op jit(solution)/shard_map/ppermute | solution.py:233
  5.3 4.6 %collective-permute-start.1 = (bf16[144,256]{1,0:T(8,128)(2,1)}, bf16[144,256]{1,0:T(8,128)(2,1)S(1)}, u32[]{:S(2)}, u32[]{:S(2)}) collective-permute-start(bf16[144,256]{1,0:T(8,128)(2,1)} %get-tuple-element.32), channel_id=1, source_target_pairs={{0,4},{2,6},{4,0},{6,2},{8,12},{10,14},{12,8},{14,10},{16,20},{18,... | collective-permute-start | bytes 221192 | tf_op jit(solution)/shard_map/ppermute | solution.py:233
  6.8 5.5 %collective-permute-start.2 = (bf16[144,256]{1,0:T(8,128)(2,1)}, bf16[144,256]{1,0:T(8,128)(2,1)S(1)}, u32[]{:S(2)}, u32[]{:S(2)}) collective-permute-start(bf16[144,256]{1,0:T(8,128)(2,1)} %get-tuple-element.33), channel_id=1, source_target_pairs={{0,6},{2,4},{4,2},{6,0},{8,14},{10,12},{12,10},{14,8},{16,22},{18,... | collective-permute-start | bytes 221192 | tf_op jit(solution)/shard_map/ppermute | solution.py:233
  8.2 4.1 %copy-start.10 = (bf16[144,256]{1,0:T(8,128)(2,1)}, bf16[144,256]{1,0:T(8,128)(2,1)S(1)}, u32[]{:S(2)}) copy-start(bf16[144,256]{1,0:T(8,128)(2,1)S(1)} %collective-permute-done.refs_1_) | copy-start | bytes 221188
  9.9 2.4 %copy-start.11 = (bf16[144,256]{1,0:T(8,128)(2,1)}, bf16[144,256]{1,0:T(8,128)(2,1)S(1)}, u32[]{:S(2)}) copy-start(bf16[144,256]{1,0:T(8,128)(2,1)S(1)} %collective-permute-done.1.refs_2_) | copy-start | bytes 221188
  14.7 17.5 %copy-start.17 = (bf16[2,144,256]{2,1,0:T(8,128)(2,1)S(1)}, bf16[2,144,256]{2,1,0:T(8,128)(2,1)}, u32[]{:S(2)}) copy-start(bf16[2,144,256]{2,1,0:T(8,128)(2,1)} %get-tuple-element.36) | copy-start | bytes 442372
  14.7 24.8 %copy-start.2 = (bf16[4,144,256]{2,1,0:T(8,128)(2,1)S(1)}, bf16[4,144,256]{2,1,0:T(8,128)(2,1)}, u32[]{:S(2)}) copy-start(bf16[4,144,256]{2,1,0:T(8,128)(2,1)} %get-tuple-element.35.own_ref) | copy-start | bytes 884740
  14.7 24.7 %collective-permute-start.5 = (bf16[4,144,256]{2,1,0:T(8,128)(2,1)}, bf16[4,144,256]{2,1,0:T(8,128)(2,1)S(1)}, u32[]{:S(2)}, u32[]{:S(2)}) collective-permute-start(bf16[4,144,256]{2,1,0:T(8,128)(2,1)} %get-tuple-element.35.own_ref), channel_id=1, source_target_pairs={{0,8},{2,10},{4,12},{6,14},{8,16},{10,18},{12,20},{14,22},{16,24},... | collective-permute-start | bytes 884744 | tf_op jit(solution)/shard_map/ppermute | solution.py:237
  20.6 3.5 %copy-start.16 = (f32[8,128]{1,0:T(8,128)S(1)}, f32[8,128]{1,0:T(8,128)}, u32[]{:S(2)}) copy-start(f32[8,128]{1,0:T(8,128)} %get-tuple-element.34) | copy-start | bytes 12292
  20.6 18.9 %collective-permute-start.7 = (bf16[128,1024]{1,0:T(8,128)(2,1)}, bf16[128,1024]{1,0:T(8,128)(2,1)S(1)}, u32[]{:S(2)}, u32[]{:S(2)}) collective-permute-start(bf16[128,1024]{1,0:T(8,128)(2,1)} %get-tuple-element.38), channel_id=1, source_target_pairs={{0,2},{2,0},{4,6},{6,4},{8,10},{10,8},{12,14},{14,12},{16,18},{18,... | collective-permute-start | bytes 786440 | tf_op jit(solution)/shard_map/ppermute | solution.py:233
  21.1 18.3 %collective-permute-start.8 = (bf16[128,1024]{1,0:T(8,128)(2,1)}, bf16[128,1024]{1,0:T(8,128)(2,1)S(1)}, u32[]{:S(2)}, u32[]{:S(2)}) collective-permute-start(bf16[128,1024]{1,0:T(8,128)(2,1)} %get-tuple-element.39), channel_id=1, source_target_pairs={{0,4},{2,6},{4,0},{6,2},{8,12},{10,14},{12,8},{14,10},{16,20},{18,... | collective-permute-start | bytes 786440 | tf_op jit(solution)/shard_map/ppermute | solution.py:233
  21.7 17.8 %collective-permute-start.9 = (bf16[128,1024]{1,0:T(8,128)(2,1)}, bf16[128,1024]{1,0:T(8,128)(2,1)S(1)}, u32[]{:S(2)}, u32[]{:S(2)}) collective-permute-start(bf16[128,1024]{1,0:T(8,128)(2,1)} %get-tuple-element.40), channel_id=1, source_target_pairs={{0,6},{2,4},{4,2},{6,0},{8,14},{10,12},{12,10},{14,8},{16,22},{18,... | collective-permute-start | bytes 786440 | tf_op jit(solution)/shard_map/ppermute | solution.py:233
  24.1 3.6 %collective-permute-start.3 = (f32[8,128]{1,0:T(8,128)S(1)}, f32[8,128]{1,0:T(8,128)S(1)}, u32[]{:S(2)}, u32[]{:S(2)}) collective-permute-start(f32[8,128]{1,0:T(8,128)S(1)} %copy-done.16), channel_id=1, source_target_pairs={{0,8},{2,10},{4,12},{6,14},{8,0},{10,2},{12,4},{14,6},{16,24},{18,... | collective-permute-start | bytes 12296 | tf_op jit(solution)/shard_map/ppermute | solution.py:233
  27.7 4.5 %collective-permute-start.4 = (f32[8,128]{1,0:T(8,128)S(1)}, f32[8,128]{1,0:T(8,128)S(1)}, u32[]{:S(2)}, u32[]{:S(2)}) collective-permute-start(f32[8,128]{1,0:T(8,128)S(1)} %add.12), channel_id=1, source_target_pairs={{0,16},{2,18},{4,20},{6,22},{8,24},{10,26},{12,28},{14,30},{16,0},... | collective-permute-start | bytes 12296 | tf_op jit(solution)/shard_map/ppermute | solution.py:233
  32.2 7.2 %collective-permute-start.6 = (bf16[2,144,256]{2,1,0:T(8,128)(2,1)S(1)}, bf16[2,144,256]{2,1,0:T(8,128)(2,1)S(1)}, u32[]{:S(2)}, u32[]{:S(2)}) collective-permute-start(bf16[2,144,256]{2,1,0:T(8,128)(2,1)S(1)} %copy-done.17), channel_id=1, source_target_pairs={{0,16},{2,18},{4,20},{6,22},{8,24},{10,26},{12,28},{14,30},{1,17},... | collective-permute-start | bytes 442376 | tf_op jit(solution)/shard_map/ppermute | solution.py:237
  39.5 0.7 copy-start.4
  40.1 0.9 %copy-start.3 = (bf16[128,1024]{1,0:T(8,128)(2,1)S(1)}, bf16[128,1024]{1,0:T(8,128)(2,1)}, u32[]{:S(2)}) copy-start(bf16[128,1024]{1,0:T(8,128)(2,1)} %get-tuple-element.37.refs_2_) | copy-start | bytes 786436
  51.9 0.8 %copy-start = (f32[512,256]{1,0:T(8,128)}, f32[512,256]{1,0:T(8,128)S(1)}, u32[]{:S(2)}) copy-start(f32[512,256]{1,0:T(8,128)S(1)} %get-tuple-element.47.own_ref) | copy-start | bytes 1572868
  52.7 0.7 copy-start.1
  53.3 13.1 %collective-permute-start.13 = (bf16[512,256]{1,0:T(8,128)(2,1)S(1)}, bf16[512,256]{1,0:T(8,128)(2,1)S(1)}, u32[]{:S(2)}, u32[]{:S(2)}) collective-permute-start(bf16[512,256]{1,0:T(8,128)(2,1)S(1)} %get-tuple-element.48), channel_id=1, source_target_pairs={{8,0},{10,2},{12,4},{14,6},{16,8},{18,10},{20,12},{22,14},{24,16},... | collective-permute-start | bytes 786440 | tf_op jit(solution)/shard_map/ppermute | solution.py:237
  54.6 15.5 %collective-permute-start.10 = (bf16[128,1024]{1,0:T(8,128)(2,1)S(1)}, bf16[128,1024]{1,0:T(8,128)(2,1)S(1)}, u32[]{:S(2)}, u32[]{:S(2)}) collective-permute-start(bf16[128,1024]{1,0:T(8,128)(2,1)S(1)} %get-tuple-element.42), channel_id=1, source_target_pairs={{0,2},{2,0},{4,6},{6,4},{8,10},{10,8},{12,14},{14,12},{16,18},{18,... | collective-permute-start | bytes 786440 | tf_op jit(solution)/shard_map/ppermute | solution.py:233
  55.2 17.3 %collective-permute-start.11 = (bf16[128,1024]{1,0:T(8,128)(2,1)S(1)}, bf16[128,1024]{1,0:T(8,128)(2,1)S(1)}, u32[]{:S(2)}, u32[]{:S(2)}) collective-permute-start(bf16[128,1024]{1,0:T(8,128)(2,1)S(1)} %get-tuple-element.43), channel_id=1, source_target_pairs={{0,4},{2,6},{4,0},{6,2},{8,12},{10,14},{12,8},{14,10},{16,20},{18,... | collective-permute-start | bytes 786440 | tf_op jit(solution)/shard_map/ppermute | solution.py:233
  55.8 16.8 %collective-permute-start.12 = (bf16[128,1024]{1,0:T(8,128)(2,1)S(1)}, bf16[128,1024]{1,0:T(8,128)(2,1)S(1)}, u32[]{:S(2)}, u32[]{:S(2)}) collective-permute-start(bf16[128,1024]{1,0:T(8,128)(2,1)S(1)} %get-tuple-element.44), channel_id=1, source_target_pairs={{0,6},{2,4},{4,2},{6,0},{8,14},{10,12},{12,10},{14,8},{16,22},{18,... | collective-permute-start | bytes 786440 | tf_op jit(solution)/shard_map/ppermute | solution.py:233
  58.2 8.2 %collective-permute-start.14 = (bf16[256,256]{1,0:T(8,128)(2,1)S(1)}, bf16[256,256]{1,0:T(8,128)(2,1)S(1)}, u32[]{:S(2)}, u32[]{:S(2)}) collective-permute-start(bf16[256,256]{1,0:T(8,128)(2,1)S(1)} %get-tuple-element.49), channel_id=1, source_target_pairs={{16,0},{18,2},{20,4},{22,6},{24,8},{26,10},{28,12},{30,14},{17,1},... | collective-permute-start | bytes 393224 | tf_op jit(solution)/shard_map/ppermute | solution.py:237
  66.4 0.7 copy-start.9
  66.4 0.7 copy-start.5
  69.1 6.6 %collective-permute-start.15 = (bf16[128,256]{1,0:T(8,128)(2,1)}, bf16[128,256]{1,0:T(8,128)(2,1)S(1)}, u32[]{:S(2)}, u32[]{:S(2)}) collective-permute-start(bf16[128,256]{1,0:T(8,128)(2,1)} %get-tuple-element.51), channel_id=1, source_target_pairs={{0,2},{2,0},{4,6},{6,4},{8,10},{10,8},{12,14},{14,12},{16,18},{18,... | collective-permute-start | bytes 196616 | tf_op jit(solution)/shard_map/ppermute | solution.py:233
  69.6 6.0 %collective-permute-start.16 = (bf16[128,256]{1,0:T(8,128)(2,1)}, bf16[128,256]{1,0:T(8,128)(2,1)S(1)}, u32[]{:S(2)}, u32[]{:S(2)}) collective-permute-start(bf16[128,256]{1,0:T(8,128)(2,1)} %get-tuple-element.52), channel_id=1, source_target_pairs={{0,4},{2,6},{4,0},{6,2},{8,12},{10,14},{12,8},{14,10},{16,20},{18,... | collective-permute-start | bytes 196616 | tf_op jit(solution)/shard_map/ppermute | solution.py:233
  70.2 2.4 %copy-start.6 = (bf16[128,1024]{1,0:T(8,128)(2,1)}, bf16[128,1024]{1,0:T(8,128)(2,1)S(1)}, u32[]{:S(2)}) copy-start(bf16[128,1024]{1,0:T(8,128)(2,1)S(1)} %collective-permute-done.10.refs_1_) | copy-start | bytes 786436
  70.2 5.5 %collective-permute-start.17 = (bf16[128,256]{1,0:T(8,128)(2,1)}, bf16[128,256]{1,0:T(8,128)(2,1)S(1)}, u32[]{:S(2)}, u32[]{:S(2)}) collective-permute-start(bf16[128,256]{1,0:T(8,128)(2,1)} %get-tuple-element.53), channel_id=1, source_target_pairs={{0,6},{2,4},{4,2},{6,0},{8,14},{10,12},{12,10},{14,8},{16,22},{18,... | collective-permute-start | bytes 196616 | tf_op jit(solution)/shard_map/ppermute | solution.py:233
  72.6 0.7 copy-start.7
  72.6 0.8 %copy-start.8 = (bf16[128,1024]{1,0:T(8,128)(2,1)}, bf16[128,1024]{1,0:T(8,128)(2,1)S(1)}, u32[]{:S(2)}) copy-start(bf16[128,1024]{1,0:T(8,128)(2,1)S(1)} %collective-permute-done.12.refs_3_) | copy-start | bytes 786436
  (4 other events, 2.5 us)

commit v2 on v1

--- a/solution.py
+++ b/solution.py
@@ -27,38 +27,72 @@
     return pl.ds(pl.multiple_of(index * size, size), size)
 
 
-def call(kernel, out_shape, scalars, vectors, scratch=(), flops=0, nbytes=0, vmem=None):
+def call(
+    kernel, out_shape, scalars, vectors, scratch=(), flops=0, nbytes=0, vmem=None, space=pltpu.VMEM
+):
+    def keep(array):
+        return pltpu.with_memory_space_constraint(array, space) if space == pltpu.HBM else array
+
     return pl.pallas_call(
         kernel,
         out_shape=out_shape,
         in_specs=[pl.BlockSpec(memory_space=pltpu.SMEM)] * len(scalars)
-        + [pl.BlockSpec(memory_space=pltpu.VMEM)] * len(vectors),
+        + [pl.BlockSpec(memory_space=space)] * len(vectors),
         out_specs=jax.tree.map(lambda _: pl.BlockSpec(memory_space=pltpu.VMEM), out_shape),
         scratch_shapes=list(scratch),
         cost_estimate=pl.CostEstimate(flops=flops, bytes_accessed=nbytes, transcendentals=0),
         compiler_params=pltpu.CompilerParams(vmem_limit_bytes=vmem),
-    )(*scalars, *vectors)
-
-
-def pack_kv_kernel(group, r_ref, key_ref, value_ref, doc_ref, mask_ref, *out_refs):
+    )(*scalars, *[keep(v) for v in vectors])
+
+
+def pack_kv_kernel(group, r_ref, key_ref, value_ref, doc_ref, mask_ref, *refs):
+    out_refs, (line_ref, sems) = refs[:group], refs[group:]
     r = r_ref[0]
     rows = key_ref.shape[0]
-    line = jnp.concatenate([doc_ref[...].astype(F32), mask_ref[...].astype(F32)], axis=1)
-    tail = jnp.broadcast_to(line, (PAD, 2 * HEAD_DIM)).astype(BF16)
+    copies = [
+        pltpu.make_async_copy(doc_ref, line_ref.at[:, 0:HEAD_DIM], sems.at[0]),
+        pltpu.make_async_copy(mask_ref, line_ref.at[:, HEAD_DIM:], sems.at[1]),
+    ]
     for j in range(group):
         cols = block_at(r ^ j, HEAD_DIM)
-        out_refs[j][0:rows, 0:HEAD_DIM] = key_ref[:, cols]
-        out_refs[j][0:rows, HEAD_DIM:] = value_ref[:, cols]
+        for i, ref in enumerate((key_ref, value_ref)):
+            into = out_refs[j].at[0:rows, i * HEAD_DIM : (i + 1) * HEAD_DIM]
+            copies.append(pltpu.make_async_copy(ref.at[:, cols], into, sems.at[2 + 2 * j + i]))
+    for copy in copies:
+        copy.start()
+    for copy in copies[:2]:
+        copy.wait()
+    tail = jnp.broadcast_to(line_ref[...].astype(F32), (PAD, 2 * HEAD_DIM)).astype(BF16)
+    for j in range(group):
         out_refs[j][rows:, :] = tail
-
-
-def pack_qg_kernel(group, r_ref, query_ref, grad_ref, *out_refs):
+    for copy in copies[2:]:
+        copy.wait()
+
+
+def pack_qg_kernel(group, r_ref, query_ref, grad_ref, *refs):
+    out_refs, sems = refs[:group], refs[group]
     r = r_ref[0]
     width = query_ref.shape[1] // group
+    copies = []
     for j in range(group):
         cols = block_at(r ^ j, width)
-        out_refs[j][:, 0:width] = query_ref[:, cols]
-        out_refs[j][:, width:] = grad_ref[:, cols]
+        for i, ref in enumerate((query_ref, grad_ref)):
+            into = out_refs[j].at[:, i * width : (i + 1) * width]
+            copies.append(pltpu.make_async_copy(ref.at[:, cols], into, sems.at[2 * j + i]))
+    for copy in copies:
+        copy.start()
+    for copy in copies:
+        copy.wait()
+
+
+def encode_count(total):
+    high = jnp.floor(total * (1.0 / 64.0))
+    return jnp.concatenate([high, total - 64.0 * high], axis=1).astype(BF16)
+
+
+def decode_count(line):
+    line = line.astype(F32)
+    return 64.0 * line[:, 0:HEAD_DIM] + line[:, HEAD_DIM:]
 
 
 def gather_kernel(group, needs, r_ref, *refs):
@@ -70,13 +104,23 @@
     for j in range(group):
         full[r ^ j] = slots[j][...]
         total = total + slots[j][rows : rows + 1, HEAD_DIM:].astype(F32)
-    count_ref[...] = jnp.broadcast_to(jnp.sum(total, axis=1, keepdims=True), count_ref.shape)
+    total = jnp.broadcast_to(jnp.sum(total, axis=1, keepdims=True), count_ref.shape)
+    count_ref[...] = total
+    full[0, rows + 8 :, :] = encode_count(total)
     for need, out in zip([n for n in needs if n < group], outs[1:-1]):
         out[...] = full[group - need :]
+        out[0, rows + 8 :, :] = encode_count(total)
+
+
+def ordered_pieces(needs, group, own_ref, halo_refs):
+    pieces = []
+    for need, ref in reversed(list(zip(needs, halo_refs))):
+        pieces += [(ref, i) for i in range(need)]
+    return pieces + [(own_ref, i) for i in range(group)]
 
 
 def attention_kernel(
-    group, needs, heads, token_count, r_ref, base_ref, window_ref, count_ref, own_ref, *refs
+    group, needs, heads, token_count, counts_ride, where_ref, count_ref, other_ref, own_ref, *refs
 ):
     halo_refs, refs = refs[: len(needs)], refs[len(needs) :]
     qg_refs, refs = refs[:group], refs[group:]
@@ -84,7 +128,7 @@
     own_out, refs = refs[0], refs[1:]
     halo_outs, refs = refs[: len(needs)], refs[len(needs) :]
     keys, values, keys_t, values_t, dkeys, dvalues, qg, od, lines = refs
-    r = r_ref[0]
+    r = where_ref[0]
     rows = own_ref.shape[1] - PAD
     hops = sum(needs)
     blocks = hops + group
@@ -92,14 +136,15 @@
     width = heads * HEAD_DIM
     scale = HEAD_DIM**-0.5
     exp_scale = scale * 1.4426950408889634
-    lowest = jnp.maximum(hops * rows - base_ref[0], 0)
-
-    pieces = []
-    for need, ref in reversed(list(zip(needs, halo_refs))):
-        pieces += [(ref, i) for i in range(need)]
-    pieces += [(own_ref, i) for i in range(group)]
+    lowest = jnp.maximum(hops * rows - where_ref[1], 0)
+
+    pieces = ordered_pieces(needs, group, own_ref, halo_refs)
     lines[...] = jnp.zeros_like(lines)
-    factor = token_count / jnp.maximum(count_ref[0:1, :], 1.0)
+    total = count_ref[...] + other_ref[...]
+    if counts_ride:
+        for ref in halo_refs:
+            total = total + decode_count(ref[0, rows + 8 :, :])
+    factor = token_count / jnp.maximum(total[0:1, :], 1.0)
     for kb, (ref, i) in enumerate(pieces):
         at = slice(kb * rows, (kb + 1) * rows)
         key, value = ref[i, 0:rows, 0:HEAD_DIM], ref[i, 0:rows, HEAD_DIM:]
@@ -138,7 +183,7 @@
             hs = range(h0, h0 + PAIR)
             low = jnp.concatenate(
                 [
-                    jnp.maximum(start, hops * rows + 1 + lane - window_ref[r * heads + h])
+                    jnp.maximum(start, hops * rows + 1 + lane - where_ref[2 + h])
                     for h in hs
                 ],
                 axis=1,
@@ -224,16 +269,20 @@
     hops = (WINDOW - 1 + rows - 1) // rows
     needs = [min(group, hops - k) for k in range(0, hops, group)]
     blocks = hops + group
+    span = (hops + 1) * rows
     index = lax.axis_index(AXIS)
     r = (index % group).reshape(1)
     base = ((index // group) * (group * rows)).reshape(1)
+    where = jnp.concatenate([r, base, lax.dynamic_slice(windows, (r[0] * heads,), (heads,))])
     shape = jax.ShapeDtypeStruct
+    vmem = pltpu.VMEM
+    counts_ride = count == 4 * group and len(needs) == 2
 
     def swap(array, by):
         return lax.ppermute(array, AXIS, [(i, i ^ by) for i in range(count)])
 
-    def shift(array, by):
-        pairs = [(i, i + by) for i in range(count) if 0 <= i + by < count]
+    def shift(array, by, around):
+        pairs = [(i, (i + by) % count) for i in range(count) if around or 0 <= i + by < count]
         return lax.ppermute(array, AXIS, pairs)
 
     message = shape((rows + PAD, 2 * HEAD_DIM), BF16)
@@ -242,6 +291,12 @@
         [message] * group,
         [r],
         [key_rows, value_rows, doc_ids.reshape(1, rows), loss_mask.reshape(1, rows)],
+        scratch=[
+            vmem((1, 2 * HEAD_DIM), jnp.int32),
+            pltpu.SemaphoreType.DMA((2 + 2 * group,)),
+        ],
+        vmem=4 << 20,
+        space=pltpu.HBM,
     )
     kv = [kv[0]] + [swap(kv[j], j) for j in range(1, group)]
     qg = call(
@@ -249,7 +304,11 @@
         [shape((rows, 2 * width), BF16)] * group,
         [r],
         [queries, grad_out],
-    )
+        scratch=[pltpu.SemaphoreType.DMA((2 * group,))],
+        vmem=4 << 20,
+        space=pltpu.HBM,
+    )
+    kv, where, _ = lax.optimization_barrier((kv, where, qg[0]))
     qg = [qg[0]] + [swap(qg[j], j) for j in range(1, group)]
     *held, counted = call(
         functools.partial(gather_kernel, group, needs),
@@ -257,25 +316,28 @@
         + [shape((8, HEAD_DIM), F32)],
         [r],
         kv,
+        vmem=4 << 20,
     )
     parts = iter(held[1:])
     halo = [
-        shift(held[0] if need == group else next(parts), group * (k + 1))
+        shift(held[0] if need == group else next(parts), group * (k + 1), counts_ride)
         for k, need in enumerate(needs)
     ]
-    by = group
-    while by < count:
-        counted = counted + swap(counted, by)
-        by *= 2
-
-    vmem = pltpu.VMEM
+    if counts_ride:
+        others = shift(counted, -group, True)
+    else:
+        summed, by = counted, group
+        while by < count:
+            summed = summed + swap(summed, by)
+            by *= 2
+        others = summed - counted
     results = call(
-        functools.partial(attention_kernel, group, needs, heads, float(count * rows)),
+        functools.partial(attention_kernel, group, needs, heads, float(count * rows), counts_ride),
         [shape((rows, 2 * width), BF16)] * group
         + [shape((group * rows, 2 * HEAD_DIM), F32)]
         + [shape((n * rows, 2 * HEAD_DIM), BF16) for n in needs],
-        [r, base, windows],
-        [counted, held[0], *halo, *qg],
+        [where],
+        [counted, others, held[0], *halo, *qg],
         scratch=[
             vmem((blocks * rows, HEAD_DIM), BF16),
             vmem((blocks * rows, HEAD_DIM), BF16),
@@ -287,12 +349,12 @@
             vmem((group, rows, 2 * width), BF16),
             vmem((HEAD_DIM, HEAD_DIM), F32),
         ],
-        flops=12 * group * heads * rows * (hops + 1) * rows * HEAD_DIM,
+        flops=12 * group * heads * rows * span * HEAD_DIM,
         nbytes=4 << 20,
-        vmem=40 << 20,
-    )
-    od, own, parts = results[:group], results[group], results[group + 1 :]
-    back = [shift(part, -group * (k + 1)) for k, part in enumerate(parts)]
+        vmem=24 << 20,
+    )
+    od, (own, *parts) = results[:group], results[group:]
+    back = [shift(part, -group * (k + 1), False) for k, part in enumerate(parts)]
     od = [od[0]] + [swap(od[j], j) for j in range(1, group)]
     dkv = call(
         functools.partial(add_kv_kernel, group, needs),
@@ -300,16 +362,22 @@
         [r],
         [own, *back],
         scratch=[vmem((group, rows, 2 * HEAD_DIM), BF16)],
+        vmem=4 << 20,
     )
     dkv = [dkv[0]] + [swap(dkv[j], j) for j in range(1, group)]
     attended, grad_queries = call(
-        functools.partial(unpack_kernel, group), [shape((rows, group * width), BF16)] * 2, [r], od
+        functools.partial(unpack_kernel, group),
+        [shape((rows, group * width), BF16)] * 2,
+        [r],
+        od,
+        vmem=4 << 20,
     )
     grad_keys, grad_values = call(
         functools.partial(unpack_kernel, group),
         [shape((rows, group * HEAD_DIM), BF16)] * 2,
         [r],
         dkv,
+        vmem=4 << 20,
     )
     return attended, grad_queries, grad_keys, grad_values
 

time: 78.4 us -> 59.1 us (0.75)
  Pallas kernels: 22.4 us -> 15.2 us
  starting transfers between devices: 29.9 us -> 23.8 us
  local copies, waits for them, and re-layouts: 5.91 us -> 0.73 us
    pallas_call x7, Pallas kernels: 22.4 us -> 15.2 us  [call(): pl.pallas_call(kernel, out_shape=out_shape, in_specs=[pl.BlockSpec(memory...]
    unnamed x36 -> x2, local copies, waits for them, and re-layouts: 5.91 us -> 0.65 us
    ppermute x14 -> x12, waiting for transfers between devices: 9.45 us -> 4.76 us  [swap(): return lax.ppermute(array, AXIS, [(i, i ^ by) for i in range(count)])]
    ppermute x14 -> x12, starting transfers between devices: 19.1 us -> 15.1 us  [swap(): return lax.ppermute(array, AXIS, [(i, i ^ by) for i in range(count)])]
    ppermute x4 -> x5, waiting for transfers between devices: 9.56 us -> 13.5 us  [shift(): return lax.ppermute(array, AXIS, pairs)]
    ppermute x4 -> x5, starting transfers between devices: 10.8 us -> 8.66 us  [shift(): return lax.ppermute(array, AXIS, pairs)]
  transfers between devices with their start and end apart: 18 -> 17, of which waited for: 7 -> 7; matrix products, arithmetic and copies ran while one was open for 0% -> 0% of each run, Pallas kernels for 8% -> 4%
where the time goes in v2:
time: 59.1 us; the launch traced here: 58.8 us
  starting transfers between devices  23.8 us (40%)
  waiting for transfers between devices  18.3 us (31%)
  Pallas kernels  15.2 us (26%)
  local copies, waits for them, and re-layouts  0.73 us (1%)
  between operations  0.72 us (1%)
    pallas_call x7, Pallas kernels, call(): pl.pallas_call(kernel, out_shape=out_shape, in_specs=[pl.BlockSpec(memory...  15.2 us
    ppermute x12, starting transfers between devices, swap(): return lax.ppermute(array, AXIS, [(i, i ^ by) for i in range(count)])  15.1 us
    ppermute x5, waiting for transfers between devices, shift(): return lax.ppermute(array, AXIS, pairs)  13.5 us
    ppermute x5, starting transfers between devices, shift(): return lax.ppermute(array, AXIS, pairs)  8.66 us
    ppermute x12, waiting for transfers between devices, swap(): return lax.ppermute(array, AXIS, [(i, i ^ by) for i in range(count)])  4.76 us
  transfers between devices with their start and end apart: 17, of which 7 were waited for; matrix products, arithmetic and copies ran while one was open for 0% of the time, Pallas kernels for 4%

profile of v2, /device:TPU:0, one launch (start us, length us, event | category | flops | bytes accessed | tf_op | source)
XLA Modules:
  0.0 58.8 jit_solution(2669037454977876715)
XLA Ops:
  0.6 1.0 %shard_map.102 = (bf16[144,256]{1,0:T(8,128)(2,1)S(1)}, bf16[144,256]{1,0:T(8,128)(2,1)S(1)}, bf16[144,256]{1,0:T(8,128)(2,1)S(1)}, bf16[144,256]{1,0:T(8,128)(2,1)S(1)}) custom-call(s32[1]{0:T(128)} %bitcast.r_ref, bf16[128,512]{1,0:T(8,128)(2,1)} %key_ref.1, bf16[128,512]{1,0:T(8,128)(2,1)} %value_ref.1, s32[1,128]{1,0:T(1,128)} %bitcast.4, s32[1,128]{1,0:T(1,128)} %bitcast.5), custom_call_target="tpu_custom_call" | custom-call | tf_op jit(solution)/shard_map/pallas_call | solution.py:36
  1.6 3.0 %collective-permute-start = (bf16[144,256]{1,0:T(8,128)(2,1)S(1)}, bf16[144,256]{1,0:T(8,128)(2,1)S(1)}, u32[]{:S(2)}, u32[]{:S(2)}) collective-permute-start(bf16[144,256]{1,0:T(8,128)(2,1)S(1)} %get-tuple-element.36), channel_id=1, source_target_pairs={{0,2},{2,0},{4,6},{6,4},{8,10},{10,8},{12,14},{14,12},{16,18},{18,... | collective-permute-start | bytes 221192 | tf_op jit(solution)/shard_map/ppermute | solution.py:282
  4.7 1.5 %collective-permute-start.1 = (bf16[144,256]{1,0:T(8,128)(2,1)S(1)}, bf16[144,256]{1,0:T(8,128)(2,1)S(1)}, u32[]{:S(2)}, u32[]{:S(2)}) collective-permute-start(bf16[144,256]{1,0:T(8,128)(2,1)S(1)} %get-tuple-element.37), channel_id=1, source_target_pairs={{0,4},{2,6},{4,0},{6,2},{8,12},{10,14},{12,8},{14,10},{16,20},{18,... | collective-permute-start | bytes 221192 | tf_op jit(solution)/shard_map/ppermute | solution.py:282
  6.2 0.7 %copy-done = s32[16]{0:T(128)S(1)} copy-done((s32[16]{0:T(128)S(1)}, s32[16]{0:T(128)}, u32[]{:S(2)}) %copy-start) | copy-done | bytes 88
  6.9 1.4 %shard_map.103 = (bf16[128,1024]{1,0:T(8,128)(2,1)S(1)}, bf16[128,1024]{1,0:T(8,128)(2,1)S(1)}, bf16[128,1024]{1,0:T(8,128)(2,1)S(1)}, bf16[128,1024]{1,0:T(8,128)(2,1)S(1)}) custom-call(s32[1]{0:T(128)} %bitcast.r_ref, bf16[128,2048]{1,0:T(8,128)(2,1)} %query_ref.1, bf16[128,2048]{1,0:T(8,128)(2,1)} %grad_ref.1), custom_call_target="tpu_custom_call" | custom-call | tf_op jit(solution)/shard_map/pallas_call | solution.py:36
  8.3 0.1 pad_add_fusion.where_ref
  8.4 0.6 %collective-permute-done.1.refs_2_ = bf16[144,256]{1,0:T(8,128)(2,1)S(1)} collective-permute-done((bf16[144,256]{1,0:T(8,128)(2,1)S(1)}, bf16[144,256]{1,0:T(8,128)(2,1)S(1)}, u32[]{:S(2)}, u32[]{:S(2)}) %collective-permute-start.1) | collective-permute-done | bytes 73760 | tf_op jit(solution)/shard_map/ppermute | solution.py:282
  9.0 2.4 %collective-permute-done.2.refs_3_ = bf16[144,256]{1,0:T(8,128)(2,1)S(1)} collective-permute-done((bf16[144,256]{1,0:T(8,128)(2,1)S(1)}, bf16[144,256]{1,0:T(8,128)(2,1)S(1)}, u32[]{:S(2)}, u32[]{:S(2)}) %collective-permute-start.2) | collective-permute-done | bytes 73760 | tf_op jit(solution)/shard_map/ppermute | solution.py:282
  11.4 0.1 shard_map.104
  11.5 1.6 %collective-permute-start.4 = (bf16[4,144,256]{2,1,0:T(8,128)(2,1)S(1)}, bf16[4,144,256]{2,1,0:T(8,128)(2,1)S(1)}, u32[]{:S(2)}, u32[]{:S(2)}) collective-permute-start(bf16[4,144,256]{2,1,0:T(8,128)(2,1)S(1)} %get-tuple-element.46.own_ref), channel_id=1, source_target_pairs={{0,8},{2,10},{4,12},{6,14},{8,16},{10,18},{12,20},{14,22},{16,24},... | collective-permute-start | bytes 884744 | tf_op jit(solution)/shard_map/ppermute | solution.py:286
  13.1 0.5 collective-permute-start.6
  13.6 0.5 collective-permute-start.7
  14.2 2.4 %collective-permute-start.8 = (bf16[128,1024]{1,0:T(8,128)(2,1)S(1)}, bf16[128,1024]{1,0:T(8,128)(2,1)S(1)}, u32[]{:S(2)}, u32[]{:S(2)}) collective-permute-start(bf16[128,1024]{1,0:T(8,128)(2,1)S(1)} %get-tuple-element.50), channel_id=1, source_target_pairs={{0,6},{2,4},{4,2},{6,0},{8,14},{10,12},{12,10},{14,8},{16,22},{18,... | collective-permute-start | bytes 786440 | tf_op jit(solution)/shard_map/ppermute | solution.py:282
  16.6 2.2 %collective-permute-start.3 = (f32[8,128]{1,0:T(8,128)S(1)}, f32[8,128]{1,0:T(8,128)S(1)}, u32[]{:S(2)}, u32[]{:S(2)}) collective-permute-start(f32[8,128]{1,0:T(8,128)S(1)} %get-tuple-element.45.count_ref), channel_id=1, source_target_pairs={{0,24},{2,26},{4,28},{6,30},{8,0},{10,2},{12,4},{14,6},{16,8},{18,... | collective-permute-start | bytes 12296 | tf_op jit(solution)/shard_map/ppermute | solution.py:286
  18.8 1.7 %collective-permute-done.3.other_ref = f32[8,128]{1,0:T(8,128)S(1)} collective-permute-done((f32[8,128]{1,0:T(8,128)S(1)}, f32[8,128]{1,0:T(8,128)S(1)}, u32[]{:S(2)}, u32[]{:S(2)}) %collective-permute-start.3) | collective-permute-done | bytes 4128 | tf_op jit(solution)/shard_map/ppermute | solution.py:286
  20.6 2.3 %collective-permute-start.5 = (bf16[2,144,256]{2,1,0:T(8,128)(2,1)S(1)}, bf16[2,144,256]{2,1,0:T(8,128)(2,1)S(1)}, u32[]{:S(2)}, u32[]{:S(2)}) collective-permute-start(bf16[2,144,256]{2,1,0:T(8,128)(2,1)S(1)} %get-tuple-element.47), channel_id=1, source_target_pairs={{0,16},{2,18},{4,20},{6,22},{8,24},{10,26},{12,28},{14,30},{16,0},... | collective-permute-start | bytes 442376 | tf_op jit(solution)/shard_map/ppermute | solution.py:286
  22.8 5.4 %collective-permute-done.5.refs_1_ = bf16[2,144,256]{2,1,0:T(8,128)(2,1)S(1)} collective-permute-done((bf16[2,144,256]{2,1,0:T(8,128)(2,1)S(1)}, bf16[2,144,256]{2,1,0:T(8,128)(2,1)S(1)}, u32[]{:S(2)}, u32[]{:S(2)}) %collective-permute-start.5) | collective-permute-done | bytes 147488 | tf_op jit(solution)/shard_map/ppermute | solution.py:286
  28.2 10.8 %shard_map.105 = (bf16[128,1024]{1,0:T(8,128)(2,1)S(1)}, bf16[128,1024]{1,0:T(8,128)(2,1)S(1)}, bf16[128,1024]{1,0:T(8,128)(2,1)S(1)}, bf16[128,1024]{1,0:T(8,12...) custom-call(s32[6]{0:T(128)S(1)} %pad_add_fusion.where_ref, ...), custom_call_target="tpu_custom_call" | custom-call | flops 2818572288 | bytes 4194304 | tf_op jit(solution)/shard_map/pallas_call | solution.py:36
  39.0 1.3 %collective-permute-start.12 = (bf16[512,256]{1,0:T(8,128)(2,1)S(1)}, bf16[512,256]{1,0:T(8,128)(2,1)S(1)}, u32[]{:S(2)}, u32[]{:S(2)}) collective-permute-start(bf16[512,256]{1,0:T(8,128)(2,1)S(1)} %get-tuple-element.58), channel_id=1, source_target_pairs={{8,0},{10,2},{12,4},{14,6},{16,8},{18,10},{20,12},{22,14},{24,16},... | collective-permute-start | bytes 786440 | tf_op jit(solution)/shard_map/ppermute | solution.py:286
  40.3 0.6 %collective-permute-start.9 = (bf16[128,1024]{1,0:T(8,128)(2,1)S(1)}, bf16[128,1024]{1,0:T(8,128)(2,1)S(1)}, u32[]{:S(2)}, u32[]{:S(2)}) collective-permute-start(bf16[128,1024]{1,0:T(8,128)(2,1)S(1)} %get-tuple-element.52), channel_id=1, source_target_pairs={{0,2},{2,0},{4,6},{6,4},{8,10},{10,8},{12,14},{14,12},{16,18},{18,... | collective-permute-start | bytes 786440 | tf_op jit(solution)/shard_map/ppermute | solution.py:282
  40.9 0.5 collective-permute-start.10
  41.5 2.4 %collective-permute-start.11 = (bf16[128,1024]{1,0:T(8,128)(2,1)S(1)}, bf16[128,1024]{1,0:T(8,128)(2,1)S(1)}, u32[]{:S(2)}, u32[]{:S(2)}) collective-permute-start(bf16[128,1024]{1,0:T(8,128)(2,1)S(1)} %get-tuple-element.54), channel_id=1, source_target_pairs={{0,6},{2,4},{4,2},{6,0},{8,14},{10,12},{12,10},{14,8},{16,22},{18,... | collective-permute-start | bytes 786440 | tf_op jit(solution)/shard_map/ppermute | solution.py:282
  43.9 1.3 %collective-permute-start.13 = (bf16[256,256]{1,0:T(8,128)(2,1)S(1)}, bf16[256,256]{1,0:T(8,128)(2,1)S(1)}, u32[]{:S(2)}, u32[]{:S(2)}) collective-permute-start(bf16[256,256]{1,0:T(8,128)(2,1)S(1)} %get-tuple-element.59), channel_id=1, source_target_pairs={{16,0},{18,2},{20,4},{22,6},{24,8},{26,10},{28,12},{30,14},{17,1},... | collective-permute-start | bytes 393224 | tf_op jit(solution)/shard_map/ppermute | solution.py:286
  45.2 6.5 %collective-permute-done.13.refs_1_ = bf16[256,256]{1,0:T(8,128)(2,1)S(1)} collective-permute-done((bf16[256,256]{1,0:T(8,128)(2,1)S(1)}, bf16[256,256]{1,0:T(8,128)(2,1)S(1)}, u32[]{:S(2)}, u32[]{:S(2)}) %collective-permute-start.13) | collective-permute-done | bytes 131104 | tf_op jit(solution)/shard_map/ppermute | solution.py:286
  51.6 0.1 shard_map.107
  51.8 0.6 %collective-permute-start.14 = (bf16[128,256]{1,0:T(8,128)(2,1)S(1)}, bf16[128,256]{1,0:T(8,128)(2,1)S(1)}, u32[]{:S(2)}, u32[]{:S(2)}) collective-permute-start(bf16[128,256]{1,0:T(8,128)(2,1)S(1)} %get-tuple-element.61), channel_id=1, source_target_pairs={{0,2},{2,0},{4,6},{6,4},{8,10},{10,8},{12,14},{14,12},{16,18},{18,... | collective-permute-start | bytes 196616 | tf_op jit(solution)/shard_map/ppermute | solution.py:282
  52.4 0.5 collective-permute-start.15
  52.9 2.4 %collective-permute-start.16 = (bf16[128,256]{1,0:T(8,128)(2,1)S(1)}, bf16[128,256]{1,0:T(8,128)(2,1)S(1)}, u32[]{:S(2)}, u32[]{:S(2)}) collective-permute-start(bf16[128,256]{1,0:T(8,128)(2,1)S(1)} %get-tuple-element.63), channel_id=1, source_target_pairs={{0,6},{2,4},{4,2},{6,0},{8,14},{10,12},{12,10},{14,8},{16,22},{18,... | collective-permute-start | bytes 196616 | tf_op jit(solution)/shard_map/ppermute | solution.py:282
  55.3 1.1 %shard_map.106 = (bf16[128,2048]{1,0:T(8,128)(2,1)}, bf16[128,2048]{1,0:T(8,128)(2,1)}) custom-call(s32[1]{0:T(128)} %bitcast.r_ref, bf16[128,1024]{1,0:T(8,128)(2,1)S(1)} %get-tuple-element.51.refs_0_, bf16[128,1024]{1,0:T(8,128)(2,1)S(1)} %collective-permute-done.9.refs_1_, bf16[128,1024]{1,0:T(8,128)(2,1)S(1)} %collective-permute-done.10.refs_2_, ...), custom_call_target="tpu_custom_call" | custom-call | tf_op jit(solution)/shard_map/pallas_call | solution.py:36
  56.4 0.2 collective-permute-done.15.refs_2_
  56.6 1.4 %collective-permute-done.16.refs_3_ = bf16[128,256]{1,0:T(8,128)(2,1)S(1)} collective-permute-done((bf16[128,256]{1,0:T(8,128)(2,1)S(1)}, bf16[128,256]{1,0:T(8,128)(2,1)S(1)}, u32[]{:S(2)}, u32[]{:S(2)}) %collective-permute-start.16) | collective-permute-done | bytes 65568 | tf_op jit(solution)/shard_map/ppermute | solution.py:282
  58.1 0.7 %shard_map.108 = (bf16[128,512]{1,0:T(8,128)(2,1)}, bf16[128,512]{1,0:T(8,128)(2,1)}) custom-call(s32[1]{0:T(128)} %bitcast.r_ref, bf16[128,256]{1,0:T(8,128)(2,1)S(1)} %get-tuple-element.60.refs_0_, bf16[128,256]{1,0:T(8,128)(2,1)S(1)} %collective-permute-done.14.refs_1_, bf16[128,256]{1,0:T(8,128)(2,1)S(1)} %collective-permute-done.15.refs_2_, ...), custom_call_target="tpu_custom_call" | custom-call | tf_op jit(solution)/shard_map/pallas_call | solution.py:36
  (13 shorter events, 0.1 us)
Async XLA Ops:
  1.6 6.7 %collective-permute-start = (bf16[144,256]{1,0:T(8,128)(2,1)S(1)}, bf16[144,256]{1,0:T(8,128)(2,1)S(1)}, u32[]{:S(2)}, u32[]{:S(2)}) collective-permute-start(bf16[144,256]{1,0:T(8,128)(2,1)S(1)} %get-tuple-element.36), channel_id=1, source_target_pairs={{0,2},{2,0},{4,6},{6,4},{8,10},{10,8},{12,14},{14,12},{16,18},{18,... | collective-permute-start | bytes 221192 | tf_op jit(solution)/shard_map/ppermute | solution.py:282
  4.7 4.4 %collective-permute-start.1 = (bf16[144,256]{1,0:T(8,128)(2,1)S(1)}, bf16[144,256]{1,0:T(8,128)(2,1)S(1)}, u32[]{:S(2)}, u32[]{:S(2)}) collective-permute-start(bf16[144,256]{1,0:T(8,128)(2,1)S(1)} %get-tuple-element.37), channel_id=1, source_target_pairs={{0,4},{2,6},{4,0},{6,2},{8,12},{10,14},{12,8},{14,10},{16,20},{18,... | collective-permute-start | bytes 221192 | tf_op jit(solution)/shard_map/ppermute | solution.py:282
  6.2 5.3 %collective-permute-start.2 = (bf16[144,256]{1,0:T(8,128)(2,1)S(1)}, bf16[144,256]{1,0:T(8,128)(2,1)S(1)}, u32[]{:S(2)}, u32[]{:S(2)}) collective-permute-start(bf16[144,256]{1,0:T(8,128)(2,1)S(1)} %get-tuple-element.38), channel_id=1, source_target_pairs={{0,6},{2,4},{4,2},{6,0},{8,14},{10,12},{12,10},{14,8},{16,22},{18,... | collective-permute-start | bytes 221192 | tf_op jit(solution)/shard_map/ppermute | solution.py:282
  6.2 0.7 %copy-start = (s32[16]{0:T(128)S(1)}, s32[16]{0:T(128)}, u32[]{:S(2)}) copy-start(s32[16]{0:T(128)} %param.13) | copy-start | bytes 196
  11.5 16.7 %collective-permute-start.4 = (bf16[4,144,256]{2,1,0:T(8,128)(2,1)S(1)}, bf16[4,144,256]{2,1,0:T(8,128)(2,1)S(1)}, u32[]{:S(2)}, u32[]{:S(2)}) collective-permute-start(bf16[4,144,256]{2,1,0:T(8,128)(2,1)S(1)} %get-tuple-element.46.own_ref), channel_id=1, source_target_pairs={{0,8},{2,10},{4,12},{6,14},{8,16},{10,18},{12,20},{14,22},{16,24},... | collective-permute-start | bytes 884744 | tf_op jit(solution)/shard_map/ppermute | solution.py:286
  13.1 15.1 %collective-permute-start.6 = (bf16[128,1024]{1,0:T(8,128)(2,1)S(1)}, bf16[128,1024]{1,0:T(8,128)(2,1)S(1)}, u32[]{:S(2)}, u32[]{:S(2)}) collective-permute-start(bf16[128,1024]{1,0:T(8,128)(2,1)S(1)} %get-tuple-element.48), channel_id=1, source_target_pairs={{0,2},{2,0},{4,6},{6,4},{8,10},{10,8},{12,14},{14,12},{16,18},{18,... | collective-permute-start | bytes 786440 | tf_op jit(solution)/shard_map/ppermute | solution.py:282
  13.6 14.5 %collective-permute-start.7 = (bf16[128,1024]{1,0:T(8,128)(2,1)S(1)}, bf16[128,1024]{1,0:T(8,128)(2,1)S(1)}, u32[]{:S(2)}, u32[]{:S(2)}) collective-permute-start(bf16[128,1024]{1,0:T(8,128)(2,1)S(1)} %get-tuple-element.49), channel_id=1, source_target_pairs={{0,4},{2,6},{4,0},{6,2},{8,12},{10,14},{12,8},{14,10},{16,20},{18,... | collective-permute-start | bytes 786440 | tf_op jit(solution)/shard_map/ppermute | solution.py:282
  14.2 14.0 %collective-permute-start.8 = (bf16[128,1024]{1,0:T(8,128)(2,1)S(1)}, bf16[128,1024]{1,0:T(8,128)(2,1)S(1)}, u32[]{:S(2)}, u32[]{:S(2)}) collective-permute-start(bf16[128,1024]{1,0:T(8,128)(2,1)S(1)} %get-tuple-element.50), channel_id=1, source_target_pairs={{0,6},{2,4},{4,2},{6,0},{8,14},{10,12},{12,10},{14,8},{16,22},{18,... | collective-permute-start | bytes 786440 | tf_op jit(solution)/shard_map/ppermute | solution.py:282
  16.6 4.0 %collective-permute-start.3 = (f32[8,128]{1,0:T(8,128)S(1)}, f32[8,128]{1,0:T(8,128)S(1)}, u32[]{:S(2)}, u32[]{:S(2)}) collective-permute-start(f32[8,128]{1,0:T(8,128)S(1)} %get-tuple-element.45.count_ref), channel_id=1, source_target_pairs={{0,24},{2,26},{4,28},{6,30},{8,0},{10,2},{12,4},{14,6},{16,8},{18,... | collective-permute-start | bytes 12296 | tf_op jit(solution)/shard_map/ppermute | solution.py:286
  20.6 7.6 %collective-permute-start.5 = (bf16[2,144,256]{2,1,0:T(8,128)(2,1)S(1)}, bf16[2,144,256]{2,1,0:T(8,128)(2,1)S(1)}, u32[]{:S(2)}, u32[]{:S(2)}) collective-permute-start(bf16[2,144,256]{2,1,0:T(8,128)(2,1)S(1)} %get-tuple-element.47), channel_id=1, source_target_pairs={{0,16},{2,18},{4,20},{6,22},{8,24},{10,26},{12,28},{14,30},{16,0},... | collective-permute-start | bytes 442376 | tf_op jit(solution)/shard_map/ppermute | solution.py:286
  39.0 12.6 %collective-permute-start.12 = (bf16[512,256]{1,0:T(8,128)(2,1)S(1)}, bf16[512,256]{1,0:T(8,128)(2,1)S(1)}, u32[]{:S(2)}, u32[]{:S(2)}) collective-permute-start(bf16[512,256]{1,0:T(8,128)(2,1)S(1)} %get-tuple-element.58), channel_id=1, source_target_pairs={{8,0},{10,2},{12,4},{14,6},{16,8},{18,10},{20,12},{22,14},{24,16},... | collective-permute-start | bytes 786440 | tf_op jit(solution)/shard_map/ppermute | solution.py:286
  40.3 12.6 %collective-permute-start.9 = (bf16[128,1024]{1,0:T(8,128)(2,1)S(1)}, bf16[128,1024]{1,0:T(8,128)(2,1)S(1)}, u32[]{:S(2)}, u32[]{:S(2)}) collective-permute-start(bf16[128,1024]{1,0:T(8,128)(2,1)S(1)} %get-tuple-element.52), channel_id=1, source_target_pairs={{0,2},{2,0},{4,6},{6,4},{8,10},{10,8},{12,14},{14,12},{16,18},{18,... | collective-permute-start | bytes 786440 | tf_op jit(solution)/shard_map/ppermute | solution.py:282
  40.9 14.4 %collective-permute-start.10 = (bf16[128,1024]{1,0:T(8,128)(2,1)S(1)}, bf16[128,1024]{1,0:T(8,128)(2,1)S(1)}, u32[]{:S(2)}, u32[]{:S(2)}) collective-permute-start(bf16[128,1024]{1,0:T(8,128)(2,1)S(1)} %get-tuple-element.53), channel_id=1, source_target_pairs={{0,4},{2,6},{4,0},{6,2},{8,12},{10,14},{12,8},{14,10},{16,20},{18,... | collective-permute-start | bytes 786440 | tf_op jit(solution)/shard_map/ppermute | solution.py:282
  41.5 13.8 %collective-permute-start.11 = (bf16[128,1024]{1,0:T(8,128)(2,1)S(1)}, bf16[128,1024]{1,0:T(8,128)(2,1)S(1)}, u32[]{:S(2)}, u32[]{:S(2)}) collective-permute-start(bf16[128,1024]{1,0:T(8,128)(2,1)S(1)} %get-tuple-element.54), channel_id=1, source_target_pairs={{0,6},{2,4},{4,2},{6,0},{8,14},{10,12},{12,10},{14,8},{16,22},{18,... | collective-permute-start | bytes 786440 | tf_op jit(solution)/shard_map/ppermute | solution.py:282
  43.9 7.7 %collective-permute-start.13 = (bf16[256,256]{1,0:T(8,128)(2,1)S(1)}, bf16[256,256]{1,0:T(8,128)(2,1)S(1)}, u32[]{:S(2)}, u32[]{:S(2)}) collective-permute-start(bf16[256,256]{1,0:T(8,128)(2,1)S(1)} %get-tuple-element.59), channel_id=1, source_target_pairs={{16,0},{18,2},{20,4},{22,6},{24,8},{26,10},{28,12},{30,14},{17,1},... | collective-permute-start | bytes 393224 | tf_op jit(solution)/shard_map/ppermute | solution.py:286
  51.8 4.6 %collective-permute-start.14 = (bf16[128,256]{1,0:T(8,128)(2,1)S(1)}, bf16[128,256]{1,0:T(8,128)(2,1)S(1)}, u32[]{:S(2)}, u32[]{:S(2)}) collective-permute-start(bf16[128,256]{1,0:T(8,128)(2,1)S(1)} %get-tuple-element.61), channel_id=1, source_target_pairs={{0,2},{2,0},{4,6},{6,4},{8,10},{10,8},{12,14},{14,12},{16,18},{18,... | collective-permute-start | bytes 196616 | tf_op jit(solution)/shard_map/ppermute | solution.py:282
  52.4 4.3 %collective-permute-start.15 = (bf16[128,256]{1,0:T(8,128)(2,1)S(1)}, bf16[128,256]{1,0:T(8,128)(2,1)S(1)}, u32[]{:S(2)}, u32[]{:S(2)}) collective-permute-start(bf16[128,256]{1,0:T(8,128)(2,1)S(1)} %get-tuple-element.62), channel_id=1, source_target_pairs={{0,4},{2,6},{4,0},{6,2},{8,12},{10,14},{12,8},{14,10},{16,20},{18,... | collective-permute-start | bytes 196616 | tf_op jit(solution)/shard_map/ppermute | solution.py:282
  52.9 5.2 %collective-permute-start.16 = (bf16[128,256]{1,0:T(8,128)(2,1)S(1)}, bf16[128,256]{1,0:T(8,128)(2,1)S(1)}, u32[]{:S(2)}, u32[]{:S(2)}) collective-permute-start(bf16[128,256]{1,0:T(8,128)(2,1)S(1)} %get-tuple-element.63), channel_id=1, source_target_pairs={{0,6},{2,4},{4,2},{6,0},{8,14},{10,12},{12,10},{14,8},{16,22},{18,... | collective-permute-start | bytes 196616 | tf_op jit(solution)/shard_map/ppermute | solution.py:282

commit v3 on v2

--- a/solution.py
+++ b/solution.py
@@ -95,10 +95,9 @@
     return 64.0 * line[:, 0:HEAD_DIM] + line[:, HEAD_DIM:]
 
 
-def gather_kernel(group, needs, r_ref, *refs):
-    slots, outs = refs[:group], refs[group:]
+def gather_kernel(group, r_ref, *refs):
+    slots, (parts, count_ref, full) = refs[:group], (refs[group:-2], *refs[-2:])
     r = r_ref[0]
-    full, count_ref = outs[0], outs[-1]
     rows = full.shape[1] - PAD
     total = jnp.zeros((1, HEAD_DIM), F32)
     for j in range(group):
@@ -106,31 +105,29 @@
         total = total + slots[j][rows : rows + 1, HEAD_DIM:].astype(F32)
     total = jnp.broadcast_to(jnp.sum(total, axis=1, keepdims=True), count_ref.shape)
     count_ref[...] = total
-    full[0, rows + 8 :, :] = encode_count(total)
-    for need, out in zip([n for n in needs if n < group], outs[1:-1]):
-        out[...] = full[group - need :]
-        out[0, rows + 8 :, :] = encode_count(total)
-
-
-def ordered_pieces(needs, group, own_ref, halo_refs):
-    pieces = []
-    for need, ref in reversed(list(zip(needs, halo_refs))):
-        pieces += [(ref, i) for i in range(need)]
-    return pieces + [(own_ref, i) for i in range(group)]
+    first = 0
+    for part in parts:
+        part[...] = full[first : first + part.shape[0]]
+        first += part.shape[0]
+    parts[-1][0, rows + 8 :, :] = encode_count(total)
+
+
+def relay_kernel(part_ref, got_ref, out_ref):
+    out_ref[...] = (part_ref[...] + got_ref[...].astype(F32)).astype(BF16)
 
 
 def attention_kernel(
-    group, needs, heads, token_count, counts_ride, where_ref, count_ref, other_ref, own_ref, *refs
+    group, sizes, links, heads, token_count, counts_ride, where_ref, count_ref, other_ref, *refs
 ):
-    halo_refs, refs = refs[: len(needs)], refs[len(needs) :]
+    shards = range(group)
+    hops = sum(sizes) - group
+    part_refs, refs = refs[: len(sizes)], refs[len(sizes) :]
     qg_refs, refs = refs[:group], refs[group:]
-    out_refs, refs = refs[:group], refs[group:]
-    own_out, refs = refs[0], refs[1:]
-    halo_outs, refs = refs[: len(needs)], refs[len(needs) :]
-    keys, values, keys_t, values_t, dkeys, dvalues, qg, od, lines = refs
+    out_refs, own_out, refs = refs[:group], refs[group], refs[group + 1 :]
+    sum_refs, (dkeys, dvalues, od, *refs) = refs[:-9], refs[-9:]
+    keys, values, keys_t, values_t, qg, lines = refs
     r = where_ref[0]
-    rows = own_ref.shape[1] - PAD
-    hops = sum(needs)
+    rows = qg_refs[0].shape[0]
     blocks = hops + group
     span = (hops + 1) * rows
     width = heads * HEAD_DIM
@@ -138,13 +135,13 @@
     exp_scale = scale * 1.4426950408889634
     lowest = jnp.maximum(hops * rows - where_ref[1], 0)
 
-    pieces = ordered_pieces(needs, group, own_ref, halo_refs)
     lines[...] = jnp.zeros_like(lines)
     total = count_ref[...] + other_ref[...]
     if counts_ride:
-        for ref in halo_refs:
-            total = total + decode_count(ref[0, rows + 8 :, :])
+        for i in links:
+            total = total + decode_count(part_refs[i][0, rows + 8 :, :])
     factor = token_count / jnp.maximum(total[0:1, :], 1.0)
+    pieces = [(ref, i) for ref in part_refs for i in range(ref.shape[0])]
     for kb, (ref, i) in enumerate(pieces):
         at = slice(kb * rows, (kb + 1) * rows)
         key, value = ref[i, 0:rows, 0:HEAD_DIM], ref[i, 0:rows, HEAD_DIM:]
@@ -156,9 +153,8 @@
         if kb < hops:
             doc = jnp.where(kb * rows < lowest, -1.0, doc)
         else:
-            s = kb - hops
             mask = ref[i, rows : rows + 1, HEAD_DIM:].astype(F32)
-            lines[blocks + s : blocks + s + 1, :] = mask * factor
+            lines[blocks + kb - hops : blocks + kb - hops + 1, :] = mask * factor
         lines[kb : kb + 1, :] = doc
     columns = lines[...].T
     dkeys[...] = jnp.zeros_like(dkeys)
@@ -170,78 +166,91 @@
     pos = lax.broadcasted_iota(jnp.int32, (span, PAIR * rows), 0)
     diag = lax.broadcasted_iota(jnp.int32, (rows, PAIR * rows), 0)
     own_lane = jnp.concatenate([lane] * PAIR, axis=1)
-    for s in range(group):
-        at = slice(s * rows, s * rows + span)
+    starts = {}
+    for s in shards:
         doc_row = lines[hops + s : hops + s + 1, :]
         start = jnp.zeros((1, rows), F32)
         for kb in range(s, s + hops + 1):
             before = jnp.where(columns[:, kb : kb + 1] < doc_row, 1.0, 0.0)
             start = start + jnp.sum(before, axis=0, keepdims=True)
-        start = jnp.maximum(start.astype(jnp.int32), lowest - s * rows)
+        starts[s] = jnp.maximum(start.astype(jnp.int32), lowest - s * rows)
+    steps = [(s, h0) for s in shards for h0 in range(0, heads, PAIR)]
+
+    def head(part, s, h):
+        return qg[s, :, part * width + h * HEAD_DIM : part * width + (h + 1) * HEAD_DIM]
+
+    def products(s, h0):
+        at = slice(s * rows, s * rows + span)
+        hs = range(h0, h0 + PAIR)
+        query = jnp.concatenate([head(0, s, h) for h in hs], axis=0)
         cot_col = columns[:, blocks + s : blocks + s + 1]
-        for h0 in range(0, heads, PAIR):
-            hs = range(h0, h0 + PAIR)
-            low = jnp.concatenate(
-                [
-                    jnp.maximum(start, hops * rows + 1 + lane - where_ref[2 + h])
-                    for h in hs
-                ],
-                axis=1,
-            )
-            query = jnp.concatenate(
-                [qg[s, :, h * HEAD_DIM : (h + 1) * HEAD_DIM] for h in hs], axis=0
-            )
-            cots = [
-                qg[s, :, width + h * HEAD_DIM : width + (h + 1) * HEAD_DIM].astype(F32) * cot_col
-                for h in hs
-            ]
-            cots = [c.astype(BF16) for c in cots]
-            cot = jnp.concatenate(cots, axis=0)
-            cot_t = jnp.concatenate([c.T for c in cots], axis=1).astype(F32)
-            scores = dot(keys[at, :], query, NT)
-            allowed = pos >= low
-            scores = jnp.where(allowed, scores, NEG)
-            last = jnp.where(diag <= own_lane, scores[hops * rows :], NEG)
-            scores = jnp.concatenate([scores[: hops * rows], last], axis=0)
-            row_max = jnp.max(scores, axis=0, keepdims=True)
-            raised = jnp.exp2(scores * exp_scale - row_max * exp_scale)
-            weights = raised * (1.0 / jnp.sum(raised, axis=0, keepdims=True))
-            weights_low = weights.astype(BF16)
-            output_t = dot(values_t[:, at], weights_low)
-            row_dot = jnp.sum(cot_t * output_t, axis=0, keepdims=True)
-            grad_prob = dot(values[at, :], cot, NT)
-            grad_score = (weights * (grad_prob - row_dot)).astype(BF16)
-            dvalues[at, :] += dot(weights_low, cot)
-            dkeys[at, :] += dot(grad_score, query)
-            grad_query_t = dot(keys_t[:, at], grad_score) * scale
-            for i, h in enumerate(hs):
-                cut = slice(i * rows, (i + 1) * rows)
-                od[s, :, h * HEAD_DIM : (h + 1) * HEAD_DIM] = output_t[:, cut].T.astype(BF16)
-                od[s, :, width + h * HEAD_DIM : width + (h + 1) * HEAD_DIM] = grad_query_t[
-                    :, cut
-                ].T.astype(BF16)
+        cots = [(head(1, s, h).astype(F32) * cot_col).astype(BF16) for h in hs]
+        cot = jnp.concatenate(cots, axis=0)
+        cot_t = jnp.concatenate([c.T for c in cots], axis=1).astype(F32)
+        scores = dot(keys[at, :], query, NT)
+        return query, cot, cot_t, scores
+
+    def softmax(s, h0, scores):
+        hs = range(h0, h0 + PAIR)
+        low = jnp.concatenate(
+            [jnp.maximum(starts[s], hops * rows + 1 + lane - where_ref[2 + h]) for h in hs],
+            axis=1,
+        )
+        scores = jnp.where(pos >= low, scores, NEG)
+        last = jnp.where(diag <= own_lane, scores[hops * rows :], NEG)
+        scores = jnp.concatenate([scores[: hops * rows], last], axis=0)
+        row_max = jnp.max(scores, axis=0, keepdims=True)
+        raised = jnp.exp2(scores * exp_scale - row_max * exp_scale)
+        return raised * (1.0 / jnp.sum(raised, axis=0, keepdims=True))
+
+    def finish(s, h0, query, cot, cot_t, weights):
+        at = slice(s * rows, s * rows + span)
+        weights_low = weights.astype(BF16)
+        output_t = dot(values_t[:, at], weights_low)
+        row_dot = jnp.sum(cot_t * output_t, axis=0, keepdims=True)
+        grad_prob = dot(values[at, :], cot, NT)
+        grad_score = (weights * (grad_prob - row_dot)).astype(BF16)
+        dvalues[at, :] += dot(weights_low, cot)
+        dkeys[at, :] += dot(grad_score, query)
+        grad_query_t = dot(keys_t[:, at], grad_score) * scale
+        for i in range(PAIR):
+            h = h0 + i
+            cut = slice(i * rows, (i + 1) * rows)
+            od[s, :, h * HEAD_DIM : (h + 1) * HEAD_DIM] = output_t[:, cut].T.astype(BF16)
+            od[s, :, width + h * HEAD_DIM : width + (h + 1) * HEAD_DIM] = grad_query_t[
+                :, cut
+            ].T.astype(BF16)
+
+    ahead = products(*steps[0])
+    for i, step in enumerate(steps):
+        query, cot, cot_t, scores = ahead
+        if i + 1 < len(steps):
+            ahead = products(*steps[i + 1])
+        finish(*step, query, cot, cot_t, softmax(*step, scores))
 
     for j in range(group):
         out_refs[j][...] = od[r ^ j]
-    first = hops * rows
-    own_out[:, 0:HEAD_DIM] = dkeys[first:, :]
-    own_out[:, HEAD_DIM:] = dvalues[first:, :]
-    for need, out in zip(needs, halo_outs):
-        first -= need * rows
-        out[:, 0:HEAD_DIM] = dkeys[first : first + need * rows, :].astype(BF16)
-        out[:, HEAD_DIM:] = dvalues[first : first + need * rows, :].astype(BF16)
-
-
-def add_kv_kernel(group, needs, r_ref, own_ref, *refs):
-    halo_refs, out_refs, total = refs[: len(needs)], refs[len(needs) : -1], refs[-1]
+    edge = hops * rows
+    own_out[:, 0:HEAD_DIM] = dkeys[edge:, :]
+    own_out[:, HEAD_DIM:] = dvalues[edge:, :]
+    edge = 0
+    for out in sum_refs:
+        at = slice(edge, edge + out.shape[0])
+        out[:, 0:HEAD_DIM] = dkeys[at, :].astype(out.dtype)
+        out[:, HEAD_DIM:] = dvalues[at, :].astype(out.dtype)
+        edge += out.shape[0]
+
+
+def add_kv_kernel(group, firsts, r_ref, own_ref, *refs):
+    got_refs, out_refs, total = refs[: len(firsts)], refs[len(firsts) : -1], refs[-1]
     r = r_ref[0]
     rows = own_ref.shape[0] // group
     scale = HEAD_DIM**-0.5
     for s in range(group):
         part = own_ref[s * rows : (s + 1) * rows, :]
-        for need, ref in zip(needs, halo_refs):
-            i = s - (group - need)
-            if i >= 0:
+        for first, ref in zip(firsts, got_refs):
+            i = s - first
+            if 0 <= i < ref.shape[0] // rows:
                 part = part + ref[i * rows : (i + 1) * rows, :].astype(F32)
         total[s, :, 0:HEAD_DIM] = (part[:, 0:HEAD_DIM] * scale).astype(BF16)
         total[s, :, HEAD_DIM:] = part[:, HEAD_DIM:].astype(BF16)
@@ -310,54 +319,81 @@
     )
     kv, where, _ = lax.optimization_barrier((kv, where, qg[0]))
     qg = [qg[0]] + [swap(qg[j], j) for j in range(1, group)]
+
+    chain = needs[-1]
+    rest = group - chain
+    own_sizes = [rest, chain] if rest else [chain]
     *held, counted = call(
-        functools.partial(gather_kernel, group, needs),
-        [shape((n, rows + PAD, 2 * HEAD_DIM), BF16) for n in [group] + [n for n in needs if n < group]]
+        functools.partial(gather_kernel, group),
+        [shape((n, rows + PAD, 2 * HEAD_DIM), BF16) for n in own_sizes]
         + [shape((8, HEAD_DIM), F32)],
         [r],
         kv,
-        vmem=4 << 20,
-    )
-    parts = iter(held[1:])
-    halo = [
-        shift(held[0] if need == group else next(parts), group * (k + 1), counts_ride)
-        for k, need in enumerate(needs)
-    ]
+        scratch=[vmem((group, rows + PAD, 2 * HEAD_DIM), BF16)],
+        vmem=4 << 20,
+    )
+    parts, sizes, links = list(held), list(own_sizes), []
+    passed = held[-1]
+    for k, need in enumerate(needs):
+        passed = shift(passed, group, counts_ride)
+        before = [passed]
+        if need > chain:
+            before = [shift(held[0], group * (k + 1), False), passed]
+        parts, sizes = before + parts, [need - chain] * (need > chain) + [chain] + sizes
+        links = [len(before) - 1] + [i + len(before) for i in links]
     if counts_ride:
-        others = shift(counted, -group, True)
+        parts[links[-1]], late = lax.optimization_barrier((parts[links[-1]], counted))
+        others = shift(late, -group, True)
     else:
         summed, by = counted, group
         while by < count:
             summed = summed + swap(summed, by)
             by *= 2
         others = summed - counted
+
+    sums = (blocks * rows, HEAD_DIM)
+    stack = (group, rows, 2 * width)
+    halo_sizes = sizes[: -len(own_sizes)]
     results = call(
-        functools.partial(attention_kernel, group, needs, heads, float(count * rows), counts_ride),
+        functools.partial(
+            attention_kernel, group, sizes, links, heads, float(count * rows), counts_ride
+        ),
         [shape((rows, 2 * width), BF16)] * group
         + [shape((group * rows, 2 * HEAD_DIM), F32)]
-        + [shape((n * rows, 2 * HEAD_DIM), BF16) for n in needs],
+        + [
+            shape((n * rows, 2 * HEAD_DIM), F32 if i in links[1:] else BF16)
+            for i, n in enumerate(halo_sizes)
+        ],
         [where],
-        [counted, others, held[0], *halo, *qg],
+        [counted, others, *parts, *qg],
         scratch=[
-            vmem((blocks * rows, HEAD_DIM), BF16),
-            vmem((blocks * rows, HEAD_DIM), BF16),
-            vmem((HEAD_DIM, blocks * rows), BF16),
-            vmem((HEAD_DIM, blocks * rows), BF16),
-            vmem((blocks * rows, HEAD_DIM), F32),
-            vmem((blocks * rows, HEAD_DIM), F32),
-            vmem((group, rows, 2 * width), BF16),
-            vmem((group, rows, 2 * width), BF16),
+            vmem(sums, F32),
+            vmem(sums, F32),
+            vmem(stack, BF16),
+            vmem(sums, BF16),
+            vmem(sums, BF16),
+            vmem(sums[::-1], BF16),
+            vmem(sums[::-1], BF16),
+            vmem(stack, BF16),
             vmem((HEAD_DIM, HEAD_DIM), F32),
         ],
         flops=12 * group * heads * rows * span * HEAD_DIM,
-        nbytes=4 << 20,
+        nbytes=16 << 20,
         vmem=24 << 20,
     )
-    od, (own, *parts) = results[:group], results[group:]
-    back = [shift(part, -group * (k + 1), False) for k, part in enumerate(parts)]
+    od, (own, *partial) = results[:group], results[group:]
+    passed = shift(partial[links[0]], -group, False)
+    for i in links[1:]:
+        passed = call(relay_kernel, shape(passed.shape, BF16), [], [partial[i], passed], vmem=2 << 20)
+        passed = shift(passed, -group, False)
+    firsts, back = [rest], [passed]
+    for k, i in enumerate(links[::-1]):
+        if needs[k] > chain:
+            firsts.append(0)
+            back.append(shift(partial[i - 1], -group * (k + 1), False))
     od = [od[0]] + [swap(od[j], j) for j in range(1, group)]
     dkv = call(
-        functools.partial(add_kv_kernel, group, needs),
+        functools.partial(add_kv_kernel, group, firsts),
         [shape((rows, 2 * HEAD_DIM), BF16)] * group,
         [r],
         [own, *back],

time: 59.1 us -> 57.6 us (0.975)
  starting transfers between devices: 23.8 us -> 28.8 us
  waiting for transfers between devices: 18.3 us -> 14.7 us
  Pallas kernels: 15.2 us -> 12.3 us
    ppermute x5 -> x7, starting transfers between devices: 8.66 us -> 13.7 us  [shift(): return lax.ppermute(array, AXIS, pairs)]
    ppermute x5 -> x7, waiting for transfers between devices: 13.5 us -> 10 us  [shift(): return lax.ppermute(array, AXIS, pairs)]
    pallas_call x7 -> x8, Pallas kernels: 15.2 us -> 12.3 us  [call(): pl.pallas_call(kernel, out_shape=out_shape, in_specs=[pl.BlockSpec(memory...]
  transfers between devices with their start and end apart: 17 -> 19, of which waited for: 7 -> 9; matrix products, arithmetic and copies ran while one was open for 0% -> 0% of each run, Pallas kernels for 4% -> 4%
where the time goes in v3:
time: 57.6 us; the launch traced here: 57.3 us
  starting transfers between devices  28.8 us (50%)
  waiting for transfers between devices  14.7 us (26%)
  Pallas kernels  12.3 us (21%)
  between operations  0.75 us (1%)
  local copies, waits for them, and re-layouts  0.73 us (1%)
    ppermute x12, starting transfers between devices, swap(): return lax.ppermute(array, AXIS, [(i, i ^ by) for i in range(count)])  15.1 us
    ppermute x7, starting transfers between devices, shift(): return lax.ppermute(array, AXIS, pairs)  13.7 us
    pallas_call x8, Pallas kernels, call(): pl.pallas_call(kernel, out_shape=out_shape, in_specs=[pl.BlockSpec(memory...  12.3 us
    ppermute x7, waiting for transfers between devices, shift(): return lax.ppermute(array, AXIS, pairs)  10 us
    ppermute x12, waiting for transfers between devices, swap(): return lax.ppermute(array, AXIS, [(i, i ^ by) for i in range(count)])  4.64 us
  transfers between devices with their start and end apart: 19, of which 9 were waited for; matrix products, arithmetic and copies ran while one was open for 0% of the time, Pallas kernels for 4%

profile of v3, /device:TPU:0, one launch (start us, length us, event | category | flops | bytes accessed | tf_op | source)
XLA Modules:
  0.0 57.3 jit_solution(1673137296836059091)
XLA Ops:
  0.6 1.0 %shard_map.102 = (bf16[144,256]{1,0:T(8,128)(2,1)S(1)}, bf16[144,256]{1,0:T(8,128)(2,1)S(1)}, bf16[144,256]{1,0:T(8,128)(2,1)S(1)}, bf16[144,256]{1,0:T(8,128)(2,1)S(1)}) custom-call(s32[1]{0:T(128)} %bitcast.r_ref, bf16[128,512]{1,0:T(8,128)(2,1)} %key_ref.1, bf16[128,512]{1,0:T(8,128)(2,1)} %value_ref.1, s32[1,128]{1,0:T(1,128)} %bitcast.4, s32[1,128]{1,0:T(1,128)} %bitcast.5), custom_call_target="tpu_custom_call" | custom-call | tf_op jit(solution)/shard_map/pallas_call | solution.py:36
  1.6 3.0 %collective-permute-start = (bf16[144,256]{1,0:T(8,128)(2,1)S(1)}, bf16[144,256]{1,0:T(8,128)(2,1)S(1)}, u32[]{:S(2)}, u32[]{:S(2)}) collective-permute-start(bf16[144,256]{1,0:T(8,128)(2,1)S(1)} %get-tuple-element.39), channel_id=1, source_target_pairs={{0,2},{2,0},{4,6},{6,4},{8,10},{10,8},{12,14},{14,12},{16,18},{18,... | collective-permute-start | bytes 221192 | tf_op jit(solution)/shard_map/ppermute | solution.py:291
  4.7 1.5 %collective-permute-start.1 = (bf16[144,256]{1,0:T(8,128)(2,1)S(1)}, bf16[144,256]{1,0:T(8,128)(2,1)S(1)}, u32[]{:S(2)}, u32[]{:S(2)}) collective-permute-start(bf16[144,256]{1,0:T(8,128)(2,1)S(1)} %get-tuple-element.40), channel_id=1, source_target_pairs={{0,4},{2,6},{4,0},{6,2},{8,12},{10,14},{12,8},{14,10},{16,20},{18,... | collective-permute-start | bytes 221192 | tf_op jit(solution)/shard_map/ppermute | solution.py:291
  6.2 0.7 %copy-done = s32[16]{0:T(128)S(1)} copy-done((s32[16]{0:T(128)S(1)}, s32[16]{0:T(128)}, u32[]{:S(2)}) %copy-start) | copy-done | bytes 88
  6.9 1.4 %shard_map.103 = (bf16[128,1024]{1,0:T(8,128)(2,1)S(1)}, bf16[128,1024]{1,0:T(8,128)(2,1)S(1)}, bf16[128,1024]{1,0:T(8,128)(2,1)S(1)}, bf16[128,1024]{1,0:T(8,128)(2,1)S(1)}) custom-call(s32[1]{0:T(128)} %bitcast.r_ref, bf16[128,2048]{1,0:T(8,128)(2,1)} %query_ref.1, bf16[128,2048]{1,0:T(8,128)(2,1)} %grad_ref.1), custom_call_target="tpu_custom_call" | custom-call | tf_op jit(solution)/shard_map/pallas_call | solution.py:36
  8.4 0.6 %collective-permute-done.1.refs_2_ = bf16[144,256]{1,0:T(8,128)(2,1)S(1)} collective-permute-done((bf16[144,256]{1,0:T(8,128)(2,1)S(1)}, bf16[144,256]{1,0:T(8,128)(2,1)S(1)}, u32[]{:S(2)}, u32[]{:S(2)}) %collective-permute-start.1) | collective-permute-done | bytes 73760 | tf_op jit(solution)/shard_map/ppermute | solution.py:291
  9.0 2.4 %collective-permute-done.2.refs_3_ = bf16[144,256]{1,0:T(8,128)(2,1)S(1)} collective-permute-done((bf16[144,256]{1,0:T(8,128)(2,1)S(1)}, bf16[144,256]{1,0:T(8,128)(2,1)S(1)}, u32[]{:S(2)}, u32[]{:S(2)}) %collective-permute-start.2) | collective-permute-done | bytes 73760 | tf_op jit(solution)/shard_map/ppermute | solution.py:291
  11.5 1.6 %collective-permute-start.3 = (bf16[2,144,256]{2,1,0:T(8,128)(2,1)S(1)}, bf16[2,144,256]{2,1,0:T(8,128)(2,1)S(1)}, u32[]{:S(2)}, u32[]{:S(2)}) collective-permute-start(bf16[2,144,256]{2,1,0:T(8,128)(2,1)S(1)} %get-tuple-element.49.refs_4_), channel_id=1, source_target_pairs={{0,8},{2,10},{4,12},{6,14},{8,16},{10,18},{12,20},{14,22},{16,24},... | collective-permute-start | bytes 442376 | tf_op jit(solution)/shard_map/ppermute | solution.py:295
  13.1 0.5 collective-permute-start.7
  13.6 0.5 collective-permute-start.8
  14.2 2.4 %collective-permute-start.9 = (bf16[128,1024]{1,0:T(8,128)(2,1)S(1)}, bf16[128,1024]{1,0:T(8,128)(2,1)S(1)}, u32[]{:S(2)}, u32[]{:S(2)}) collective-permute-start(bf16[128,1024]{1,0:T(8,128)(2,1)S(1)} %get-tuple-element.55), channel_id=1, source_target_pairs={{0,6},{2,4},{4,2},{6,0},{8,14},{10,12},{12,10},{14,8},{16,22},{18,... | collective-permute-start | bytes 786440 | tf_op jit(solution)/shard_map/ppermute | solution.py:291
  16.6 3.5 %collective-permute-start.6 = (bf16[2,144,256]{2,1,0:T(8,128)(2,1)S(1)}, bf16[2,144,256]{2,1,0:T(8,128)(2,1)S(1)}, u32[]{:S(2)}, u32[]{:S(2)}) collective-permute-start(bf16[2,144,256]{2,1,0:T(8,128)(2,1)S(1)} %get-tuple-element.51.refs_3_), channel_id=1, source_target_pairs={{0,8},{2,10},{4,12},{6,14},{8,16},{10,18},{12,20},{14,22},{16,24},... | collective-permute-start | bytes 442376 | tf_op jit(solution)/shard_map/ppermute | solution.py:295
  20.1 1.6 %collective-permute-start.5 = (bf16[2,144,256]{2,1,0:T(8,128)(2,1)S(1)}, bf16[2,144,256]{2,1,0:T(8,128)(2,1)S(1)}, u32[]{:S(2)}, u32[]{:S(2)}) collective-permute-start(bf16[2,144,256]{2,1,0:T(8,128)(2,1)S(1)} %collective-permute-done.3.refs_2_), channel_id=1, source_target_pairs={{0,8},{2,10},{4,12},{6,14},{8,16},{10,18},{12,20},{14,22},{16,24},... | collective-permute-start | bytes 442376 | tf_op jit(solution)/shard_map/ppermute | solution.py:295
  21.7 1.0 %collective-permute-done.6.refs_1_ = bf16[2,144,256]{2,1,0:T(8,128)(2,1)S(1)} collective-permute-done((bf16[2,144,256]{2,1,0:T(8,128)(2,1)S(1)}, bf16[2,144,256]{2,1,0:T(8,128)(2,1)S(1)}, u32[]{:S(2)}, u32[]{:S(2)}) %collective-permute-start.6) | collective-permute-done | bytes 147488 | tf_op jit(solution)/shard_map/ppermute | solution.py:295
  22.8 3.1 %collective-permute-start.4 = (f32[8,128]{1,0:T(8,128)S(1)}, f32[8,128]{1,0:T(8,128)S(1)}, u32[]{:S(2)}, u32[]{:S(2)}) collective-permute-start(f32[8,128]{1,0:T(8,128)S(1)} %get-tuple-element.50.count_ref), channel_id=1, source_target_pairs={{0,24},{2,26},{4,28},{6,30},{8,0},{10,2},{12,4},{14,6},{16,8},{18,... | collective-permute-start | bytes 12296 | tf_op jit(solution)/shard_map/ppermute | solution.py:295
  25.9 1.3 %collective-permute-done.4.other_ref = f32[8,128]{1,0:T(8,128)S(1)} collective-permute-done((f32[8,128]{1,0:T(8,128)S(1)}, f32[8,128]{1,0:T(8,128)S(1)}, u32[]{:S(2)}, u32[]{:S(2)}) %collective-permute-start.4) | collective-permute-done | bytes 4128 | tf_op jit(solution)/shard_map/ppermute | solution.py:295
  27.2 7.9 %shard_map.105 = (bf16[128,1024]{1,0:T(8,128)(2,1)S(1)}, bf16[128,1024]{1,0:T(8,128)(2,1)S(1)}, bf16[128,1024]{1,0:T(8,128)(2,1)S(1)}, bf16[128,1024]{1,0:T(8,12...) custom-call(s32[6]{0:T(128)S(1)} %pad_add_fusion.where_ref, ...), custom_call_target="tpu_custom_call" | custom-call | flops 2818572288 | bytes 16777216 | tf_op jit(solution)/shard_map/pallas_call | solution.py:36
  35.2 1.3 %collective-permute-start.13 = (bf16[256,256]{1,0:T(8,128)(2,1)S(1)}, bf16[256,256]{1,0:T(8,128)(2,1)S(1)}, u32[]{:S(2)}, u32[]{:S(2)}) collective-permute-start(bf16[256,256]{1,0:T(8,128)(2,1)S(1)} %get-tuple-element.64), channel_id=1, source_target_pairs={{8,0},{10,2},{12,4},{14,6},{16,8},{18,10},{20,12},{22,14},{24,16},... | collective-permute-start | bytes 393224 | tf_op jit(solution)/shard_map/ppermute | solution.py:295
  36.5 0.6 %collective-permute-start.10 = (bf16[128,1024]{1,0:T(8,128)(2,1)S(1)}, bf16[128,1024]{1,0:T(8,128)(2,1)S(1)}, u32[]{:S(2)}, u32[]{:S(2)}) collective-permute-start(bf16[128,1024]{1,0:T(8,128)(2,1)S(1)} %get-tuple-element.57), channel_id=1, source_target_pairs={{0,2},{2,0},{4,6},{6,4},{8,10},{10,8},{12,14},{14,12},{16,18},{18,... | collective-permute-start | bytes 786440 | tf_op jit(solution)/shard_map/ppermute | solution.py:291
  37.1 0.5 collective-permute-start.11
  37.5 2.5 %collective-permute-start.12 = (bf16[128,1024]{1,0:T(8,128)(2,1)S(1)}, bf16[128,1024]{1,0:T(8,128)(2,1)S(1)}, u32[]{:S(2)}, u32[]{:S(2)}) collective-permute-start(bf16[128,1024]{1,0:T(8,128)(2,1)S(1)} %get-tuple-element.59), channel_id=1, source_target_pairs={{0,6},{2,4},{4,2},{6,0},{8,14},{10,12},{12,10},{14,8},{16,22},{18,... | collective-permute-start | bytes 786440 | tf_op jit(solution)/shard_map/ppermute | solution.py:291
  40.0 1.3 %collective-permute-start.15 = (bf16[256,256]{1,0:T(8,128)(2,1)S(1)}, bf16[256,256]{1,0:T(8,128)(2,1)S(1)}, u32[]{:S(2)}, u32[]{:S(2)}) collective-permute-start(bf16[256,256]{1,0:T(8,128)(2,1)S(1)} %get-tuple-element.65), channel_id=1, source_target_pairs={{8,0},{10,2},{12,4},{14,6},{16,8},{18,10},{20,12},{22,14},{24,16},... | collective-permute-start | bytes 393224 | tf_op jit(solution)/shard_map/ppermute | solution.py:295
  41.3 2.1 %collective-permute-done.13.got_ref = bf16[256,256]{1,0:T(8,128)(2,1)S(1)} collective-permute-done((bf16[256,256]{1,0:T(8,128)(2,1)S(1)}, bf16[256,256]{1,0:T(8,128)(2,1)S(1)}, u32[]{:S(2)}, u32[]{:S(2)}) %collective-permute-start.13) | collective-permute-done | bytes 131104 | tf_op jit(solution)/shard_map/ppermute | solution.py:295
  43.4 1.3 %collective-permute-start.14 = (bf16[256,256]{1,0:T(8,128)(2,1)S(1)}, bf16[256,256]{1,0:T(8,128)(2,1)S(1)}, u32[]{:S(2)}, u32[]{:S(2)}) collective-permute-start(bf16[256,256]{1,0:T(8,128)(2,1)S(1)} %shard_map.107), channel_id=1, source_target_pairs={{8,0},{10,2},{12,4},{14,6},{16,8},{18,10},{20,12},{22,14},{24,16},... | collective-permute-start | bytes 393224 | tf_op jit(solution)/shard_map/ppermute | solution.py:295
  44.7 2.8 %collective-permute-done.15.refs_1_ = bf16[256,256]{1,0:T(8,128)(2,1)S(1)} collective-permute-done((bf16[256,256]{1,0:T(8,128)(2,1)S(1)}, bf16[256,256]{1,0:T(8,128)(2,1)S(1)}, u32[]{:S(2)}, u32[]{:S(2)}) %collective-permute-start.15) | collective-permute-done | bytes 131104 | tf_op jit(solution)/shard_map/ppermute | solution.py:295
  47.5 2.8 %collective-permute-done.14.refs_0_ = bf16[256,256]{1,0:T(8,128)(2,1)S(1)} collective-permute-done((bf16[256,256]{1,0:T(8,128)(2,1)S(1)}, bf16[256,256]{1,0:T(8,128)(2,1)S(1)}, u32[]{:S(2)}, u32[]{:S(2)}) %collective-permute-start.14) | collective-permute-done | bytes 131104 | tf_op jit(solution)/shard_map/ppermute | solution.py:295
  50.4 0.7 %collective-permute-start.16 = (bf16[128,256]{1,0:T(8,128)(2,1)S(1)}, bf16[128,256]{1,0:T(8,128)(2,1)S(1)}, u32[]{:S(2)}, u32[]{:S(2)}) collective-permute-start(bf16[128,256]{1,0:T(8,128)(2,1)S(1)} %get-tuple-element.67), channel_id=1, source_target_pairs={{0,2},{2,0},{4,6},{6,4},{8,10},{10,8},{12,14},{14,12},{16,18},{18,... | collective-permute-start | bytes 196616 | tf_op jit(solution)/shard_map/ppermute | solution.py:291
  51.0 0.4 collective-permute-start.17
  51.4 2.5 %collective-permute-start.18 = (bf16[128,256]{1,0:T(8,128)(2,1)S(1)}, bf16[128,256]{1,0:T(8,128)(2,1)S(1)}, u32[]{:S(2)}, u32[]{:S(2)}) collective-permute-start(bf16[128,256]{1,0:T(8,128)(2,1)S(1)} %get-tuple-element.69), channel_id=1, source_target_pairs={{0,6},{2,4},{4,2},{6,0},{8,14},{10,12},{12,10},{14,8},{16,22},{18,... | collective-permute-start | bytes 196616 | tf_op jit(solution)/shard_map/ppermute | solution.py:291
  53.9 1.1 %shard_map.106 = (bf16[128,2048]{1,0:T(8,128)(2,1)}, bf16[128,2048]{1,0:T(8,128)(2,1)}) custom-call(s32[1]{0:T(128)} %bitcast.r_ref, bf16[128,1024]{1,0:T(8,128)(2,1)S(1)} %get-tuple-element.56.refs_0_, bf16[128,1024]{1,0:T(8,128)(2,1)S(1)} %collective-permute-done.10.refs_1_, bf16[128,1024]{1,0:T(8,128)(2,1)S(1)} %collective-permute-done.11.refs_2_, ...), custom_call_target="tpu_custom_call" | custom-call | tf_op jit(solution)/shard_map/pallas_call | solution.py:36
  55.3 1.3 %collective-permute-done.18.refs_3_ = bf16[128,256]{1,0:T(8,128)(2,1)S(1)} collective-permute-done((bf16[128,256]{1,0:T(8,128)(2,1)S(1)}, bf16[128,256]{1,0:T(8,128)(2,1)S(1)}, u32[]{:S(2)}, u32[]{:S(2)}) %collective-permute-start.18) | collective-permute-done | bytes 65568 | tf_op jit(solution)/shard_map/ppermute | solution.py:291
  56.6 0.7 %shard_map.109 = (bf16[128,512]{1,0:T(8,128)(2,1)}, bf16[128,512]{1,0:T(8,128)(2,1)}) custom-call(s32[1]{0:T(128)} %bitcast.r_ref, bf16[128,256]{1,0:T(8,128)(2,1)S(1)} %get-tuple-element.66.refs_0_, bf16[128,256]{1,0:T(8,128)(2,1)S(1)} %collective-permute-done.16.refs_1_, bf16[128,256]{1,0:T(8,128)(2,1)S(1)} %collective-permute-done.17.refs_2_, ...), custom_call_target="tpu_custom_call" | custom-call | tf_op jit(solution)/shard_map/pallas_call | solution.py:36
  (18 shorter events, 0.7 us)
Async XLA Ops:
  1.6 6.7 %collective-permute-start = (bf16[144,256]{1,0:T(8,128)(2,1)S(1)}, bf16[144,256]{1,0:T(8,128)(2,1)S(1)}, u32[]{:S(2)}, u32[]{:S(2)}) collective-permute-start(bf16[144,256]{1,0:T(8,128)(2,1)S(1)} %get-tuple-element.39), channel_id=1, source_target_pairs={{0,2},{2,0},{4,6},{6,4},{8,10},{10,8},{12,14},{14,12},{16,18},{18,... | collective-permute-start | bytes 221192 | tf_op jit(solution)/shard_map/ppermute | solution.py:291
  4.7 4.4 %collective-permute-start.1 = (bf16[144,256]{1,0:T(8,128)(2,1)S(1)}, bf16[144,256]{1,0:T(8,128)(2,1)S(1)}, u32[]{:S(2)}, u32[]{:S(2)}) collective-permute-start(bf16[144,256]{1,0:T(8,128)(2,1)S(1)} %get-tuple-element.40), channel_id=1, source_target_pairs={{0,4},{2,6},{4,0},{6,2},{8,12},{10,14},{12,8},{14,10},{16,20},{18,... | collective-permute-start | bytes 221192 | tf_op jit(solution)/shard_map/ppermute | solution.py:291
  6.2 5.3 %collective-permute-start.2 = (bf16[144,256]{1,0:T(8,128)(2,1)S(1)}, bf16[144,256]{1,0:T(8,128)(2,1)S(1)}, u32[]{:S(2)}, u32[]{:S(2)}) collective-permute-start(bf16[144,256]{1,0:T(8,128)(2,1)S(1)} %get-tuple-element.41), channel_id=1, source_target_pairs={{0,6},{2,4},{4,2},{6,0},{8,14},{10,12},{12,10},{14,8},{16,22},{18,... | collective-permute-start | bytes 221192 | tf_op jit(solution)/shard_map/ppermute | solution.py:291
  6.2 0.7 %copy-start = (s32[16]{0:T(128)S(1)}, s32[16]{0:T(128)}, u32[]{:S(2)}) copy-start(s32[16]{0:T(128)} %param.13) | copy-start | bytes 196
  11.5 8.6 %collective-permute-start.3 = (bf16[2,144,256]{2,1,0:T(8,128)(2,1)S(1)}, bf16[2,144,256]{2,1,0:T(8,128)(2,1)S(1)}, u32[]{:S(2)}, u32[]{:S(2)}) collective-permute-start(bf16[2,144,256]{2,1,0:T(8,128)(2,1)S(1)} %get-tuple-element.49.refs_4_), channel_id=1, source_target_pairs={{0,8},{2,10},{4,12},{6,14},{8,16},{10,18},{12,20},{14,22},{16,24},... | collective-permute-start | bytes 442376 | tf_op jit(solution)/shard_map/ppermute | solution.py:295
  13.1 14.1 %collective-permute-start.7 = (bf16[128,1024]{1,0:T(8,128)(2,1)S(1)}, bf16[128,1024]{1,0:T(8,128)(2,1)S(1)}, u32[]{:S(2)}, u32[]{:S(2)}) collective-permute-start(bf16[128,1024]{1,0:T(8,128)(2,1)S(1)} %get-tuple-element.53), channel_id=1, source_target_pairs={{0,2},{2,0},{4,6},{6,4},{8,10},{10,8},{12,14},{14,12},{16,18},{18,... | collective-permute-start | bytes 786440 | tf_op jit(solution)/shard_map/ppermute | solution.py:291
  13.6 13.6 %collective-permute-start.8 = (bf16[128,1024]{1,0:T(8,128)(2,1)S(1)}, bf16[128,1024]{1,0:T(8,128)(2,1)S(1)}, u32[]{:S(2)}, u32[]{:S(2)}) collective-permute-start(bf16[128,1024]{1,0:T(8,128)(2,1)S(1)} %get-tuple-element.54), channel_id=1, source_target_pairs={{0,4},{2,6},{4,0},{6,2},{8,12},{10,14},{12,8},{14,10},{16,20},{18,... | collective-permute-start | bytes 786440 | tf_op jit(solution)/shard_map/ppermute | solution.py:291
  14.2 13.0 %collective-permute-start.9 = (bf16[128,1024]{1,0:T(8,128)(2,1)S(1)}, bf16[128,1024]{1,0:T(8,128)(2,1)S(1)}, u32[]{:S(2)}, u32[]{:S(2)}) collective-permute-start(bf16[128,1024]{1,0:T(8,128)(2,1)S(1)} %get-tuple-element.55), channel_id=1, source_target_pairs={{0,6},{2,4},{4,2},{6,0},{8,14},{10,12},{12,10},{14,8},{16,22},{18,... | collective-permute-start | bytes 786440 | tf_op jit(solution)/shard_map/ppermute | solution.py:291
  16.6 6.2 %collective-permute-start.6 = (bf16[2,144,256]{2,1,0:T(8,128)(2,1)S(1)}, bf16[2,144,256]{2,1,0:T(8,128)(2,1)S(1)}, u32[]{:S(2)}, u32[]{:S(2)}) collective-permute-start(bf16[2,144,256]{2,1,0:T(8,128)(2,1)S(1)} %get-tuple-element.51.refs_3_), channel_id=1, source_target_pairs={{0,8},{2,10},{4,12},{6,14},{8,16},{10,18},{12,20},{14,22},{16,24},... | collective-permute-start | bytes 442376 | tf_op jit(solution)/shard_map/ppermute | solution.py:295
  20.1 7.1 %collective-permute-start.5 = (bf16[2,144,256]{2,1,0:T(8,128)(2,1)S(1)}, bf16[2,144,256]{2,1,0:T(8,128)(2,1)S(1)}, u32[]{:S(2)}, u32[]{:S(2)}) collective-permute-start(bf16[2,144,256]{2,1,0:T(8,128)(2,1)S(1)} %collective-permute-done.3.refs_2_), channel_id=1, source_target_pairs={{0,8},{2,10},{4,12},{6,14},{8,16},{10,18},{12,20},{14,22},{16,24},... | collective-permute-start | bytes 442376 | tf_op jit(solution)/shard_map/ppermute | solution.py:295
  22.8 4.4 %collective-permute-start.4 = (f32[8,128]{1,0:T(8,128)S(1)}, f32[8,128]{1,0:T(8,128)S(1)}, u32[]{:S(2)}, u32[]{:S(2)}) collective-permute-start(f32[8,128]{1,0:T(8,128)S(1)} %get-tuple-element.50.count_ref), channel_id=1, source_target_pairs={{0,24},{2,26},{4,28},{6,30},{8,0},{10,2},{12,4},{14,6},{16,8},{18,... | collective-permute-start | bytes 12296 | tf_op jit(solution)/shard_map/ppermute | solution.py:295
  35.2 8.2 %collective-permute-start.13 = (bf16[256,256]{1,0:T(8,128)(2,1)S(1)}, bf16[256,256]{1,0:T(8,128)(2,1)S(1)}, u32[]{:S(2)}, u32[]{:S(2)}) collective-permute-start(bf16[256,256]{1,0:T(8,128)(2,1)S(1)} %get-tuple-element.64), channel_id=1, source_target_pairs={{8,0},{10,2},{12,4},{14,6},{16,8},{18,10},{20,12},{22,14},{24,16},... | collective-permute-start | bytes 393224 | tf_op jit(solution)/shard_map/ppermute | solution.py:295
  36.5 14.9 %collective-permute-start.10 = (bf16[128,1024]{1,0:T(8,128)(2,1)S(1)}, bf16[128,1024]{1,0:T(8,128)(2,1)S(1)}, u32[]{:S(2)}, u32[]{:S(2)}) collective-permute-start(bf16[128,1024]{1,0:T(8,128)(2,1)S(1)} %get-tuple-element.57), channel_id=1, source_target_pairs={{0,2},{2,0},{4,6},{6,4},{8,10},{10,8},{12,14},{14,12},{16,18},{18,... | collective-permute-start | bytes 786440 | tf_op jit(solution)/shard_map/ppermute | solution.py:291
  37.1 16.9 %collective-permute-start.11 = (bf16[128,1024]{1,0:T(8,128)(2,1)S(1)}, bf16[128,1024]{1,0:T(8,128)(2,1)S(1)}, u32[]{:S(2)}, u32[]{:S(2)}) collective-permute-start(bf16[128,1024]{1,0:T(8,128)(2,1)S(1)} %get-tuple-element.58), channel_id=1, source_target_pairs={{0,4},{2,6},{4,0},{6,2},{8,12},{10,14},{12,8},{14,10},{16,20},{18,... | collective-permute-start | bytes 786440 | tf_op jit(solution)/shard_map/ppermute | solution.py:291
  37.5 16.4 %collective-permute-start.12 = (bf16[128,1024]{1,0:T(8,128)(2,1)S(1)}, bf16[128,1024]{1,0:T(8,128)(2,1)S(1)}, u32[]{:S(2)}, u32[]{:S(2)}) collective-permute-start(bf16[128,1024]{1,0:T(8,128)(2,1)S(1)} %get-tuple-element.59), channel_id=1, source_target_pairs={{0,6},{2,4},{4,2},{6,0},{8,14},{10,12},{12,10},{14,8},{16,22},{18,... | collective-permute-start | bytes 786440 | tf_op jit(solution)/shard_map/ppermute | solution.py:291
  40.0 7.5 %collective-permute-start.15 = (bf16[256,256]{1,0:T(8,128)(2,1)S(1)}, bf16[256,256]{1,0:T(8,128)(2,1)S(1)}, u32[]{:S(2)}, u32[]{:S(2)}) collective-permute-start(bf16[256,256]{1,0:T(8,128)(2,1)S(1)} %get-tuple-element.65), channel_id=1, source_target_pairs={{8,0},{10,2},{12,4},{14,6},{16,8},{18,10},{20,12},{22,14},{24,16},... | collective-permute-start | bytes 393224 | tf_op jit(solution)/shard_map/ppermute | solution.py:295
  43.4 6.9 %collective-permute-start.14 = (bf16[256,256]{1,0:T(8,128)(2,1)S(1)}, bf16[256,256]{1,0:T(8,128)(2,1)S(1)}, u32[]{:S(2)}, u32[]{:S(2)}) collective-permute-start(bf16[256,256]{1,0:T(8,128)(2,1)S(1)} %shard_map.107), channel_id=1, source_target_pairs={{8,0},{10,2},{12,4},{14,6},{16,8},{18,10},{20,12},{22,14},{24,16},... | collective-permute-start | bytes 393224 | tf_op jit(solution)/shard_map/ppermute | solution.py:295
  50.4 4.6 %collective-permute-start.16 = (bf16[128,256]{1,0:T(8,128)(2,1)S(1)}, bf16[128,256]{1,0:T(8,128)(2,1)S(1)}, u32[]{:S(2)}, u32[]{:S(2)}) collective-permute-start(bf16[128,256]{1,0:T(8,128)(2,1)S(1)} %get-tuple-element.67), channel_id=1, source_target_pairs={{0,2},{2,0},{4,6},{6,4},{8,10},{10,8},{12,14},{14,12},{16,18},{18,... | collective-permute-start | bytes 196616 | tf_op jit(solution)/shard_map/ppermute | solution.py:291
  51.0 4.3 %collective-permute-start.17 = (bf16[128,256]{1,0:T(8,128)(2,1)S(1)}, bf16[128,256]{1,0:T(8,128)(2,1)S(1)}, u32[]{:S(2)}, u32[]{:S(2)}) collective-permute-start(bf16[128,256]{1,0:T(8,128)(2,1)S(1)} %get-tuple-element.68), channel_id=1, source_target_pairs={{0,4},{2,6},{4,0},{6,2},{8,12},{10,14},{12,8},{14,10},{16,20},{18,... | collective-permute-start | bytes 196616 | tf_op jit(solution)/shard_map/ppermute | solution.py:291
  51.4 5.2 %collective-permute-start.18 = (bf16[128,256]{1,0:T(8,128)(2,1)S(1)}, bf16[128,256]{1,0:T(8,128)(2,1)S(1)}, u32[]{:S(2)}, u32[]{:S(2)}) collective-permute-start(bf16[128,256]{1,0:T(8,128)(2,1)S(1)} %get-tuple-element.69), channel_id=1, source_target_pairs={{0,6},{2,4},{4,2},{6,0},{8,14},{10,12},{12,10},{14,8},{16,22},{18,... | collective-permute-start | bytes 196616 | tf_op jit(solution)/shard_map/ppermute | solution.py:291

commit v4 on v3

--- a/solution.py
+++ b/solution.py
@@ -72,12 +72,12 @@
 def pack_qg_kernel(group, r_ref, query_ref, grad_ref, *refs):
     out_refs, sems = refs[:group], refs[group]
     r = r_ref[0]
-    width = query_ref.shape[1] // group
+    rows, width = query_ref.shape[0], query_ref.shape[1] // group
     copies = []
     for j in range(group):
         cols = block_at(r ^ j, width)
         for i, ref in enumerate((query_ref, grad_ref)):
-            into = out_refs[j].at[:, i * width : (i + 1) * width]
+            into = out_refs[j].at[0:rows, i * width : (i + 1) * width]
             copies.append(pltpu.make_async_copy(ref.at[:, cols], into, sems.at[2 * j + i]))
     for copy in copies:
         copy.start()
@@ -87,7 +87,7 @@
 
 def encode_count(total):
     high = jnp.floor(total * (1.0 / 64.0))
-    return jnp.concatenate([high, total - 64.0 * high], axis=1).astype(BF16)
+    return jnp.concatenate([high, total - 64.0 * high], axis=1)
 
 
 def decode_count(line):
@@ -96,38 +96,53 @@
 
 
 def gather_kernel(group, r_ref, *refs):
-    slots, (parts, count_ref, full) = refs[:group], (refs[group:-2], *refs[-2:])
+    slots, (part, count_ref, full, lines) = refs[:group], refs[group:]
     r = r_ref[0]
-    rows = full.shape[1] - PAD
-    total = jnp.zeros((1, HEAD_DIM), F32)
-    for j in range(group):
-        full[r ^ j] = slots[j][...]
-        total = total + slots[j][rows : rows + 1, HEAD_DIM:].astype(F32)
-    total = jnp.broadcast_to(jnp.sum(total, axis=1, keepdims=True), count_ref.shape)
+    rows = full.shape[1]
+    lines[...] = jnp.zeros_like(lines)
+    for j in range(group):
+        full[r ^ j] = slots[j][0:rows, :]
+        lines[pl.ds(r ^ j, 1), :] = slots[j][rows : rows + 1, :].astype(F32)
+    total = jnp.sum(jnp.sum(lines[:, HEAD_DIM:], axis=0, keepdims=True), axis=1, keepdims=True)
+    total = jnp.broadcast_to(total, count_ref.shape)
     count_ref[...] = total
-    first = 0
-    for part in parts:
-        part[...] = full[first : first + part.shape[0]]
-        first += part.shape[0]
-    parts[-1][0, rows + 8 :, :] = encode_count(total)
+    for s in range(group):
+        part[s * rows : (s + 1) * rows, :] = full[s]
+    tail = jnp.concatenate([lines[...], encode_count(total)], axis=0)
+    part[group * rows :, :] = tail.astype(BF16)
+
+
+def cut_kernel(skip, part_ref, out_ref):
+    rows = HEAD_DIM
+    size = out_ref.shape[0] - PAD
+    out_ref[0:size, :] = part_ref[skip * rows : skip * rows + size, :]
+    tail = part_ref[skip * rows + size :, :].astype(F32)
+    tail = jnp.concatenate([tail[skip : PAD // 2], tail[:skip], tail[PAD // 2 :]], axis=0)
+    out_ref[size:, :] = tail.astype(BF16)
+
+
+def count_kernel(count_ref, near_ref, out_ref):
+    out_ref[...] = count_ref[...] + decode_count(near_ref[near_ref.shape[0] - PAD // 2 :, :])
 
 
 def relay_kernel(part_ref, got_ref, out_ref):
-    out_ref[...] = (part_ref[...] + got_ref[...].astype(F32)).astype(BF16)
+    got = got_ref[0 : part_ref.shape[0], :].astype(F32)
+    out_ref[...] = (part_ref[...] + got).astype(BF16)
 
 
 def attention_kernel(
-    group, sizes, links, heads, token_count, counts_ride, where_ref, count_ref, other_ref, *refs
+    group, sizes, heads, token_count, others, near_count, where_ref, count_ref, *refs
 ):
     shards = range(group)
     hops = sum(sizes) - group
+    other_refs, refs = refs[:others], refs[others:]
     part_refs, refs = refs[: len(sizes)], refs[len(sizes) :]
     qg_refs, refs = refs[:group], refs[group:]
     out_refs, own_out, refs = refs[:group], refs[group], refs[group + 1 :]
     sum_refs, (dkeys, dvalues, od, *refs) = refs[:-9], refs[-9:]
     keys, values, keys_t, values_t, qg, lines = refs
     r = where_ref[0]
-    rows = qg_refs[0].shape[0]
+    rows = lines.shape[0]
     blocks = hops + group
     span = (hops + 1) * rows
     width = heads * HEAD_DIM
@@ -136,31 +151,34 @@
     lowest = jnp.maximum(hops * rows - where_ref[1], 0)
 
     lines[...] = jnp.zeros_like(lines)
-    total = count_ref[...] + other_ref[...]
-    if counts_ride:
-        for i in links:
-            total = total + decode_count(part_refs[i][0, rows + 8 :, :])
+    total = count_ref[...]
+    for ref in other_refs:
+        total = total + ref[...]
+    if near_count:
+        near = part_refs[-2]
+        total = total + decode_count(near[near.shape[0] - PAD // 2 :, :])
     factor = token_count / jnp.maximum(total[0:1, :], 1.0)
-    pieces = [(ref, i) for ref in part_refs for i in range(ref.shape[0])]
-    for kb, (ref, i) in enumerate(pieces):
+    pieces = [(ref, n, i) for ref, n in zip(part_refs, sizes) for i in range(n)]
+    for kb, (ref, n, i) in enumerate(pieces):
         at = slice(kb * rows, (kb + 1) * rows)
-        key, value = ref[i, 0:rows, 0:HEAD_DIM], ref[i, 0:rows, HEAD_DIM:]
+        piece = ref[i * rows : (i + 1) * rows, :]
+        key, value = piece[:, 0:HEAD_DIM], piece[:, HEAD_DIM:]
+        line = ref[n * rows : n * rows + PAD // 2, :].astype(F32)[i : i + 1, :]
         keys[at, :] = key
         values[at, :] = value
         keys_t[:, at] = key.T
         values_t[:, at] = value.T
-        doc = ref[i, rows : rows + 1, 0:HEAD_DIM].astype(F32)
+        doc = line[:, 0:HEAD_DIM]
         if kb < hops:
             doc = jnp.where(kb * rows < lowest, -1.0, doc)
         else:
-            mask = ref[i, rows : rows + 1, HEAD_DIM:].astype(F32)
-            lines[blocks + kb - hops : blocks + kb - hops + 1, :] = mask * factor
+            lines[blocks + kb - hops : blocks + kb - hops + 1, :] = line[:, HEAD_DIM:] * factor
         lines[kb : kb + 1, :] = doc
     columns = lines[...].T
     dkeys[...] = jnp.zeros_like(dkeys)
     dvalues[...] = jnp.zeros_like(dvalues)
     for j in range(group):
-        qg[r ^ j] = qg_refs[j][...]
+        qg[r ^ j] = qg_refs[j][0:rows, :]
 
     lane = lax.broadcasted_iota(jnp.int32, (1, rows), 1)
     pos = lax.broadcasted_iota(jnp.int32, (span, PAIR * rows), 0)
@@ -285,12 +303,12 @@
     where = jnp.concatenate([r, base, lax.dynamic_slice(windows, (r[0] * heads,), (heads,))])
     shape = jax.ShapeDtypeStruct
     vmem = pltpu.VMEM
-    counts_ride = count == 4 * group and len(needs) == 2
+    near_count = count == 4 * group and group > 1
 
     def swap(array, by):
         return lax.ppermute(array, AXIS, [(i, i ^ by) for i in range(count)])
 
-    def shift(array, by, around):
+    def shift(array, by, around=False):
         pairs = [(i, (i + by) % count) for i in range(count) if around or 0 <= i + by < count]
         return lax.ppermute(array, AXIS, pairs)
 
@@ -320,52 +338,60 @@
     kv, where, _ = lax.optimization_barrier((kv, where, qg[0]))
     qg = [qg[0]] + [swap(qg[j], j) for j in range(1, group)]
 
-    chain = needs[-1]
-    rest = group - chain
-    own_sizes = [rest, chain] if rest else [chain]
-    *held, counted = call(
+    held, counted = call(
         functools.partial(gather_kernel, group),
-        [shape((n, rows + PAD, 2 * HEAD_DIM), BF16) for n in own_sizes]
-        + [shape((8, HEAD_DIM), F32)],
+        [shape((group * rows + PAD, 2 * HEAD_DIM), BF16), shape((8, HEAD_DIM), F32)],
         [r],
         kv,
-        scratch=[vmem((group, rows + PAD, 2 * HEAD_DIM), BF16)],
-        vmem=4 << 20,
-    )
-    parts, sizes, links = list(held), list(own_sizes), []
-    passed = held[-1]
+        scratch=[vmem((group, rows, 2 * HEAD_DIM), BF16), vmem((8, 2 * HEAD_DIM), F32)],
+        vmem=4 << 20,
+    )
+    halo, passed, size = [], held, group
     for k, need in enumerate(needs):
-        passed = shift(passed, group, counts_ride)
-        before = [passed]
-        if need > chain:
-            before = [shift(held[0], group * (k + 1), False), passed]
-        parts, sizes = before + parts, [need - chain] * (need > chain) + [chain] + sizes
-        links = [len(before) - 1] + [i + len(before) for i in links]
-    if counts_ride:
-        parts[links[-1]], late = lax.optimization_barrier((parts[links[-1]], counted))
-        others = shift(late, -group, True)
+        if need < size:
+            passed = call(
+                functools.partial(cut_kernel, size - need),
+                shape((need * rows + PAD, 2 * HEAD_DIM), BF16),
+                [],
+                [passed],
+                vmem=2 << 20,
+            )
+        passed, size = shift(passed, group, near_count and k == 0), need
+        halo.append(passed)
+    sizes = needs[::-1] + [group]
+    if near_count:
+        pair = call(count_kernel, shape(counted.shape, F32), [], [counted, halo[0]], vmem=1 << 20)
+        others = [swap(pair, 2 * group)]
     else:
-        summed, by = counted, group
+        others, by = [jnp.zeros_like(counted)], group
         while by < count:
-            summed = summed + swap(summed, by)
+            counted, others = counted + others[0], [swap(counted + others[0], by)]
             by *= 2
-        others = summed - counted
 
     sums = (blocks * rows, HEAD_DIM)
     stack = (group, rows, 2 * width)
-    halo_sizes = sizes[: -len(own_sizes)]
+    chain = needs[-1]
+    joined = len(needs) == 2 and needs[0] > chain
+    pieces, links = [], []
+    for k, need in reversed(list(enumerate(needs))):
+        if need > chain and joined:
+            pieces[-1] = need
+        elif need > chain:
+            pieces.append(need - chain)
+        pieces.append(chain)
+        links.append(len(pieces) - 1)
     results = call(
         functools.partial(
-            attention_kernel, group, sizes, links, heads, float(count * rows), counts_ride
+            attention_kernel, group, sizes, heads, float(count * rows), len(others), near_count
         ),
         [shape((rows, 2 * width), BF16)] * group
         + [shape((group * rows, 2 * HEAD_DIM), F32)]
         + [
             shape((n * rows, 2 * HEAD_DIM), F32 if i in links[1:] else BF16)
-            for i, n in enumerate(halo_sizes)
+            for i, n in enumerate(pieces)
         ],
         [where],
-        [counted, others, *parts, *qg],
+        [counted, *others, *halo[::-1], held, *qg],
         scratch=[
             vmem(sums, F32),
             vmem(sums, F32),
@@ -382,15 +408,22 @@
         vmem=24 << 20,
     )
     od, (own, *partial) = results[:group], results[group:]
-    passed = shift(partial[links[0]], -group, False)
+    firsts, back = [], []
+    passed = shift(partial[links[0]], -group)
+    if joined:
+        firsts.append(-chain)
+        back.append(passed)
     for i in links[1:]:
-        passed = call(relay_kernel, shape(passed.shape, BF16), [], [partial[i], passed], vmem=2 << 20)
-        passed = shift(passed, -group, False)
-    firsts, back = [rest], [passed]
+        passed = call(
+            relay_kernel, shape((chain * rows, 2 * HEAD_DIM), BF16), [], [partial[i], passed], vmem=2 << 20
+        )
+        passed = shift(passed, -group)
+    firsts.append(group - chain)
+    back.append(passed)
     for k, i in enumerate(links[::-1]):
-        if needs[k] > chain:
+        if needs[k] > chain and not joined:
             firsts.append(0)
-            back.append(shift(partial[i - 1], -group * (k + 1), False))
+            back.append(shift(partial[i - 1], -group * (k + 1)))
     od = [od[0]] + [swap(od[j], j) for j in range(1, group)]
     dkv = call(
         functools.partial(add_kv_kernel, group, firsts),

time: 57.6 us -> 57.4 us (level)
  starting transfers between devices: 28.8 us -> 23.6 us
  waiting for transfers between devices: 14.7 us -> 19.5 us
    ppermute x7 -> x4, starting transfers between devices: 13.7 us -> 5.79 us  [shift(): return lax.ppermute(array, AXIS, pairs)]
    ppermute x7 -> x4, waiting for transfers between devices: 10 us -> 12.8 us  [shift(): return lax.ppermute(array, AXIS, pairs)]
    ppermute x12 -> x13, starting transfers between devices: 15.1 us -> 17.8 us  [swap(): return lax.ppermute(array, AXIS, [(i, i ^ by) for i in range(count)])]
    ppermute x12 -> x13, waiting for transfers between devices: 4.64 us -> 6.78 us  [swap(): return lax.ppermute(array, AXIS, [(i, i ^ by) for i in range(count)])]
    pallas_call x8 -> x10, Pallas kernels: 12.3 us -> 12.4 us  [call(): pl.pallas_call(kernel, out_shape=out_shape, in_specs=[pl.BlockSpec(memory...]
  transfers between devices with their start and end apart: 19 -> 17, of which waited for: 9 -> 9; matrix products, arithmetic and copies ran while one was open for 0% -> 0% of each run, Pallas kernels for 4% -> 4%
where the time goes in v4:
time: 57.4 us; the launch traced here: 57.1 us
  starting transfers between devices  23.6 us (41%)
  waiting for transfers between devices  19.5 us (34%)
  Pallas kernels  12.4 us (22%)
  local copies, waits for them, and re-layouts  0.73 us (1%)
  between operations  0.73 us (1%)
    ppermute x13, starting transfers between devices, swap(): return lax.ppermute(array, AXIS, [(i, i ^ by) for i in range(count)])  17.8 us
    ppermute x4, waiting for transfers between devices, shift(): return lax.ppermute(array, AXIS, pairs)  12.8 us
    pallas_call x10, Pallas kernels, call(): pl.pallas_call(kernel, out_shape=out_shape, in_specs=[pl.BlockSpec(memory...  12.4 us
    ppermute x13, waiting for transfers between devices, swap(): return lax.ppermute(array, AXIS, [(i, i ^ by) for i in range(count)])  6.78 us
    ppermute x4, starting transfers between devices, shift(): return lax.ppermute(array, AXIS, pairs)  5.79 us
  transfers between devices with their start and end apart: 17, of which 9 were waited for; matrix products, arithmetic and copies ran while one was open for 0% of the time, Pallas kernels for 4%

profile of v4, /device:TPU:0, one launch (start us, length us, event | category | flops | bytes accessed | tf_op | source)
XLA Modules:
  0.0 57.1 jit_solution(17005984669194270304)
XLA Ops:
  0.6 1.0 %shard_map.102 = (bf16[144,256]{1,0:T(8,128)(2,1)S(1)}, bf16[144,256]{1,0:T(8,128)(2,1)S(1)}, bf16[144,256]{1,0:T(8,128)(2,1)S(1)}, bf16[144,256]{1,0:T(8,128)(2,1)S(1)}) custom-call(s32[1]{0:T(128)} %bitcast.r_ref, bf16[128,512]{1,0:T(8,128)(2,1)} %key_ref.1, bf16[128,512]{1,0:T(8,128)(2,1)} %value_ref.1, s32[1,128]{1,0:T(1,128)} %bitcast.4, s32[1,128]{1,0:T(1,128)} %bitcast.5), custom_call_target="tpu_custom_call" | custom-call | tf_op jit(solution)/shard_map/pallas_call | solution.py:36
  1.6 3.0 %collective-permute-start = (bf16[144,256]{1,0:T(8,128)(2,1)S(1)}, bf16[144,256]{1,0:T(8,128)(2,1)S(1)}, u32[]{:S(2)}, u32[]{:S(2)}) collective-permute-start(bf16[144,256]{1,0:T(8,128)(2,1)S(1)} %get-tuple-element.35), channel_id=1, source_target_pairs={{0,2},{2,0},{4,6},{6,4},{8,10},{10,8},{12,14},{14,12},{16,18},{18,... | collective-permute-start | bytes 221192 | tf_op jit(solution)/shard_map/ppermute | solution.py:309
  4.7 1.5 %collective-permute-start.1 = (bf16[144,256]{1,0:T(8,128)(2,1)S(1)}, bf16[144,256]{1,0:T(8,128)(2,1)S(1)}, u32[]{:S(2)}, u32[]{:S(2)}) collective-permute-start(bf16[144,256]{1,0:T(8,128)(2,1)S(1)} %get-tuple-element.36), channel_id=1, source_target_pairs={{0,4},{2,6},{4,0},{6,2},{8,12},{10,14},{12,8},{14,10},{16,20},{18,... | collective-permute-start | bytes 221192 | tf_op jit(solution)/shard_map/ppermute | solution.py:309
  6.2 0.7 %copy-done = s32[16]{0:T(128)S(1)} copy-done((s32[16]{0:T(128)S(1)}, s32[16]{0:T(128)}, u32[]{:S(2)}) %copy-start) | copy-done | bytes 88
  6.9 1.4 %shard_map.103 = (bf16[128,1024]{1,0:T(8,128)(2,1)S(1)}, bf16[128,1024]{1,0:T(8,128)(2,1)S(1)}, bf16[128,1024]{1,0:T(8,128)(2,1)S(1)}, bf16[128,1024]{1,0:T(8,128)(2,1)S(1)}) custom-call(s32[1]{0:T(128)} %bitcast.r_ref, bf16[128,2048]{1,0:T(8,128)(2,1)} %query_ref.1, bf16[128,2048]{1,0:T(8,128)(2,1)} %grad_ref.1), custom_call_target="tpu_custom_call" | custom-call | tf_op jit(solution)/shard_map/pallas_call | solution.py:36
  8.4 0.6 %collective-permute-done.1.refs_2_ = bf16[144,256]{1,0:T(8,128)(2,1)S(1)} collective-permute-done((bf16[144,256]{1,0:T(8,128)(2,1)S(1)}, bf16[144,256]{1,0:T(8,128)(2,1)S(1)}, u32[]{:S(2)}, u32[]{:S(2)}) %collective-permute-start.1) | collective-permute-done | bytes 73760 | tf_op jit(solution)/shard_map/ppermute | solution.py:309
  9.0 2.4 %collective-permute-done.2.refs_3_ = bf16[144,256]{1,0:T(8,128)(2,1)S(1)} collective-permute-done((bf16[144,256]{1,0:T(8,128)(2,1)S(1)}, bf16[144,256]{1,0:T(8,128)(2,1)S(1)}, u32[]{:S(2)}, u32[]{:S(2)}) %collective-permute-start.2) | collective-permute-done | bytes 73760 | tf_op jit(solution)/shard_map/ppermute | solution.py:309
  11.4 0.1 shard_map.104
  11.5 1.6 %collective-permute-start.3 = (bf16[528,256]{1,0:T(8,128)(2,1)S(1)}, bf16[528,256]{1,0:T(8,128)(2,1)S(1)}, u32[]{:S(2)}, u32[]{:S(2)}) collective-permute-start(bf16[528,256]{1,0:T(8,128)(2,1)S(1)} %get-tuple-element.45.refs_3_), channel_id=1, source_target_pairs={{0,8},{2,10},{4,12},{6,14},{8,16},{10,18},{12,20},{14,22},{16,24},... | collective-permute-start | bytes 811016 | tf_op jit(solution)/shard_map/ppermute | solution.py:313
  13.1 0.5 collective-permute-start.6
  13.7 0.5 collective-permute-start.7
  14.2 2.4 %collective-permute-start.8 = (bf16[128,1024]{1,0:T(8,128)(2,1)S(1)}, bf16[128,1024]{1,0:T(8,128)(2,1)S(1)}, u32[]{:S(2)}, u32[]{:S(2)}) collective-permute-start(bf16[128,1024]{1,0:T(8,128)(2,1)S(1)} %get-tuple-element.48), channel_id=1, source_target_pairs={{0,6},{2,4},{4,2},{6,0},{8,14},{10,12},{12,10},{14,8},{16,22},{18,... | collective-permute-start | bytes 786440 | tf_op jit(solution)/shard_map/ppermute | solution.py:309
  16.6 3.4 %collective-permute-done.3.near_ref.part_ref.refs_2_ = bf16[528,256]{1,0:T(8,128)(2,1)S(1)} collective-permute-done((bf16[528,256]{1,0:T(8,128)(2,1)S(1)}, bf16[528,256]{1,0:T(8,128)(2,1)S(1)}, u32[]{:S(2)}, u32[]{:S(2)}) %collective-permute-start.3) | collective-permute-done | bytes 270368 | tf_op jit(solution)/shard_map/ppermute | solution.py:313
  20.0 1.6 %collective-permute-start.5 = (bf16[272,256]{1,0:T(8,128)(2,1)S(1)}, bf16[272,256]{1,0:T(8,128)(2,1)S(1)}, u32[]{:S(2)}, u32[]{:S(2)}) collective-permute-start(bf16[272,256]{1,0:T(8,128)(2,1)S(1)} %shard_map.106), channel_id=1, source_target_pairs={{0,8},{2,10},{4,12},{6,14},{8,16},{10,18},{12,20},{14,22},{16,24},... | collective-permute-start | bytes 417800 | tf_op jit(solution)/shard_map/ppermute | solution.py:313
  21.6 2.7 %collective-permute-start.4 = (f32[8,128]{1,0:T(8,128)S(1)}, f32[8,128]{1,0:T(8,128)S(1)}, u32[]{:S(2)}, u32[]{:S(2)}) collective-permute-start(f32[8,128]{1,0:T(8,128)S(1)} %shard_map.105), channel_id=1, source_target_pairs={{0,16},{2,18},{4,20},{6,22},{8,24},{10,26},{12,28},{14,30},{16,0},... | collective-permute-start | bytes 12296 | tf_op jit(solution)/shard_map/ppermute | solution.py:309
  24.3 1.2 %collective-permute-done.7.refs_6_ = bf16[128,1024]{1,0:T(8,128)(2,1)S(1)} collective-permute-done((bf16[128,1024]{1,0:T(8,128)(2,1)S(1)}, bf16[128,1024]{1,0:T(8,128)(2,1)S(1)}, u32[]{:S(2)}, u32[]{:S(2)}) %collective-permute-start.7) | collective-permute-done | bytes 262176 | tf_op jit(solution)/shard_map/ppermute | solution.py:309
  25.5 0.7 %collective-permute-done.4.refs_0_ = f32[8,128]{1,0:T(8,128)S(1)} collective-permute-done((f32[8,128]{1,0:T(8,128)S(1)}, f32[8,128]{1,0:T(8,128)S(1)}, u32[]{:S(2)}, u32[]{:S(2)}) %collective-permute-start.4) | collective-permute-done | bytes 4128 | tf_op jit(solution)/shard_map/ppermute | solution.py:309
  26.2 8.0 %shard_map.107 = (bf16[128,1024]{1,0:T(8,128)(2,1)S(1)}, bf16[128,1024]{1,0:T(8,128)(2,1)S(1)}, bf16[128,1024]{1,0:T(8,128)(2,1)S(1)}, bf16[128,1024]{1,0:T(8,12...) custom-call(s32[6]{0:T(128)S(1)} %pad_add_fusion.where_ref, ...), custom_call_target="tpu_custom_call" | custom-call | flops 2818572288 | bytes 16777216 | tf_op jit(solution)/shard_map/pallas_call | solution.py:36
  34.3 1.3 %collective-permute-start.12 = (bf16[512,256]{1,0:T(8,128)(2,1)S(1)}, bf16[512,256]{1,0:T(8,128)(2,1)S(1)}, u32[]{:S(2)}, u32[]{:S(2)}) collective-permute-start(bf16[512,256]{1,0:T(8,128)(2,1)S(1)} %get-tuple-element.56), channel_id=1, source_target_pairs={{8,0},{10,2},{12,4},{14,6},{16,8},{18,10},{20,12},{22,14},{24,16},... | collective-permute-start | bytes 786440 | tf_op jit(solution)/shard_map/ppermute | solution.py:313
  35.6 1.0 %collective-permute-start.9 = (bf16[128,1024]{1,0:T(8,128)(2,1)S(1)}, bf16[128,1024]{1,0:T(8,128)(2,1)S(1)}, u32[]{:S(2)}, u32[]{:S(2)}) collective-permute-start(bf16[128,1024]{1,0:T(8,128)(2,1)S(1)} %get-tuple-element.50), channel_id=1, source_target_pairs={{0,2},{2,0},{4,6},{6,4},{8,10},{10,8},{12,14},{14,12},{16,18},{18,... | collective-permute-start | bytes 786440 | tf_op jit(solution)/shard_map/ppermute | solution.py:309
  36.6 0.6 %collective-permute-start.10 = (bf16[128,1024]{1,0:T(8,128)(2,1)S(1)}, bf16[128,1024]{1,0:T(8,128)(2,1)S(1)}, u32[]{:S(2)}, u32[]{:S(2)}) collective-permute-start(bf16[128,1024]{1,0:T(8,128)(2,1)S(1)} %get-tuple-element.51), channel_id=1, source_target_pairs={{0,4},{2,6},{4,0},{6,2},{8,12},{10,14},{12,8},{14,10},{16,20},{18,... | collective-permute-start | bytes 786440 | tf_op jit(solution)/shard_map/ppermute | solution.py:309
  37.2 1.9 %collective-permute-start.11 = (bf16[128,1024]{1,0:T(8,128)(2,1)S(1)}, bf16[128,1024]{1,0:T(8,128)(2,1)S(1)}, u32[]{:S(2)}, u32[]{:S(2)}) collective-permute-start(bf16[128,1024]{1,0:T(8,128)(2,1)S(1)} %get-tuple-element.52), channel_id=1, source_target_pairs={{0,6},{2,4},{4,2},{6,0},{8,14},{10,12},{12,10},{14,8},{16,22},{18,... | collective-permute-start | bytes 786440 | tf_op jit(solution)/shard_map/ppermute | solution.py:309
  39.1 3.8 %collective-permute-done.12.got_ref.refs_0_ = bf16[512,256]{1,0:T(8,128)(2,1)S(1)} collective-permute-done((bf16[512,256]{1,0:T(8,128)(2,1)S(1)}, bf16[512,256]{1,0:T(8,128)(2,1)S(1)}, u32[]{:S(2)}, u32[]{:S(2)}) %collective-permute-start.12) | collective-permute-done | bytes 262176 | tf_op jit(solution)/shard_map/ppermute | solution.py:313
  43.0 1.3 %collective-permute-start.13 = (bf16[256,256]{1,0:T(8,128)(2,1)S(1)}, bf16[256,256]{1,0:T(8,128)(2,1)S(1)}, u32[]{:S(2)}, u32[]{:S(2)}) collective-permute-start(bf16[256,256]{1,0:T(8,128)(2,1)S(1)} %shard_map.109), channel_id=1, source_target_pairs={{8,0},{10,2},{12,4},{14,6},{16,8},{18,10},{20,12},{22,14},{24,16},... | collective-permute-start | bytes 393224 | tf_op jit(solution)/shard_map/ppermute | solution.py:313
  44.3 5.6 %collective-permute-done.13.refs_1_ = bf16[256,256]{1,0:T(8,128)(2,1)S(1)} collective-permute-done((bf16[256,256]{1,0:T(8,128)(2,1)S(1)}, bf16[256,256]{1,0:T(8,128)(2,1)S(1)}, u32[]{:S(2)}, u32[]{:S(2)}) %collective-permute-start.13) | collective-permute-done | bytes 131104 | tf_op jit(solution)/shard_map/ppermute | solution.py:313
  49.9 0.6 %collective-permute-start.14 = (bf16[128,256]{1,0:T(8,128)(2,1)S(1)}, bf16[128,256]{1,0:T(8,128)(2,1)S(1)}, u32[]{:S(2)}, u32[]{:S(2)}) collective-permute-start(bf16[128,256]{1,0:T(8,128)(2,1)S(1)} %get-tuple-element.59), channel_id=1, source_target_pairs={{0,2},{2,0},{4,6},{6,4},{8,10},{10,8},{12,14},{14,12},{16,18},{18,... | collective-permute-start | bytes 196616 | tf_op jit(solution)/shard_map/ppermute | solution.py:309
  50.5 0.6 %collective-permute-start.15 = (bf16[128,256]{1,0:T(8,128)(2,1)S(1)}, bf16[128,256]{1,0:T(8,128)(2,1)S(1)}, u32[]{:S(2)}, u32[]{:S(2)}) collective-permute-start(bf16[128,256]{1,0:T(8,128)(2,1)S(1)} %get-tuple-element.60), channel_id=1, source_target_pairs={{0,4},{2,6},{4,0},{6,2},{8,12},{10,14},{12,8},{14,10},{16,20},{18,... | collective-permute-start | bytes 196616 | tf_op jit(solution)/shard_map/ppermute | solution.py:309
  51.2 2.3 %collective-permute-start.16 = (bf16[128,256]{1,0:T(8,128)(2,1)S(1)}, bf16[128,256]{1,0:T(8,128)(2,1)S(1)}, u32[]{:S(2)}, u32[]{:S(2)}) collective-permute-start(bf16[128,256]{1,0:T(8,128)(2,1)S(1)} %get-tuple-element.61), channel_id=1, source_target_pairs={{0,6},{2,4},{4,2},{6,0},{8,14},{10,12},{12,10},{14,8},{16,22},{18,... | collective-permute-start | bytes 196616 | tf_op jit(solution)/shard_map/ppermute | solution.py:309
  53.5 1.0 %shard_map.108 = (bf16[128,2048]{1,0:T(8,128)(2,1)}, bf16[128,2048]{1,0:T(8,128)(2,1)}) custom-call(s32[1]{0:T(128)} %bitcast.r_ref, bf16[128,1024]{1,0:T(8,128)(2,1)S(1)} %get-tuple-element.49.refs_0_, bf16[128,1024]{1,0:T(8,128)(2,1)S(1)} %collective-permute-done.9.refs_1_, bf16[128,1024]{1,0:T(8,128)(2,1)S(1)} %collective-permute-done.10.refs_2_, ...), custom_call_target="tpu_custom_call" | custom-call | tf_op jit(solution)/shard_map/pallas_call | solution.py:36
  54.5 0.3 collective-permute-done.15.refs_2_
  54.8 1.5 %collective-permute-done.16.refs_3_ = bf16[128,256]{1,0:T(8,128)(2,1)S(1)} collective-permute-done((bf16[128,256]{1,0:T(8,128)(2,1)S(1)}, bf16[128,256]{1,0:T(8,128)(2,1)S(1)}, u32[]{:S(2)}, u32[]{:S(2)}) %collective-permute-start.16) | collective-permute-done | bytes 65568 | tf_op jit(solution)/shard_map/ppermute | solution.py:309
  56.3 0.7 %shard_map.111 = (bf16[128,512]{1,0:T(8,128)(2,1)}, bf16[128,512]{1,0:T(8,128)(2,1)}) custom-call(s32[1]{0:T(128)} %bitcast.r_ref, bf16[128,256]{1,0:T(8,128)(2,1)S(1)} %get-tuple-element.58.refs_0_, bf16[128,256]{1,0:T(8,128)(2,1)S(1)} %collective-permute-done.14.refs_1_, bf16[128,256]{1,0:T(8,128)(2,1)S(1)} %collective-permute-done.15.refs_2_, ...), custom_call_target="tpu_custom_call" | custom-call | tf_op jit(solution)/shard_map/pallas_call | solution.py:36
  (16 shorter events, 0.3 us)
Async XLA Ops:
  1.6 6.7 %collective-permute-start = (bf16[144,256]{1,0:T(8,128)(2,1)S(1)}, bf16[144,256]{1,0:T(8,128)(2,1)S(1)}, u32[]{:S(2)}, u32[]{:S(2)}) collective-permute-start(bf16[144,256]{1,0:T(8,128)(2,1)S(1)} %get-tuple-element.35), channel_id=1, source_target_pairs={{0,2},{2,0},{4,6},{6,4},{8,10},{10,8},{12,14},{14,12},{16,18},{18,... | collective-permute-start | bytes 221192 | tf_op jit(solution)/shard_map/ppermute | solution.py:309
  4.7 4.4 %collective-permute-start.1 = (bf16[144,256]{1,0:T(8,128)(2,1)S(1)}, bf16[144,256]{1,0:T(8,128)(2,1)S(1)}, u32[]{:S(2)}, u32[]{:S(2)}) collective-permute-start(bf16[144,256]{1,0:T(8,128)(2,1)S(1)} %get-tuple-element.36), channel_id=1, source_target_pairs={{0,4},{2,6},{4,0},{6,2},{8,12},{10,14},{12,8},{14,10},{16,20},{18,... | collective-permute-start | bytes 221192 | tf_op jit(solution)/shard_map/ppermute | solution.py:309
  6.2 5.3 %collective-permute-start.2 = (bf16[144,256]{1,0:T(8,128)(2,1)S(1)}, bf16[144,256]{1,0:T(8,128)(2,1)S(1)}, u32[]{:S(2)}, u32[]{:S(2)}) collective-permute-start(bf16[144,256]{1,0:T(8,128)(2,1)S(1)} %get-tuple-element.37), channel_id=1, source_target_pairs={{0,6},{2,4},{4,2},{6,0},{8,14},{10,12},{12,10},{14,8},{16,22},{18,... | collective-permute-start | bytes 221192 | tf_op jit(solution)/shard_map/ppermute | solution.py:309
  6.2 0.7 %copy-start = (s32[16]{0:T(128)S(1)}, s32[16]{0:T(128)}, u32[]{:S(2)}) copy-start(s32[16]{0:T(128)} %param.13) | copy-start | bytes 196
  11.5 8.4 %collective-permute-start.3 = (bf16[528,256]{1,0:T(8,128)(2,1)S(1)}, bf16[528,256]{1,0:T(8,128)(2,1)S(1)}, u32[]{:S(2)}, u32[]{:S(2)}) collective-permute-start(bf16[528,256]{1,0:T(8,128)(2,1)S(1)} %get-tuple-element.45.refs_3_), channel_id=1, source_target_pairs={{0,8},{2,10},{4,12},{6,14},{8,16},{10,18},{12,20},{14,22},{16,24},... | collective-permute-start | bytes 811016 | tf_op jit(solution)/shard_map/ppermute | solution.py:313
  13.1 11.2 %collective-permute-start.6 = (bf16[128,1024]{1,0:T(8,128)(2,1)S(1)}, bf16[128,1024]{1,0:T(8,128)(2,1)S(1)}, u32[]{:S(2)}, u32[]{:S(2)}) collective-permute-start(bf16[128,1024]{1,0:T(8,128)(2,1)S(1)} %get-tuple-element.46), channel_id=1, source_target_pairs={{0,2},{2,0},{4,6},{6,4},{8,10},{10,8},{12,14},{14,12},{16,18},{18,... | collective-permute-start | bytes 786440 | tf_op jit(solution)/shard_map/ppermute | solution.py:309
  13.7 11.9 %collective-permute-start.7 = (bf16[128,1024]{1,0:T(8,128)(2,1)S(1)}, bf16[128,1024]{1,0:T(8,128)(2,1)S(1)}, u32[]{:S(2)}, u32[]{:S(2)}) collective-permute-start(bf16[128,1024]{1,0:T(8,128)(2,1)S(1)} %get-tuple-element.47), channel_id=1, source_target_pairs={{0,4},{2,6},{4,0},{6,2},{8,12},{10,14},{12,8},{14,10},{16,20},{18,... | collective-permute-start | bytes 786440 | tf_op jit(solution)/shard_map/ppermute | solution.py:309
  14.2 11.3 %collective-permute-start.8 = (bf16[128,1024]{1,0:T(8,128)(2,1)S(1)}, bf16[128,1024]{1,0:T(8,128)(2,1)S(1)}, u32[]{:S(2)}, u32[]{:S(2)}) collective-permute-start(bf16[128,1024]{1,0:T(8,128)(2,1)S(1)} %get-tuple-element.48), channel_id=1, source_target_pairs={{0,6},{2,4},{4,2},{6,0},{8,14},{10,12},{12,10},{14,8},{16,22},{18,... | collective-permute-start | bytes 786440 | tf_op jit(solution)/shard_map/ppermute | solution.py:309
  20.0 6.2 %collective-permute-start.5 = (bf16[272,256]{1,0:T(8,128)(2,1)S(1)}, bf16[272,256]{1,0:T(8,128)(2,1)S(1)}, u32[]{:S(2)}, u32[]{:S(2)}) collective-permute-start(bf16[272,256]{1,0:T(8,128)(2,1)S(1)} %shard_map.106), channel_id=1, source_target_pairs={{0,8},{2,10},{4,12},{6,14},{8,16},{10,18},{12,20},{14,22},{16,24},... | collective-permute-start | bytes 417800 | tf_op jit(solution)/shard_map/ppermute | solution.py:313
  21.6 4.6 %collective-permute-start.4 = (f32[8,128]{1,0:T(8,128)S(1)}, f32[8,128]{1,0:T(8,128)S(1)}, u32[]{:S(2)}, u32[]{:S(2)}) collective-permute-start(f32[8,128]{1,0:T(8,128)S(1)} %shard_map.105), channel_id=1, source_target_pairs={{0,16},{2,18},{4,20},{6,22},{8,24},{10,26},{12,28},{14,30},{16,0},... | collective-permute-start | bytes 12296 | tf_op jit(solution)/shard_map/ppermute | solution.py:309
  34.3 8.7 %collective-permute-start.12 = (bf16[512,256]{1,0:T(8,128)(2,1)S(1)}, bf16[512,256]{1,0:T(8,128)(2,1)S(1)}, u32[]{:S(2)}, u32[]{:S(2)}) collective-permute-start(bf16[512,256]{1,0:T(8,128)(2,1)S(1)} %get-tuple-element.56), channel_id=1, source_target_pairs={{8,0},{10,2},{12,4},{14,6},{16,8},{18,10},{20,12},{22,14},{24,16},... | collective-permute-start | bytes 786440 | tf_op jit(solution)/shard_map/ppermute | solution.py:313
  35.6 15.6 %collective-permute-start.9 = (bf16[128,1024]{1,0:T(8,128)(2,1)S(1)}, bf16[128,1024]{1,0:T(8,128)(2,1)S(1)}, u32[]{:S(2)}, u32[]{:S(2)}) collective-permute-start(bf16[128,1024]{1,0:T(8,128)(2,1)S(1)} %get-tuple-element.50), channel_id=1, source_target_pairs={{0,2},{2,0},{4,6},{6,4},{8,10},{10,8},{12,14},{14,12},{16,18},{18,... | collective-permute-start | bytes 786440 | tf_op jit(solution)/shard_map/ppermute | solution.py:309
  36.6 16.9 %collective-permute-start.10 = (bf16[128,1024]{1,0:T(8,128)(2,1)S(1)}, bf16[128,1024]{1,0:T(8,128)(2,1)S(1)}, u32[]{:S(2)}, u32[]{:S(2)}) collective-permute-start(bf16[128,1024]{1,0:T(8,128)(2,1)S(1)} %get-tuple-element.51), channel_id=1, source_target_pairs={{0,4},{2,6},{4,0},{6,2},{8,12},{10,14},{12,8},{14,10},{16,20},{18,... | collective-permute-start | bytes 786440 | tf_op jit(solution)/shard_map/ppermute | solution.py:309
  37.2 16.3 %collective-permute-start.11 = (bf16[128,1024]{1,0:T(8,128)(2,1)S(1)}, bf16[128,1024]{1,0:T(8,128)(2,1)S(1)}, u32[]{:S(2)}, u32[]{:S(2)}) collective-permute-start(bf16[128,1024]{1,0:T(8,128)(2,1)S(1)} %get-tuple-element.52), channel_id=1, source_target_pairs={{0,6},{2,4},{4,2},{6,0},{8,14},{10,12},{12,10},{14,8},{16,22},{18,... | collective-permute-start | bytes 786440 | tf_op jit(solution)/shard_map/ppermute | solution.py:309
  43.0 6.9 %collective-permute-start.13 = (bf16[256,256]{1,0:T(8,128)(2,1)S(1)}, bf16[256,256]{1,0:T(8,128)(2,1)S(1)}, u32[]{:S(2)}, u32[]{:S(2)}) collective-permute-start(bf16[256,256]{1,0:T(8,128)(2,1)S(1)} %shard_map.109), channel_id=1, source_target_pairs={{8,0},{10,2},{12,4},{14,6},{16,8},{18,10},{20,12},{22,14},{24,16},... | collective-permute-start | bytes 393224 | tf_op jit(solution)/shard_map/ppermute | solution.py:313
  49.9 4.6 %collective-permute-start.14 = (bf16[128,256]{1,0:T(8,128)(2,1)S(1)}, bf16[128,256]{1,0:T(8,128)(2,1)S(1)}, u32[]{:S(2)}, u32[]{:S(2)}) collective-permute-start(bf16[128,256]{1,0:T(8,128)(2,1)S(1)} %get-tuple-element.59), channel_id=1, source_target_pairs={{0,2},{2,0},{4,6},{6,4},{8,10},{10,8},{12,14},{14,12},{16,18},{18,... | collective-permute-start | bytes 196616 | tf_op jit(solution)/shard_map/ppermute | solution.py:309
  50.5 4.3 %collective-permute-start.15 = (bf16[128,256]{1,0:T(8,128)(2,1)S(1)}, bf16[128,256]{1,0:T(8,128)(2,1)S(1)}, u32[]{:S(2)}, u32[]{:S(2)}) collective-permute-start(bf16[128,256]{1,0:T(8,128)(2,1)S(1)} %get-tuple-element.60), channel_id=1, source_target_pairs={{0,4},{2,6},{4,0},{6,2},{8,12},{10,14},{12,8},{14,10},{16,20},{18,... | collective-permute-start | bytes 196616 | tf_op jit(solution)/shard_map/ppermute | solution.py:309
  51.2 5.2 %collective-permute-start.16 = (bf16[128,256]{1,0:T(8,128)(2,1)S(1)}, bf16[128,256]{1,0:T(8,128)(2,1)S(1)}, u32[]{:S(2)}, u32[]{:S(2)}) collective-permute-start(bf16[128,256]{1,0:T(8,128)(2,1)S(1)} %get-tuple-element.61), channel_id=1, source_target_pairs={{0,6},{2,4},{4,2},{6,0},{8,14},{10,12},{12,10},{14,8},{16,22},{18,... | collective-permute-start | bytes 196616 | tf_op jit(solution)/shard_map/ppermute | solution.py:309

commit v5 on v4

--- a/solution.py
+++ b/solution.py
@@ -308,6 +308,10 @@
     def swap(array, by):
         return lax.ppermute(array, AXIS, [(i, i ^ by) for i in range(count)])
 
+    def swap_all(slots):
+        got = {j: swap(slots[j], j) for j in range(group - 1, 0, -1)}
+        return [slots[0]] + [got[j] for j in range(1, group)]
+
     def shift(array, by, around=False):
         pairs = [(i, (i + by) % count) for i in range(count) if around or 0 <= i + by < count]
         return lax.ppermute(array, AXIS, pairs)
@@ -325,7 +329,7 @@
         vmem=4 << 20,
         space=pltpu.HBM,
     )
-    kv = [kv[0]] + [swap(kv[j], j) for j in range(1, group)]
+    kv = swap_all(kv)
     qg = call(
         functools.partial(pack_qg_kernel, group),
         [shape((rows, 2 * width), BF16)] * group,
@@ -336,7 +340,7 @@
         space=pltpu.HBM,
     )
     kv, where, _ = lax.optimization_barrier((kv, where, qg[0]))
-    qg = [qg[0]] + [swap(qg[j], j) for j in range(1, group)]
+    qg = swap_all(qg)
 
     held, counted = call(
         functools.partial(gather_kernel, group),
@@ -409,7 +413,7 @@
     )
     od, (own, *partial) = results[:group], results[group:]
     firsts, back = [], []
-    passed = shift(partial[links[0]], -group)
+    passed = shift(partial[links[0]], -group, True)
     if joined:
         firsts.append(-chain)
         back.append(passed)
@@ -417,14 +421,14 @@
         passed = call(
             relay_kernel, shape((chain * rows, 2 * HEAD_DIM), BF16), [], [partial[i], passed], vmem=2 << 20
         )
-        passed = shift(passed, -group)
+        passed = shift(passed, -group, True)
     firsts.append(group - chain)
     back.append(passed)
     for k, i in enumerate(links[::-1]):
         if needs[k] > chain and not joined:
             firsts.append(0)
             back.append(shift(partial[i - 1], -group * (k + 1)))
-    od = [od[0]] + [swap(od[j], j) for j in range(1, group)]
+    od = swap_all(od)
     dkv = call(
         functools.partial(add_kv_kernel, group, firsts),
         [shape((rows, 2 * HEAD_DIM), BF16)] * group,
@@ -433,7 +437,7 @@
         scratch=[vmem((group, rows, 2 * HEAD_DIM), BF16)],
         vmem=4 << 20,
     )
-    dkv = [dkv[0]] + [swap(dkv[j], j) for j in range(1, group)]
+    dkv = swap_all(dkv)
     attended, grad_queries = call(
         functools.partial(unpack_kernel, group),
         [shape((rows, group * width), BF16)] * 2,

time: 57.4 us -> 55.5 us (0.967)
  waiting for transfers between devices: 19.5 us -> 14.7 us
  starting transfers between devices: 23.6 us -> 26.7 us
    ppermute x4, waiting for transfers between devices: 12.8 us -> 7.66 us  [shift(): return lax.ppermute(array, AXIS, pairs)]
    ppermute x4, starting transfers between devices: 5.79 us -> 8.93 us  [shift(): return lax.ppermute(array, AXIS, pairs)]
  transfers between devices with their start and end apart: 17 -> 17, of which waited for: 9 -> 9; matrix products, arithmetic and copies ran while one was open for 0% -> 0% of each run, Pallas kernels for 4% -> 5%
where the time goes in v5:
time: 55.5 us; the launch traced here: 55.2 us
  starting transfers between devices  26.7 us (48%)
  waiting for transfers between devices  14.7 us (26%)
  Pallas kernels  12.4 us (22%)
  local copies, waits for them, and re-layouts  0.73 us (1%)
  between operations  0.71 us (1%)
    ppermute x13, starting transfers between devices, swap(): return lax.ppermute(array, AXIS, [(i, i ^ by) for i in range(count)])  17.7 us
    pallas_call x10, Pallas kernels, call(): pl.pallas_call(kernel, out_shape=out_shape, in_specs=[pl.BlockSpec(memory...  12.4 us
    ppermute x4, starting transfers between devices, shift(): return lax.ppermute(array, AXIS, pairs)  8.93 us
    ppermute x4, waiting for transfers between devices, shift(): return lax.ppermute(array, AXIS, pairs)  7.66 us
    ppermute x13, waiting for transfers between devices, swap(): return lax.ppermute(array, AXIS, [(i, i ^ by) for i in range(count)])  7 us
  transfers between devices with their start and end apart: 17, of which 9 were waited for; matrix products, arithmetic and copies ran while one was open for 0% of the time, Pallas kernels for 5%

profile of v5, /device:TPU:0, one launch (start us, length us, event | category | flops | bytes accessed | tf_op | source)
XLA Modules:
  0.0 55.2 jit_solution(8937714343955035299)
XLA Ops:
  0.6 1.0 %shard_map.102 = (bf16[144,256]{1,0:T(8,128)(2,1)S(1)}, bf16[144,256]{1,0:T(8,128)(2,1)S(1)}, bf16[144,256]{1,0:T(8,128)(2,1)S(1)}, bf16[144,256]{1,0:T(8,128)(2,1)S(1)}) custom-call(s32[1]{0:T(128)} %bitcast.r_ref, bf16[128,512]{1,0:T(8,128)(2,1)} %key_ref.1, bf16[128,512]{1,0:T(8,128)(2,1)} %value_ref.1, s32[1,128]{1,0:T(1,128)} %bitcast.4, s32[1,128]{1,0:T(1,128)} %bitcast.5), custom_call_target="tpu_custom_call" | custom-call | tf_op jit(solution)/shard_map/pallas_call | solution.py:36
  1.6 3.0 %collective-permute-start = (bf16[144,256]{1,0:T(8,128)(2,1)S(1)}, bf16[144,256]{1,0:T(8,128)(2,1)S(1)}, u32[]{:S(2)}, u32[]{:S(2)}) collective-permute-start(bf16[144,256]{1,0:T(8,128)(2,1)S(1)} %get-tuple-element.35), channel_id=1, source_target_pairs={{0,2},{2,0},{4,6},{6,4},{8,10},{10,8},{12,14},{14,12},{16,18},{18,... | collective-permute-start | bytes 221192 | tf_op jit(solution)/shard_map/ppermute | solution.py:309
  4.7 1.5 %collective-permute-start.1 = (bf16[144,256]{1,0:T(8,128)(2,1)S(1)}, bf16[144,256]{1,0:T(8,128)(2,1)S(1)}, u32[]{:S(2)}, u32[]{:S(2)}) collective-permute-start(bf16[144,256]{1,0:T(8,128)(2,1)S(1)} %get-tuple-element.36), channel_id=1, source_target_pairs={{0,4},{2,6},{4,0},{6,2},{8,12},{10,14},{12,8},{14,10},{16,20},{18,... | collective-permute-start | bytes 221192 | tf_op jit(solution)/shard_map/ppermute | solution.py:309
  6.2 0.7 %copy-done = s32[16]{0:T(128)S(1)} copy-done((s32[16]{0:T(128)S(1)}, s32[16]{0:T(128)}, u32[]{:S(2)}) %copy-start) | copy-done | bytes 88
  6.9 1.4 %shard_map.103 = (bf16[128,1024]{1,0:T(8,128)(2,1)S(1)}, bf16[128,1024]{1,0:T(8,128)(2,1)S(1)}, bf16[128,1024]{1,0:T(8,128)(2,1)S(1)}, bf16[128,1024]{1,0:T(8,128)(2,1)S(1)}) custom-call(s32[1]{0:T(128)} %bitcast.r_ref, bf16[128,2048]{1,0:T(8,128)(2,1)} %query_ref.1, bf16[128,2048]{1,0:T(8,128)(2,1)} %grad_ref.1), custom_call_target="tpu_custom_call" | custom-call | tf_op jit(solution)/shard_map/pallas_call | solution.py:36
  8.4 0.6 %collective-permute-done.1.refs_2_ = bf16[144,256]{1,0:T(8,128)(2,1)S(1)} collective-permute-done((bf16[144,256]{1,0:T(8,128)(2,1)S(1)}, bf16[144,256]{1,0:T(8,128)(2,1)S(1)}, u32[]{:S(2)}, u32[]{:S(2)}) %collective-permute-start.1) | collective-permute-done | bytes 73760 | tf_op jit(solution)/shard_map/ppermute | solution.py:309
  9.0 2.4 %collective-permute-done.2.refs_3_ = bf16[144,256]{1,0:T(8,128)(2,1)S(1)} collective-permute-done((bf16[144,256]{1,0:T(8,128)(2,1)S(1)}, bf16[144,256]{1,0:T(8,128)(2,1)S(1)}, u32[]{:S(2)}, u32[]{:S(2)}) %collective-permute-start.2) | collective-permute-done | bytes 73760 | tf_op jit(solution)/shard_map/ppermute | solution.py:309
  11.4 0.1 shard_map.104
  11.5 1.6 %collective-permute-start.3 = (bf16[528,256]{1,0:T(8,128)(2,1)S(1)}, bf16[528,256]{1,0:T(8,128)(2,1)S(1)}, u32[]{:S(2)}, u32[]{:S(2)}) collective-permute-start(bf16[528,256]{1,0:T(8,128)(2,1)S(1)} %get-tuple-element.45.refs_3_), channel_id=1, source_target_pairs={{0,8},{2,10},{4,12},{6,14},{8,16},{10,18},{12,20},{14,22},{16,24},... | collective-permute-start | bytes 811016 | tf_op jit(solution)/shard_map/ppermute | solution.py:317
  13.1 0.5 collective-permute-start.6
  13.7 0.5 collective-permute-start.7
  14.2 2.4 %collective-permute-start.8 = (bf16[128,1024]{1,0:T(8,128)(2,1)S(1)}, bf16[128,1024]{1,0:T(8,128)(2,1)S(1)}, u32[]{:S(2)}, u32[]{:S(2)}) collective-permute-start(bf16[128,1024]{1,0:T(8,128)(2,1)S(1)} %get-tuple-element.48), channel_id=1, source_target_pairs={{0,6},{2,4},{4,2},{6,0},{8,14},{10,12},{12,10},{14,8},{16,22},{18,... | collective-permute-start | bytes 786440 | tf_op jit(solution)/shard_map/ppermute | solution.py:309
  16.6 3.4 %collective-permute-done.3.near_ref.part_ref.refs_2_ = bf16[528,256]{1,0:T(8,128)(2,1)S(1)} collective-permute-done((bf16[528,256]{1,0:T(8,128)(2,1)S(1)}, bf16[528,256]{1,0:T(8,128)(2,1)S(1)}, u32[]{:S(2)}, u32[]{:S(2)}) %collective-permute-start.3) | collective-permute-done | bytes 270368 | tf_op jit(solution)/shard_map/ppermute | solution.py:317
  20.0 1.6 %collective-permute-start.5 = (bf16[272,256]{1,0:T(8,128)(2,1)S(1)}, bf16[272,256]{1,0:T(8,128)(2,1)S(1)}, u32[]{:S(2)}, u32[]{:S(2)}) collective-permute-start(bf16[272,256]{1,0:T(8,128)(2,1)S(1)} %shard_map.106), channel_id=1, source_target_pairs={{0,8},{2,10},{4,12},{6,14},{8,16},{10,18},{12,20},{14,22},{16,24},... | collective-permute-start | bytes 417800 | tf_op jit(solution)/shard_map/ppermute | solution.py:317
  21.6 2.7 %collective-permute-start.4 = (f32[8,128]{1,0:T(8,128)S(1)}, f32[8,128]{1,0:T(8,128)S(1)}, u32[]{:S(2)}, u32[]{:S(2)}) collective-permute-start(f32[8,128]{1,0:T(8,128)S(1)} %shard_map.105), channel_id=1, source_target_pairs={{0,16},{2,18},{4,20},{6,22},{8,24},{10,26},{12,28},{14,30},{16,0},... | collective-permute-start | bytes 12296 | tf_op jit(solution)/shard_map/ppermute | solution.py:309
  24.3 1.2 %collective-permute-done.7.refs_6_ = bf16[128,1024]{1,0:T(8,128)(2,1)S(1)} collective-permute-done((bf16[128,1024]{1,0:T(8,128)(2,1)S(1)}, bf16[128,1024]{1,0:T(8,128)(2,1)S(1)}, u32[]{:S(2)}, u32[]{:S(2)}) %collective-permute-start.7) | collective-permute-done | bytes 262176 | tf_op jit(solution)/shard_map/ppermute | solution.py:309
  25.5 0.7 %collective-permute-done.4.refs_0_ = f32[8,128]{1,0:T(8,128)S(1)} collective-permute-done((f32[8,128]{1,0:T(8,128)S(1)}, f32[8,128]{1,0:T(8,128)S(1)}, u32[]{:S(2)}, u32[]{:S(2)}) %collective-permute-start.4) | collective-permute-done | bytes 4128 | tf_op jit(solution)/shard_map/ppermute | solution.py:309
  26.2 8.0 %shard_map.107 = (bf16[128,1024]{1,0:T(8,128)(2,1)S(1)}, bf16[128,1024]{1,0:T(8,128)(2,1)S(1)}, bf16[128,1024]{1,0:T(8,128)(2,1)S(1)}, bf16[128,1024]{1,0:T(8,12...) custom-call(s32[6]{0:T(128)S(1)} %pad_add_fusion.where_ref, ...), custom_call_target="tpu_custom_call" | custom-call | flops 2818572288 | bytes 16777216 | tf_op jit(solution)/shard_map/pallas_call | solution.py:36
  34.3 2.6 %collective-permute-start.12 = (bf16[512,256]{1,0:T(8,128)(2,1)S(1)}, bf16[512,256]{1,0:T(8,128)(2,1)S(1)}, u32[]{:S(2)}, u32[]{:S(2)}) collective-permute-start(bf16[512,256]{1,0:T(8,128)(2,1)S(1)} %get-tuple-element.56), channel_id=1, source_target_pairs={{0,24},{2,26},{4,28},{6,30},{8,0},{10,2},{12,4},{14,6},{16,8},{18,... | collective-permute-start | bytes 786440 | tf_op jit(solution)/shard_map/ppermute | solution.py:317
  36.8 1.0 %collective-permute-start.9 = (bf16[128,1024]{1,0:T(8,128)(2,1)S(1)}, bf16[128,1024]{1,0:T(8,128)(2,1)S(1)}, u32[]{:S(2)}, u32[]{:S(2)}) collective-permute-start(bf16[128,1024]{1,0:T(8,128)(2,1)S(1)} %get-tuple-element.50), channel_id=1, source_target_pairs={{0,2},{2,0},{4,6},{6,4},{8,10},{10,8},{12,14},{14,12},{16,18},{18,... | collective-permute-start | bytes 786440 | tf_op jit(solution)/shard_map/ppermute | solution.py:309
  37.8 0.6 %collective-permute-start.10 = (bf16[128,1024]{1,0:T(8,128)(2,1)S(1)}, bf16[128,1024]{1,0:T(8,128)(2,1)S(1)}, u32[]{:S(2)}, u32[]{:S(2)}) collective-permute-start(bf16[128,1024]{1,0:T(8,128)(2,1)S(1)} %get-tuple-element.51), channel_id=1, source_target_pairs={{0,4},{2,6},{4,0},{6,2},{8,12},{10,14},{12,8},{14,10},{16,20},{18,... | collective-permute-start | bytes 786440 | tf_op jit(solution)/shard_map/ppermute | solution.py:309
  38.4 1.9 %collective-permute-start.11 = (bf16[128,1024]{1,0:T(8,128)(2,1)S(1)}, bf16[128,1024]{1,0:T(8,128)(2,1)S(1)}, u32[]{:S(2)}, u32[]{:S(2)}) collective-permute-start(bf16[128,1024]{1,0:T(8,128)(2,1)S(1)} %get-tuple-element.52), channel_id=1, source_target_pairs={{0,6},{2,4},{4,2},{6,0},{8,14},{10,12},{12,10},{14,8},{16,22},{18,... | collective-permute-start | bytes 786440 | tf_op jit(solution)/shard_map/ppermute | solution.py:309
  40.3 1.8 %collective-permute-done.12.got_ref.refs_0_ = bf16[512,256]{1,0:T(8,128)(2,1)S(1)} collective-permute-done((bf16[512,256]{1,0:T(8,128)(2,1)S(1)}, bf16[512,256]{1,0:T(8,128)(2,1)S(1)}, u32[]{:S(2)}, u32[]{:S(2)}) %collective-permute-start.12) | collective-permute-done | bytes 262176 | tf_op jit(solution)/shard_map/ppermute | solution.py:317
  42.1 3.2 %collective-permute-start.13 = (bf16[256,256]{1,0:T(8,128)(2,1)S(1)}, bf16[256,256]{1,0:T(8,128)(2,1)S(1)}, u32[]{:S(2)}, u32[]{:S(2)}) collective-permute-start(bf16[256,256]{1,0:T(8,128)(2,1)S(1)} %shard_map.109), channel_id=1, source_target_pairs={{0,24},{2,26},{4,28},{6,30},{8,0},{10,2},{12,4},{14,6},{16,8},{18,... | collective-permute-start | bytes 393224 | tf_op jit(solution)/shard_map/ppermute | solution.py:317
  45.3 2.5 %collective-permute-done.13.refs_1_ = bf16[256,256]{1,0:T(8,128)(2,1)S(1)} collective-permute-done((bf16[256,256]{1,0:T(8,128)(2,1)S(1)}, bf16[256,256]{1,0:T(8,128)(2,1)S(1)}, u32[]{:S(2)}, u32[]{:S(2)}) %collective-permute-start.13) | collective-permute-done | bytes 131104 | tf_op jit(solution)/shard_map/ppermute | solution.py:317
  47.9 0.8 %collective-permute-start.14 = (bf16[128,256]{1,0:T(8,128)(2,1)S(1)}, bf16[128,256]{1,0:T(8,128)(2,1)S(1)}, u32[]{:S(2)}, u32[]{:S(2)}) collective-permute-start(bf16[128,256]{1,0:T(8,128)(2,1)S(1)} %get-tuple-element.59), channel_id=1, source_target_pairs={{0,2},{2,0},{4,6},{6,4},{8,10},{10,8},{12,14},{14,12},{16,18},{18,... | collective-permute-start | bytes 196616 | tf_op jit(solution)/shard_map/ppermute | solution.py:309
  48.7 0.6 %collective-permute-start.15 = (bf16[128,256]{1,0:T(8,128)(2,1)S(1)}, bf16[128,256]{1,0:T(8,128)(2,1)S(1)}, u32[]{:S(2)}, u32[]{:S(2)}) collective-permute-start(bf16[128,256]{1,0:T(8,128)(2,1)S(1)} %get-tuple-element.60), channel_id=1, source_target_pairs={{0,4},{2,6},{4,0},{6,2},{8,12},{10,14},{12,8},{14,10},{16,20},{18,... | collective-permute-start | bytes 196616 | tf_op jit(solution)/shard_map/ppermute | solution.py:309
  49.3 2.1 %collective-permute-start.16 = (bf16[128,256]{1,0:T(8,128)(2,1)S(1)}, bf16[128,256]{1,0:T(8,128)(2,1)S(1)}, u32[]{:S(2)}, u32[]{:S(2)}) collective-permute-start(bf16[128,256]{1,0:T(8,128)(2,1)S(1)} %get-tuple-element.61), channel_id=1, source_target_pairs={{0,6},{2,4},{4,2},{6,0},{8,14},{10,12},{12,10},{14,8},{16,22},{18,... | collective-permute-start | bytes 196616 | tf_op jit(solution)/shard_map/ppermute | solution.py:309
  51.4 1.0 %shard_map.108 = (bf16[128,2048]{1,0:T(8,128)(2,1)}, bf16[128,2048]{1,0:T(8,128)(2,1)}) custom-call(s32[1]{0:T(128)} %bitcast.r_ref, bf16[128,1024]{1,0:T(8,128)(2,1)S(1)} %get-tuple-element.49.refs_0_, bf16[128,1024]{1,0:T(8,128)(2,1)S(1)} %collective-permute-done.9.refs_1_, bf16[128,1024]{1,0:T(8,128)(2,1)S(1)} %collective-permute-done.10.refs_2_, ...), custom_call_target="tpu_custom_call" | custom-call | tf_op jit(solution)/shard_map/pallas_call | solution.py:36
  52.5 0.5 collective-permute-done.15.refs_2_
  53.0 1.5 %collective-permute-done.16.refs_3_ = bf16[128,256]{1,0:T(8,128)(2,1)S(1)} collective-permute-done((bf16[128,256]{1,0:T(8,128)(2,1)S(1)}, bf16[128,256]{1,0:T(8,128)(2,1)S(1)}, u32[]{:S(2)}, u32[]{:S(2)}) %collective-permute-start.16) | collective-permute-done | bytes 65568 | tf_op jit(solution)/shard_map/ppermute | solution.py:309
  54.5 0.7 %shard_map.111 = (bf16[128,512]{1,0:T(8,128)(2,1)}, bf16[128,512]{1,0:T(8,128)(2,1)}) custom-call(s32[1]{0:T(128)} %bitcast.r_ref, bf16[128,256]{1,0:T(8,128)(2,1)S(1)} %get-tuple-element.58.refs_0_, bf16[128,256]{1,0:T(8,128)(2,1)S(1)} %collective-permute-done.14.refs_1_, bf16[128,256]{1,0:T(8,128)(2,1)S(1)} %collective-permute-done.15.refs_2_, ...), custom_call_target="tpu_custom_call" | custom-call | tf_op jit(solution)/shard_map/pallas_call | solution.py:36
  (16 shorter events, 0.3 us)
Async XLA Ops:
  1.6 6.7 %collective-permute-start = (bf16[144,256]{1,0:T(8,128)(2,1)S(1)}, bf16[144,256]{1,0:T(8,128)(2,1)S(1)}, u32[]{:S(2)}, u32[]{:S(2)}) collective-permute-start(bf16[144,256]{1,0:T(8,128)(2,1)S(1)} %get-tuple-element.35), channel_id=1, source_target_pairs={{0,2},{2,0},{4,6},{6,4},{8,10},{10,8},{12,14},{14,12},{16,18},{18,... | collective-permute-start | bytes 221192 | tf_op jit(solution)/shard_map/ppermute | solution.py:309
  4.7 4.4 %collective-permute-start.1 = (bf16[144,256]{1,0:T(8,128)(2,1)S(1)}, bf16[144,256]{1,0:T(8,128)(2,1)S(1)}, u32[]{:S(2)}, u32[]{:S(2)}) collective-permute-start(bf16[144,256]{1,0:T(8,128)(2,1)S(1)} %get-tuple-element.36), channel_id=1, source_target_pairs={{0,4},{2,6},{4,0},{6,2},{8,12},{10,14},{12,8},{14,10},{16,20},{18,... | collective-permute-start | bytes 221192 | tf_op jit(solution)/shard_map/ppermute | solution.py:309
  6.2 5.3 %collective-permute-start.2 = (bf16[144,256]{1,0:T(8,128)(2,1)S(1)}, bf16[144,256]{1,0:T(8,128)(2,1)S(1)}, u32[]{:S(2)}, u32[]{:S(2)}) collective-permute-start(bf16[144,256]{1,0:T(8,128)(2,1)S(1)} %get-tuple-element.37), channel_id=1, source_target_pairs={{0,6},{2,4},{4,2},{6,0},{8,14},{10,12},{12,10},{14,8},{16,22},{18,... | collective-permute-start | bytes 221192 | tf_op jit(solution)/shard_map/ppermute | solution.py:309
  6.2 0.7 %copy-start = (s32[16]{0:T(128)S(1)}, s32[16]{0:T(128)}, u32[]{:S(2)}) copy-start(s32[16]{0:T(128)} %param.13) | copy-start | bytes 196
  11.5 8.4 %collective-permute-start.3 = (bf16[528,256]{1,0:T(8,128)(2,1)S(1)}, bf16[528,256]{1,0:T(8,128)(2,1)S(1)}, u32[]{:S(2)}, u32[]{:S(2)}) collective-permute-start(bf16[528,256]{1,0:T(8,128)(2,1)S(1)} %get-tuple-element.45.refs_3_), channel_id=1, source_target_pairs={{0,8},{2,10},{4,12},{6,14},{8,16},{10,18},{12,20},{14,22},{16,24},... | collective-permute-start | bytes 811016 | tf_op jit(solution)/shard_map/ppermute | solution.py:317
  13.1 11.2 %collective-permute-start.6 = (bf16[128,1024]{1,0:T(8,128)(2,1)S(1)}, bf16[128,1024]{1,0:T(8,128)(2,1)S(1)}, u32[]{:S(2)}, u32[]{:S(2)}) collective-permute-start(bf16[128,1024]{1,0:T(8,128)(2,1)S(1)} %get-tuple-element.46), channel_id=1, source_target_pairs={{0,2},{2,0},{4,6},{6,4},{8,10},{10,8},{12,14},{14,12},{16,18},{18,... | collective-permute-start | bytes 786440 | tf_op jit(solution)/shard_map/ppermute | solution.py:309
  13.7 11.9 %collective-permute-start.7 = (bf16[128,1024]{1,0:T(8,128)(2,1)S(1)}, bf16[128,1024]{1,0:T(8,128)(2,1)S(1)}, u32[]{:S(2)}, u32[]{:S(2)}) collective-permute-start(bf16[128,1024]{1,0:T(8,128)(2,1)S(1)} %get-tuple-element.47), channel_id=1, source_target_pairs={{0,4},{2,6},{4,0},{6,2},{8,12},{10,14},{12,8},{14,10},{16,20},{18,... | collective-permute-start | bytes 786440 | tf_op jit(solution)/shard_map/ppermute | solution.py:309
  14.2 11.3 %collective-permute-start.8 = (bf16[128,1024]{1,0:T(8,128)(2,1)S(1)}, bf16[128,1024]{1,0:T(8,128)(2,1)S(1)}, u32[]{:S(2)}, u32[]{:S(2)}) collective-permute-start(bf16[128,1024]{1,0:T(8,128)(2,1)S(1)} %get-tuple-element.48), channel_id=1, source_target_pairs={{0,6},{2,4},{4,2},{6,0},{8,14},{10,12},{12,10},{14,8},{16,22},{18,... | collective-permute-start | bytes 786440 | tf_op jit(solution)/shard_map/ppermute | solution.py:309
  20.0 6.2 %collective-permute-start.5 = (bf16[272,256]{1,0:T(8,128)(2,1)S(1)}, bf16[272,256]{1,0:T(8,128)(2,1)S(1)}, u32[]{:S(2)}, u32[]{:S(2)}) collective-permute-start(bf16[272,256]{1,0:T(8,128)(2,1)S(1)} %shard_map.106), channel_id=1, source_target_pairs={{0,8},{2,10},{4,12},{6,14},{8,16},{10,18},{12,20},{14,22},{16,24},... | collective-permute-start | bytes 417800 | tf_op jit(solution)/shard_map/ppermute | solution.py:317
  21.6 4.6 %collective-permute-start.4 = (f32[8,128]{1,0:T(8,128)S(1)}, f32[8,128]{1,0:T(8,128)S(1)}, u32[]{:S(2)}, u32[]{:S(2)}) collective-permute-start(f32[8,128]{1,0:T(8,128)S(1)} %shard_map.105), channel_id=1, source_target_pairs={{0,16},{2,18},{4,20},{6,22},{8,24},{10,26},{12,28},{14,30},{16,0},... | collective-permute-start | bytes 12296 | tf_op jit(solution)/shard_map/ppermute | solution.py:309
  34.3 7.8 %collective-permute-start.12 = (bf16[512,256]{1,0:T(8,128)(2,1)S(1)}, bf16[512,256]{1,0:T(8,128)(2,1)S(1)}, u32[]{:S(2)}, u32[]{:S(2)}) collective-permute-start(bf16[512,256]{1,0:T(8,128)(2,1)S(1)} %get-tuple-element.56), channel_id=1, source_target_pairs={{0,24},{2,26},{4,28},{6,30},{8,0},{10,2},{12,4},{14,6},{16,8},{18,... | collective-permute-start | bytes 786440 | tf_op jit(solution)/shard_map/ppermute | solution.py:317
  36.8 12.5 %collective-permute-start.9 = (bf16[128,1024]{1,0:T(8,128)(2,1)S(1)}, bf16[128,1024]{1,0:T(8,128)(2,1)S(1)}, u32[]{:S(2)}, u32[]{:S(2)}) collective-permute-start(bf16[128,1024]{1,0:T(8,128)(2,1)S(1)} %get-tuple-element.50), channel_id=1, source_target_pairs={{0,2},{2,0},{4,6},{6,4},{8,10},{10,8},{12,14},{14,12},{16,18},{18,... | collective-permute-start | bytes 786440 | tf_op jit(solution)/shard_map/ppermute | solution.py:309
  37.8 13.7 %collective-permute-start.10 = (bf16[128,1024]{1,0:T(8,128)(2,1)S(1)}, bf16[128,1024]{1,0:T(8,128)(2,1)S(1)}, u32[]{:S(2)}, u32[]{:S(2)}) collective-permute-start(bf16[128,1024]{1,0:T(8,128)(2,1)S(1)} %get-tuple-element.51), channel_id=1, source_target_pairs={{0,4},{2,6},{4,0},{6,2},{8,12},{10,14},{12,8},{14,10},{16,20},{18,... | collective-permute-start | bytes 786440 | tf_op jit(solution)/shard_map/ppermute | solution.py:309
  38.4 13.0 %collective-permute-start.11 = (bf16[128,1024]{1,0:T(8,128)(2,1)S(1)}, bf16[128,1024]{1,0:T(8,128)(2,1)S(1)}, u32[]{:S(2)}, u32[]{:S(2)}) collective-permute-start(bf16[128,1024]{1,0:T(8,128)(2,1)S(1)} %get-tuple-element.52), channel_id=1, source_target_pairs={{0,6},{2,4},{4,2},{6,0},{8,14},{10,12},{12,10},{14,8},{16,22},{18,... | collective-permute-start | bytes 786440 | tf_op jit(solution)/shard_map/ppermute | solution.py:309
  42.1 5.7 %collective-permute-start.13 = (bf16[256,256]{1,0:T(8,128)(2,1)S(1)}, bf16[256,256]{1,0:T(8,128)(2,1)S(1)}, u32[]{:S(2)}, u32[]{:S(2)}) collective-permute-start(bf16[256,256]{1,0:T(8,128)(2,1)S(1)} %shard_map.109), channel_id=1, source_target_pairs={{0,24},{2,26},{4,28},{6,30},{8,0},{10,2},{12,4},{14,6},{16,8},{18,... | collective-permute-start | bytes 393224 | tf_op jit(solution)/shard_map/ppermute | solution.py:317
  47.9 4.6 %collective-permute-start.14 = (bf16[128,256]{1,0:T(8,128)(2,1)S(1)}, bf16[128,256]{1,0:T(8,128)(2,1)S(1)}, u32[]{:S(2)}, u32[]{:S(2)}) collective-permute-start(bf16[128,256]{1,0:T(8,128)(2,1)S(1)} %get-tuple-element.59), channel_id=1, source_target_pairs={{0,2},{2,0},{4,6},{6,4},{8,10},{10,8},{12,14},{14,12},{16,18},{18,... | collective-permute-start | bytes 196616 | tf_op jit(solution)/shard_map/ppermute | solution.py:309
  48.7 4.3 %collective-permute-start.15 = (bf16[128,256]{1,0:T(8,128)(2,1)S(1)}, bf16[128,256]{1,0:T(8,128)(2,1)S(1)}, u32[]{:S(2)}, u32[]{:S(2)}) collective-permute-start(bf16[128,256]{1,0:T(8,128)(2,1)S(1)} %get-tuple-element.60), channel_id=1, source_target_pairs={{0,4},{2,6},{4,0},{6,2},{8,12},{10,14},{12,8},{14,10},{16,20},{18,... | collective-permute-start | bytes 196616 | tf_op jit(solution)/shard_map/ppermute | solution.py:309
  49.3 5.2 %collective-permute-start.16 = (bf16[128,256]{1,0:T(8,128)(2,1)S(1)}, bf16[128,256]{1,0:T(8,128)(2,1)S(1)}, u32[]{:S(2)}, u32[]{:S(2)}) collective-permute-start(bf16[128,256]{1,0:T(8,128)(2,1)S(1)} %get-tuple-element.61), channel_id=1, source_target_pairs={{0,6},{2,4},{4,2},{6,0},{8,14},{10,12},{12,10},{14,8},{16,22},{18,... | collective-permute-start | bytes 196616 | tf_op jit(solution)/shard_map/ppermute | solution.py:309

commit v6 on v5

--- a/solution.py
+++ b/solution.py
@@ -28,7 +28,7 @@
 
 
 def call(
-    kernel, out_shape, scalars, vectors, scratch=(), flops=0, nbytes=0, vmem=None, space=pltpu.VMEM
+    kernel, out_shape, scalars, vectors, scratch=(), flops=0, nbytes=0, vmem=None, space=pltpu.VMEM, into=pltpu.VMEM
 ):
     def keep(array):
         return pltpu.with_memory_space_constraint(array, space) if space == pltpu.HBM else array
@@ -38,7 +38,7 @@
         out_shape=out_shape,
         in_specs=[pl.BlockSpec(memory_space=pltpu.SMEM)] * len(scalars)
         + [pl.BlockSpec(memory_space=space)] * len(vectors),
-        out_specs=jax.tree.map(lambda _: pl.BlockSpec(memory_space=pltpu.VMEM), out_shape),
+        out_specs=jax.tree.map(lambda _: pl.BlockSpec(memory_space=into), out_shape),
         scratch_shapes=list(scratch),
         cost_estimate=pl.CostEstimate(flops=flops, bytes_accessed=nbytes, transcendentals=0),
         compiler_params=pltpu.CompilerParams(vmem_limit_bytes=vmem),
@@ -277,13 +277,19 @@
 
 
 def unpack_kernel(group, r_ref, *refs):
-    slots, (left_ref, right_ref) = refs[:group], refs[group:]
+    slots, (left_ref, right_ref, sems) = refs[:group], refs[group:]
     r = r_ref[0]
     width = left_ref.shape[1] // group
+    copies = []
     for j in range(group):
         cols = block_at(r ^ j, width)
-        left_ref[:, cols] = slots[j][:, 0:width]
-        right_ref[:, cols] = slots[j][:, width:]
+        for i, ref in enumerate((left_ref, right_ref)):
+            part = slots[j].at[:, i * width : (i + 1) * width]
+            copies.append(pltpu.make_async_copy(part, ref.at[:, cols], sems.at[2 * j + i]))
+    for copy in copies:
+        copy.start()
+    for copy in copies:
+        copy.wait()
 
 
 def per_device(queries, key_rows, value_rows, grad_out, doc_ids, loss_mask, windows):
@@ -443,14 +449,18 @@
         [shape((rows, group * width), BF16)] * 2,
         [r],
         od,
-        vmem=4 << 20,
+        scratch=[pltpu.SemaphoreType.DMA((2 * group,))],
+        vmem=4 << 20,
+        into=pltpu.HBM,
     )
     grad_keys, grad_values = call(
         functools.partial(unpack_kernel, group),
         [shape((rows, group * HEAD_DIM), BF16)] * 2,
         [r],
         dkv,
-        vmem=4 << 20,
+        scratch=[pltpu.SemaphoreType.DMA((2 * group,))],
+        vmem=4 << 20,
+        into=pltpu.HBM,
     )
     return attended, grad_queries, grad_keys, grad_values
 

time: 55.5 us -> 55.5 us (level)
  no operation moved by 1% of the time
where the time goes in v6:
time: 55.5 us; the launch traced here: 55.3 us
  starting transfers between devices  26.7 us (48%)
  waiting for transfers between devices  14.7 us (26%)
  Pallas kernels  12.4 us (22%)
  local copies, waits for them, and re-layouts  0.73 us (1%)
  between operations  0.73 us (1%)
    ppermute x13, starting transfers between devices, swap(): return lax.ppermute(array, AXIS, [(i, i ^ by) for i in range(count)])  17.7 us
    pallas_call x10, Pallas kernels, call(): pl.pallas_call(kernel, out_shape=out_shape, in_specs=[pl.BlockSpec(memory...  12.4 us
    ppermute x4, starting transfers between devices, shift(): return lax.ppermute(array, AXIS, pairs)  8.93 us
    ppermute x4, waiting for transfers between devices, shift(): return lax.ppermute(array, AXIS, pairs)  7.66 us
    ppermute x13, waiting for transfers between devices, swap(): return lax.ppermute(array, AXIS, [(i, i ^ by) for i in range(count)])  7 us
  transfers between devices with their start and end apart: 17, of which 9 were waited for; matrix products, arithmetic and copies ran while one was open for 0% of the time, Pallas kernels for 5%

profile of v6, /device:TPU:0, one launch (start us, length us, event | category | flops | bytes accessed | tf_op | source)
XLA Modules:
  0.0 55.3 jit_solution(2114167890002321946)
XLA Ops:
  0.6 1.0 %shard_map.102 = (bf16[144,256]{1,0:T(8,128)(2,1)S(1)}, bf16[144,256]{1,0:T(8,128)(2,1)S(1)}, bf16[144,256]{1,0:T(8,128)(2,1)S(1)}, bf16[144,256]{1,0:T(8,128)(2,1)S(1)}) custom-call(s32[1]{0:T(128)} %bitcast.r_ref, bf16[128,512]{1,0:T(8,128)(2,1)} %key_ref.1, bf16[128,512]{1,0:T(8,128)(2,1)} %value_ref.1, s32[1,128]{1,0:T(1,128)} %bitcast.4, s32[1,128]{1,0:T(1,128)} %bitcast.5), custom_call_target="tpu_custom_call" | custom-call | tf_op jit(solution)/shard_map/pallas_call | solution.py:36
  1.6 3.0 %collective-permute-start = (bf16[144,256]{1,0:T(8,128)(2,1)S(1)}, bf16[144,256]{1,0:T(8,128)(2,1)S(1)}, u32[]{:S(2)}, u32[]{:S(2)}) collective-permute-start(bf16[144,256]{1,0:T(8,128)(2,1)S(1)} %get-tuple-element.35), channel_id=1, source_target_pairs={{0,2},{2,0},{4,6},{6,4},{8,10},{10,8},{12,14},{14,12},{16,18},{18,... | collective-permute-start | bytes 221192 | tf_op jit(solution)/shard_map/ppermute | solution.py:315
  4.7 1.5 %collective-permute-start.1 = (bf16[144,256]{1,0:T(8,128)(2,1)S(1)}, bf16[144,256]{1,0:T(8,128)(2,1)S(1)}, u32[]{:S(2)}, u32[]{:S(2)}) collective-permute-start(bf16[144,256]{1,0:T(8,128)(2,1)S(1)} %get-tuple-element.36), channel_id=1, source_target_pairs={{0,4},{2,6},{4,0},{6,2},{8,12},{10,14},{12,8},{14,10},{16,20},{18,... | collective-permute-start | bytes 221192 | tf_op jit(solution)/shard_map/ppermute | solution.py:315
  6.2 0.7 %copy-done = s32[16]{0:T(128)S(1)} copy-done((s32[16]{0:T(128)S(1)}, s32[16]{0:T(128)}, u32[]{:S(2)}) %copy-start) | copy-done | bytes 88
  6.9 1.4 %shard_map.103 = (bf16[128,1024]{1,0:T(8,128)(2,1)S(1)}, bf16[128,1024]{1,0:T(8,128)(2,1)S(1)}, bf16[128,1024]{1,0:T(8,128)(2,1)S(1)}, bf16[128,1024]{1,0:T(8,128)(2,1)S(1)}) custom-call(s32[1]{0:T(128)} %bitcast.r_ref, bf16[128,2048]{1,0:T(8,128)(2,1)} %query_ref.1, bf16[128,2048]{1,0:T(8,128)(2,1)} %grad_ref.1), custom_call_target="tpu_custom_call" | custom-call | tf_op jit(solution)/shard_map/pallas_call | solution.py:36
  8.4 0.6 %collective-permute-done.1.refs_2_ = bf16[144,256]{1,0:T(8,128)(2,1)S(1)} collective-permute-done((bf16[144,256]{1,0:T(8,128)(2,1)S(1)}, bf16[144,256]{1,0:T(8,128)(2,1)S(1)}, u32[]{:S(2)}, u32[]{:S(2)}) %collective-permute-start.1) | collective-permute-done | bytes 73760 | tf_op jit(solution)/shard_map/ppermute | solution.py:315
  9.0 2.4 %collective-permute-done.2.refs_3_ = bf16[144,256]{1,0:T(8,128)(2,1)S(1)} collective-permute-done((bf16[144,256]{1,0:T(8,128)(2,1)S(1)}, bf16[144,256]{1,0:T(8,128)(2,1)S(1)}, u32[]{:S(2)}, u32[]{:S(2)}) %collective-permute-start.2) | collective-permute-done | bytes 73760 | tf_op jit(solution)/shard_map/ppermute | solution.py:315
  11.4 0.1 shard_map.104
  11.5 1.6 %collective-permute-start.3 = (bf16[528,256]{1,0:T(8,128)(2,1)S(1)}, bf16[528,256]{1,0:T(8,128)(2,1)S(1)}, u32[]{:S(2)}, u32[]{:S(2)}) collective-permute-start(bf16[528,256]{1,0:T(8,128)(2,1)S(1)} %get-tuple-element.45.refs_3_), channel_id=1, source_target_pairs={{0,8},{2,10},{4,12},{6,14},{8,16},{10,18},{12,20},{14,22},{16,24},... | collective-permute-start | bytes 811016 | tf_op jit(solution)/shard_map/ppermute | solution.py:323
  13.1 0.5 collective-permute-start.6
  13.7 0.5 collective-permute-start.7
  14.2 2.4 %collective-permute-start.8 = (bf16[128,1024]{1,0:T(8,128)(2,1)S(1)}, bf16[128,1024]{1,0:T(8,128)(2,1)S(1)}, u32[]{:S(2)}, u32[]{:S(2)}) collective-permute-start(bf16[128,1024]{1,0:T(8,128)(2,1)S(1)} %get-tuple-element.48), channel_id=1, source_target_pairs={{0,6},{2,4},{4,2},{6,0},{8,14},{10,12},{12,10},{14,8},{16,22},{18,... | collective-permute-start | bytes 786440 | tf_op jit(solution)/shard_map/ppermute | solution.py:315
  16.6 3.4 %collective-permute-done.3.near_ref.part_ref.refs_2_ = bf16[528,256]{1,0:T(8,128)(2,1)S(1)} collective-permute-done((bf16[528,256]{1,0:T(8,128)(2,1)S(1)}, bf16[528,256]{1,0:T(8,128)(2,1)S(1)}, u32[]{:S(2)}, u32[]{:S(2)}) %collective-permute-start.3) | collective-permute-done | bytes 270368 | tf_op jit(solution)/shard_map/ppermute | solution.py:323
  20.0 1.6 %collective-permute-start.5 = (bf16[272,256]{1,0:T(8,128)(2,1)S(1)}, bf16[272,256]{1,0:T(8,128)(2,1)S(1)}, u32[]{:S(2)}, u32[]{:S(2)}) collective-permute-start(bf16[272,256]{1,0:T(8,128)(2,1)S(1)} %shard_map.106), channel_id=1, source_target_pairs={{0,8},{2,10},{4,12},{6,14},{8,16},{10,18},{12,20},{14,22},{16,24},... | collective-permute-start | bytes 417800 | tf_op jit(solution)/shard_map/ppermute | solution.py:323
  21.6 2.7 %collective-permute-start.4 = (f32[8,128]{1,0:T(8,128)S(1)}, f32[8,128]{1,0:T(8,128)S(1)}, u32[]{:S(2)}, u32[]{:S(2)}) collective-permute-start(f32[8,128]{1,0:T(8,128)S(1)} %shard_map.105), channel_id=1, source_target_pairs={{0,16},{2,18},{4,20},{6,22},{8,24},{10,26},{12,28},{14,30},{16,0},... | collective-permute-start | bytes 12296 | tf_op jit(solution)/shard_map/ppermute | solution.py:315
  24.3 1.2 %collective-permute-done.7.refs_6_ = bf16[128,1024]{1,0:T(8,128)(2,1)S(1)} collective-permute-done((bf16[128,1024]{1,0:T(8,128)(2,1)S(1)}, bf16[128,1024]{1,0:T(8,128)(2,1)S(1)}, u32[]{:S(2)}, u32[]{:S(2)}) %collective-permute-start.7) | collective-permute-done | bytes 262176 | tf_op jit(solution)/shard_map/ppermute | solution.py:315
  25.5 0.7 %collective-permute-done.4.refs_0_ = f32[8,128]{1,0:T(8,128)S(1)} collective-permute-done((f32[8,128]{1,0:T(8,128)S(1)}, f32[8,128]{1,0:T(8,128)S(1)}, u32[]{:S(2)}, u32[]{:S(2)}) %collective-permute-start.4) | collective-permute-done | bytes 4128 | tf_op jit(solution)/shard_map/ppermute | solution.py:315
  26.2 8.0 %shard_map.107 = (bf16[128,1024]{1,0:T(8,128)(2,1)S(1)}, bf16[128,1024]{1,0:T(8,128)(2,1)S(1)}, bf16[128,1024]{1,0:T(8,128)(2,1)S(1)}, bf16[128,1024]{1,0:T(8,12...) custom-call(s32[6]{0:T(128)S(1)} %pad_add_fusion.where_ref, ...), custom_call_target="tpu_custom_call" | custom-call | flops 2818572288 | bytes 16777216 | tf_op jit(solution)/shard_map/pallas_call | solution.py:36
  34.3 2.6 %collective-permute-start.12 = (bf16[512,256]{1,0:T(8,128)(2,1)S(1)}, bf16[512,256]{1,0:T(8,128)(2,1)S(1)}, u32[]{:S(2)}, u32[]{:S(2)}) collective-permute-start(bf16[512,256]{1,0:T(8,128)(2,1)S(1)} %get-tuple-element.56), channel_id=1, source_target_pairs={{0,24},{2,26},{4,28},{6,30},{8,0},{10,2},{12,4},{14,6},{16,8},{18,... | collective-permute-start | bytes 786440 | tf_op jit(solution)/shard_map/ppermute | solution.py:323
  36.8 1.0 %collective-permute-start.9 = (bf16[128,1024]{1,0:T(8,128)(2,1)S(1)}, bf16[128,1024]{1,0:T(8,128)(2,1)S(1)}, u32[]{:S(2)}, u32[]{:S(2)}) collective-permute-start(bf16[128,1024]{1,0:T(8,128)(2,1)S(1)} %get-tuple-element.50), channel_id=1, source_target_pairs={{0,2},{2,0},{4,6},{6,4},{8,10},{10,8},{12,14},{14,12},{16,18},{18,... | collective-permute-start | bytes 786440 | tf_op jit(solution)/shard_map/ppermute | solution.py:315
  37.8 0.6 %collective-permute-start.10 = (bf16[128,1024]{1,0:T(8,128)(2,1)S(1)}, bf16[128,1024]{1,0:T(8,128)(2,1)S(1)}, u32[]{:S(2)}, u32[]{:S(2)}) collective-permute-start(bf16[128,1024]{1,0:T(8,128)(2,1)S(1)} %get-tuple-element.51), channel_id=1, source_target_pairs={{0,4},{2,6},{4,0},{6,2},{8,12},{10,14},{12,8},{14,10},{16,20},{18,... | collective-permute-start | bytes 786440 | tf_op jit(solution)/shard_map/ppermute | solution.py:315
  38.4 1.9 %collective-permute-start.11 = (bf16[128,1024]{1,0:T(8,128)(2,1)S(1)}, bf16[128,1024]{1,0:T(8,128)(2,1)S(1)}, u32[]{:S(2)}, u32[]{:S(2)}) collective-permute-start(bf16[128,1024]{1,0:T(8,128)(2,1)S(1)} %get-tuple-element.52), channel_id=1, source_target_pairs={{0,6},{2,4},{4,2},{6,0},{8,14},{10,12},{12,10},{14,8},{16,22},{18,... | collective-permute-start | bytes 786440 | tf_op jit(solution)/shard_map/ppermute | solution.py:315
  40.3 1.8 %collective-permute-done.12.got_ref.refs_0_ = bf16[512,256]{1,0:T(8,128)(2,1)S(1)} collective-permute-done((bf16[512,256]{1,0:T(8,128)(2,1)S(1)}, bf16[512,256]{1,0:T(8,128)(2,1)S(1)}, u32[]{:S(2)}, u32[]{:S(2)}) %collective-permute-start.12) | collective-permute-done | bytes 262176 | tf_op jit(solution)/shard_map/ppermute | solution.py:323
  42.1 3.2 %collective-permute-start.13 = (bf16[256,256]{1,0:T(8,128)(2,1)S(1)}, bf16[256,256]{1,0:T(8,128)(2,1)S(1)}, u32[]{:S(2)}, u32[]{:S(2)}) collective-permute-start(bf16[256,256]{1,0:T(8,128)(2,1)S(1)} %shard_map.109), channel_id=1, source_target_pairs={{0,24},{2,26},{4,28},{6,30},{8,0},{10,2},{12,4},{14,6},{16,8},{18,... | collective-permute-start | bytes 393224 | tf_op jit(solution)/shard_map/ppermute | solution.py:323
  45.3 2.5 %collective-permute-done.13.refs_1_ = bf16[256,256]{1,0:T(8,128)(2,1)S(1)} collective-permute-done((bf16[256,256]{1,0:T(8,128)(2,1)S(1)}, bf16[256,256]{1,0:T(8,128)(2,1)S(1)}, u32[]{:S(2)}, u32[]{:S(2)}) %collective-permute-start.13) | collective-permute-done | bytes 131104 | tf_op jit(solution)/shard_map/ppermute | solution.py:323
  47.9 0.8 %collective-permute-start.14 = (bf16[128,256]{1,0:T(8,128)(2,1)S(1)}, bf16[128,256]{1,0:T(8,128)(2,1)S(1)}, u32[]{:S(2)}, u32[]{:S(2)}) collective-permute-start(bf16[128,256]{1,0:T(8,128)(2,1)S(1)} %get-tuple-element.59), channel_id=1, source_target_pairs={{0,2},{2,0},{4,6},{6,4},{8,10},{10,8},{12,14},{14,12},{16,18},{18,... | collective-permute-start | bytes 196616 | tf_op jit(solution)/shard_map/ppermute | solution.py:315
  48.7 0.6 %collective-permute-start.15 = (bf16[128,256]{1,0:T(8,128)(2,1)S(1)}, bf16[128,256]{1,0:T(8,128)(2,1)S(1)}, u32[]{:S(2)}, u32[]{:S(2)}) collective-permute-start(bf16[128,256]{1,0:T(8,128)(2,1)S(1)} %get-tuple-element.60), channel_id=1, source_target_pairs={{0,4},{2,6},{4,0},{6,2},{8,12},{10,14},{12,8},{14,10},{16,20},{18,... | collective-permute-start | bytes 196616 | tf_op jit(solution)/shard_map/ppermute | solution.py:315
  49.3 2.1 %collective-permute-start.16 = (bf16[128,256]{1,0:T(8,128)(2,1)S(1)}, bf16[128,256]{1,0:T(8,128)(2,1)S(1)}, u32[]{:S(2)}, u32[]{:S(2)}) collective-permute-start(bf16[128,256]{1,0:T(8,128)(2,1)S(1)} %get-tuple-element.61), channel_id=1, source_target_pairs={{0,6},{2,4},{4,2},{6,0},{8,14},{10,12},{12,10},{14,8},{16,22},{18,... | collective-permute-start | bytes 196616 | tf_op jit(solution)/shard_map/ppermute | solution.py:315
  51.4 1.0 %shard_map.108 = (bf16[128,2048]{1,0:T(8,128)(2,1)}, bf16[128,2048]{1,0:T(8,128)(2,1)}) custom-call(s32[1]{0:T(128)} %bitcast.r_ref, bf16[128,1024]{1,0:T(8,128)(2,1)S(1)} %get-tuple-element.49.refs_0_, bf16[128,1024]{1,0:T(8,128)(2,1)S(1)} %collective-permute-done.9.refs_1_, bf16[128,1024]{1,0:T(8,128)(2,1)S(1)} %collective-permute-done.10.refs_2_, ...), custom_call_target="tpu_custom_call" | custom-call | tf_op jit(solution)/shard_map/pallas_call | solution.py:36
  52.5 0.5 collective-permute-done.15.refs_2_
  53.0 1.5 %collective-permute-done.16.refs_3_ = bf16[128,256]{1,0:T(8,128)(2,1)S(1)} collective-permute-done((bf16[128,256]{1,0:T(8,128)(2,1)S(1)}, bf16[128,256]{1,0:T(8,128)(2,1)S(1)}, u32[]{:S(2)}, u32[]{:S(2)}) %collective-permute-start.16) | collective-permute-done | bytes 65568 | tf_op jit(solution)/shard_map/ppermute | solution.py:315
  54.5 0.8 %shard_map.111 = (bf16[128,512]{1,0:T(8,128)(2,1)}, bf16[128,512]{1,0:T(8,128)(2,1)}) custom-call(s32[1]{0:T(128)} %bitcast.r_ref, bf16[128,256]{1,0:T(8,128)(2,1)S(1)} %get-tuple-element.58.refs_0_, bf16[128,256]{1,0:T(8,128)(2,1)S(1)} %collective-permute-done.14.refs_1_, bf16[128,256]{1,0:T(8,128)(2,1)S(1)} %collective-permute-done.15.refs_2_, ...), custom_call_target="tpu_custom_call" | custom-call | tf_op jit(solution)/shard_map/pallas_call | solution.py:36
  (16 shorter events, 0.3 us)
Async XLA Ops:
  1.6 6.7 %collective-permute-start = (bf16[144,256]{1,0:T(8,128)(2,1)S(1)}, bf16[144,256]{1,0:T(8,128)(2,1)S(1)}, u32[]{:S(2)}, u32[]{:S(2)}) collective-permute-start(bf16[144,256]{1,0:T(8,128)(2,1)S(1)} %get-tuple-element.35), channel_id=1, source_target_pairs={{0,2},{2,0},{4,6},{6,4},{8,10},{10,8},{12,14},{14,12},{16,18},{18,... | collective-permute-start | bytes 221192 | tf_op jit(solution)/shard_map/ppermute | solution.py:315
  4.7 4.4 %collective-permute-start.1 = (bf16[144,256]{1,0:T(8,128)(2,1)S(1)}, bf16[144,256]{1,0:T(8,128)(2,1)S(1)}, u32[]{:S(2)}, u32[]{:S(2)}) collective-permute-start(bf16[144,256]{1,0:T(8,128)(2,1)S(1)} %get-tuple-element.36), channel_id=1, source_target_pairs={{0,4},{2,6},{4,0},{6,2},{8,12},{10,14},{12,8},{14,10},{16,20},{18,... | collective-permute-start | bytes 221192 | tf_op jit(solution)/shard_map/ppermute | solution.py:315
  6.2 5.3 %collective-permute-start.2 = (bf16[144,256]{1,0:T(8,128)(2,1)S(1)}, bf16[144,256]{1,0:T(8,128)(2,1)S(1)}, u32[]{:S(2)}, u32[]{:S(2)}) collective-permute-start(bf16[144,256]{1,0:T(8,128)(2,1)S(1)} %get-tuple-element.37), channel_id=1, source_target_pairs={{0,6},{2,4},{4,2},{6,0},{8,14},{10,12},{12,10},{14,8},{16,22},{18,... | collective-permute-start | bytes 221192 | tf_op jit(solution)/shard_map/ppermute | solution.py:315
  6.2 0.7 %copy-start = (s32[16]{0:T(128)S(1)}, s32[16]{0:T(128)}, u32[]{:S(2)}) copy-start(s32[16]{0:T(128)} %param.13) | copy-start | bytes 196
  11.5 8.4 %collective-permute-start.3 = (bf16[528,256]{1,0:T(8,128)(2,1)S(1)}, bf16[528,256]{1,0:T(8,128)(2,1)S(1)}, u32[]{:S(2)}, u32[]{:S(2)}) collective-permute-start(bf16[528,256]{1,0:T(8,128)(2,1)S(1)} %get-tuple-element.45.refs_3_), channel_id=1, source_target_pairs={{0,8},{2,10},{4,12},{6,14},{8,16},{10,18},{12,20},{14,22},{16,24},... | collective-permute-start | bytes 811016 | tf_op jit(solution)/shard_map/ppermute | solution.py:323
  13.1 11.2 %collective-permute-start.6 = (bf16[128,1024]{1,0:T(8,128)(2,1)S(1)}, bf16[128,1024]{1,0:T(8,128)(2,1)S(1)}, u32[]{:S(2)}, u32[]{:S(2)}) collective-permute-start(bf16[128,1024]{1,0:T(8,128)(2,1)S(1)} %get-tuple-element.46), channel_id=1, source_target_pairs={{0,2},{2,0},{4,6},{6,4},{8,10},{10,8},{12,14},{14,12},{16,18},{18,... | collective-permute-start | bytes 786440 | tf_op jit(solution)/shard_map/ppermute | solution.py:315
  13.7 11.9 %collective-permute-start.7 = (bf16[128,1024]{1,0:T(8,128)(2,1)S(1)}, bf16[128,1024]{1,0:T(8,128)(2,1)S(1)}, u32[]{:S(2)}, u32[]{:S(2)}) collective-permute-start(bf16[128,1024]{1,0:T(8,128)(2,1)S(1)} %get-tuple-element.47), channel_id=1, source_target_pairs={{0,4},{2,6},{4,0},{6,2},{8,12},{10,14},{12,8},{14,10},{16,20},{18,... | collective-permute-start | bytes 786440 | tf_op jit(solution)/shard_map/ppermute | solution.py:315
  14.2 11.3 %collective-permute-start.8 = (bf16[128,1024]{1,0:T(8,128)(2,1)S(1)}, bf16[128,1024]{1,0:T(8,128)(2,1)S(1)}, u32[]{:S(2)}, u32[]{:S(2)}) collective-permute-start(bf16[128,1024]{1,0:T(8,128)(2,1)S(1)} %get-tuple-element.48), channel_id=1, source_target_pairs={{0,6},{2,4},{4,2},{6,0},{8,14},{10,12},{12,10},{14,8},{16,22},{18,... | collective-permute-start | bytes 786440 | tf_op jit(solution)/shard_map/ppermute | solution.py:315
  20.0 6.2 %collective-permute-start.5 = (bf16[272,256]{1,0:T(8,128)(2,1)S(1)}, bf16[272,256]{1,0:T(8,128)(2,1)S(1)}, u32[]{:S(2)}, u32[]{:S(2)}) collective-permute-start(bf16[272,256]{1,0:T(8,128)(2,1)S(1)} %shard_map.106), channel_id=1, source_target_pairs={{0,8},{2,10},{4,12},{6,14},{8,16},{10,18},{12,20},{14,22},{16,24},... | collective-permute-start | bytes 417800 | tf_op jit(solution)/shard_map/ppermute | solution.py:323
  21.6 4.6 %collective-permute-start.4 = (f32[8,128]{1,0:T(8,128)S(1)}, f32[8,128]{1,0:T(8,128)S(1)}, u32[]{:S(2)}, u32[]{:S(2)}) collective-permute-start(f32[8,128]{1,0:T(8,128)S(1)} %shard_map.105), channel_id=1, source_target_pairs={{0,16},{2,18},{4,20},{6,22},{8,24},{10,26},{12,28},{14,30},{16,0},... | collective-permute-start | bytes 12296 | tf_op jit(solution)/shard_map/ppermute | solution.py:315
  34.3 7.8 %collective-permute-start.12 = (bf16[512,256]{1,0:T(8,128)(2,1)S(1)}, bf16[512,256]{1,0:T(8,128)(2,1)S(1)}, u32[]{:S(2)}, u32[]{:S(2)}) collective-permute-start(bf16[512,256]{1,0:T(8,128)(2,1)S(1)} %get-tuple-element.56), channel_id=1, source_target_pairs={{0,24},{2,26},{4,28},{6,30},{8,0},{10,2},{12,4},{14,6},{16,8},{18,... | collective-permute-start | bytes 786440 | tf_op jit(solution)/shard_map/ppermute | solution.py:323
  36.8 12.5 %collective-permute-start.9 = (bf16[128,1024]{1,0:T(8,128)(2,1)S(1)}, bf16[128,1024]{1,0:T(8,128)(2,1)S(1)}, u32[]{:S(2)}, u32[]{:S(2)}) collective-permute-start(bf16[128,1024]{1,0:T(8,128)(2,1)S(1)} %get-tuple-element.50), channel_id=1, source_target_pairs={{0,2},{2,0},{4,6},{6,4},{8,10},{10,8},{12,14},{14,12},{16,18},{18,... | collective-permute-start | bytes 786440 | tf_op jit(solution)/shard_map/ppermute | solution.py:315
  37.8 13.7 %collective-permute-start.10 = (bf16[128,1024]{1,0:T(8,128)(2,1)S(1)}, bf16[128,1024]{1,0:T(8,128)(2,1)S(1)}, u32[]{:S(2)}, u32[]{:S(2)}) collective-permute-start(bf16[128,1024]{1,0:T(8,128)(2,1)S(1)} %get-tuple-element.51), channel_id=1, source_target_pairs={{0,4},{2,6},{4,0},{6,2},{8,12},{10,14},{12,8},{14,10},{16,20},{18,... | collective-permute-start | bytes 786440 | tf_op jit(solution)/shard_map/ppermute | solution.py:315
  38.4 13.0 %collective-permute-start.11 = (bf16[128,1024]{1,0:T(8,128)(2,1)S(1)}, bf16[128,1024]{1,0:T(8,128)(2,1)S(1)}, u32[]{:S(2)}, u32[]{:S(2)}) collective-permute-start(bf16[128,1024]{1,0:T(8,128)(2,1)S(1)} %get-tuple-element.52), channel_id=1, source_target_pairs={{0,6},{2,4},{4,2},{6,0},{8,14},{10,12},{12,10},{14,8},{16,22},{18,... | collective-permute-start | bytes 786440 | tf_op jit(solution)/shard_map/ppermute | solution.py:315
  42.1 5.7 %collective-permute-start.13 = (bf16[256,256]{1,0:T(8,128)(2,1)S(1)}, bf16[256,256]{1,0:T(8,128)(2,1)S(1)}, u32[]{:S(2)}, u32[]{:S(2)}) collective-permute-start(bf16[256,256]{1,0:T(8,128)(2,1)S(1)} %shard_map.109), channel_id=1, source_target_pairs={{0,24},{2,26},{4,28},{6,30},{8,0},{10,2},{12,4},{14,6},{16,8},{18,... | collective-permute-start | bytes 393224 | tf_op jit(solution)/shard_map/ppermute | solution.py:323
  47.9 4.6 %collective-permute-start.14 = (bf16[128,256]{1,0:T(8,128)(2,1)S(1)}, bf16[128,256]{1,0:T(8,128)(2,1)S(1)}, u32[]{:S(2)}, u32[]{:S(2)}) collective-permute-start(bf16[128,256]{1,0:T(8,128)(2,1)S(1)} %get-tuple-element.59), channel_id=1, source_target_pairs={{0,2},{2,0},{4,6},{6,4},{8,10},{10,8},{12,14},{14,12},{16,18},{18,... | collective-permute-start | bytes 196616 | tf_op jit(solution)/shard_map/ppermute | solution.py:315
  48.7 4.3 %collective-permute-start.15 = (bf16[128,256]{1,0:T(8,128)(2,1)S(1)}, bf16[128,256]{1,0:T(8,128)(2,1)S(1)}, u32[]{:S(2)}, u32[]{:S(2)}) collective-permute-start(bf16[128,256]{1,0:T(8,128)(2,1)S(1)} %get-tuple-element.60), channel_id=1, source_target_pairs={{0,4},{2,6},{4,0},{6,2},{8,12},{10,14},{12,8},{14,10},{16,20},{18,... | collective-permute-start | bytes 196616 | tf_op jit(solution)/shard_map/ppermute | solution.py:315
  49.3 5.2 %collective-permute-start.16 = (bf16[128,256]{1,0:T(8,128)(2,1)S(1)}, bf16[128,256]{1,0:T(8,128)(2,1)S(1)}, u32[]{:S(2)}, u32[]{:S(2)}) collective-permute-start(bf16[128,256]{1,0:T(8,128)(2,1)S(1)} %get-tuple-element.61), channel_id=1, source_target_pairs={{0,6},{2,4},{4,2},{6,0},{8,14},{10,12},{12,10},{14,8},{16,22},{18,... | collective-permute-start | bytes 196616 | tf_op jit(solution)/shard_map/ppermute | solution.py:315
